TPU v7x, 32 devices: a whole 2x2x4 slice. The times are simulated.
32 devices in a mesh: dp: 4 (over y, x), seq: 8 (over z, core).
Axes of the slice: x: 2, y: 2, z: 4, core: 2. Of those that a mesh axis runs over, the one named last changes fastest.
Arguments:
- tokens: bfloat16 [4, 2048, 1024], P('dp', 'seq'), may hold values from -6 to 6
- segment_ids: int32 [4, 2048], P('dp'), may hold values from 0 to 7, never falling along the last dimension, each value on 1 to 1024 neighbouring positions
- w_query: bfloat16 [1024, 1024], P(('dp', 'seq')), may hold values from -0.1875 to 0.1875
- w_key: bfloat16 [1024, 512], P(('dp', 'seq')), may hold values from -0.1875 to 0.1875
- w_value: bfloat16 [1024, 512], P(('dp', 'seq')), may hold values from -0.1875 to 0.1875
- w_out: bfloat16 [1024, 1024], P(('dp', 'seq')), may hold values from -1.5 to 1.5
- attn_gain: bfloat16 [1024], P(('dp', 'seq')), may hold values from 0.5 to 1.5
- query_gain: bfloat16 [64], replicated, may hold values from 0.25 to 1.75
- key_gain: bfloat16 [64], replicated, may hold values from 0.25 to 1.75
- w_gate: bfloat16 [1024, 4608], P(('dp', 'seq')), may hold values from -0.1875 to 0.1875
- w_up: bfloat16 [1024, 4608], P(('dp', 'seq')), may hold values from -0.1875 to 0.1875
- w_down: bfloat16 [4608, 1024], P(('dp', 'seq')), may hold values from -0.09375 to 0.09375
- ffn_gain: bfloat16 [1024], P(('dp', 'seq')), may hold values from 0.5 to 1.5
- cotangent: bfloat16 [4, 2048, 1024], P('dp', 'seq'), may hold values from -6 to 6
Outputs:
- output: bfloat16 [4, 2048, 1024], P('dp', 'seq')
- d_tokens: float32 [4, 2048, 1024], P('dp', 'seq')
- d_w_query: float32 [1024, 1024], P(('dp', 'seq'))
- d_w_key: float32 [1024, 512], P(('dp', 'seq'))
- d_w_value: float32 [1024, 512], P(('dp', 'seq'))
- d_w_out: float32 [1024, 1024], P(('dp', 'seq'))
- d_attn_gain: float32 [1024], P(('dp', 'seq'))
- d_query_gain: float32 [64], replicated
- d_key_gain: float32 [64], replicated
- d_w_gate: float32 [1024, 4608], P(('dp', 'seq'))
- d_w_up: float32 [1024, 4608], P(('dp', 'seq'))
- d_w_down: float32 [4608, 1024], P(('dp', 'seq'))
- d_ffn_gain: float32 [1024], P(('dp', 'seq'))
Inputs may be any that keep to these rules, and one draw needn't show every extreme that they name: `segment_ids`: within a sequence the ids never fall; every document holds 1 to 1024 positions, and some document holds exactly 1024.
All inputs are finite; a program needn't handle non-finite values.
Results may differ from a plain program's by a relative error of at most 0.015.
Values may be sent and summed in bfloat16 or wider, within the bound.
No kernel may reach another device: no remote copies, remote signals or barrier semaphores. Data moves between devices by JAX's collectives and lax.ppermute only.
A program may use at most 192 MiB of HBM per device.

v0:
```python
import jax
import jax.numpy as jnp
from jax import lax
from jax.sharding import PartitionSpec as P

EPSILON = 1e-05
ROPE_BASE = 1000000.0


def rms_scale(values):
    return lax.rsqrt(jnp.mean(values * values, axis=-1, keepdims=True) + EPSILON)


def rope_tables(positions, head_width):
    half_width = head_width // 2
    frequency = ROPE_BASE ** (-(jnp.arange(half_width, dtype=jnp.float32) * 2.0 / head_width))
    angles = positions.astype(jnp.float32)[:, None] * frequency[None, :]
    return (jnp.cos(angles), jnp.sin(angles))


def rotate(values, cosine_table, sine_table):
    half_width = values.shape[-1] // 2
    front_half = values[..., :half_width]
    back_half = values[..., half_width:]
    return jnp.concatenate(
        [
            front_half * cosine_table - back_half * sine_table,
            back_half * cosine_table + front_half * sine_table,
        ],
        axis=-1,
    )


def unrotate(incoming, cosine_table, sine_table):
    half_width = incoming.shape[-1] // 2
    front_half = incoming[..., :half_width]
    back_half = incoming[..., half_width:]
    return jnp.concatenate(
        [
            front_half * cosine_table + back_half * sine_table,
            back_half * cosine_table - front_half * sine_table,
        ],
        axis=-1,
    )


def norm_back(incoming, values, scale_vec, gain_vector, sum_axes):
    upstream = incoming * gain_vector
    grad_values = scale_vec * (
        upstream
        - values * scale_vec * scale_vec * jnp.mean(upstream * values, axis=-1, keepdims=True)
    )
    grad_gain = jnp.sum(incoming * values * scale_vec, axis=sum_axes)
    return (grad_values, grad_gain)


def body(
    tokens,
    segment_ids,
    w_query,
    w_key,
    w_value,
    w_out,
    attn_gain,
    query_gain,
    key_gain,
    w_gate,
    w_up,
    w_down,
    ffn_gain,
    cotangent,
):
    seq_count, local_len, model_width = tokens.shape
    seq_len = segment_ids.shape[1]
    head_width = query_gain.shape[0]
    query_heads = w_query.shape[1] // head_width
    key_heads = w_key.shape[1] // head_width
    group_size = query_heads // key_heads
    softmax_scale = head_width ** (-0.5)
    dev_rank = lax.axis_index("seq")
    first_row = dev_rank * local_len
    last_row = first_row + local_len - 1
    query_pos = first_row + jnp.arange(local_len, dtype=jnp.int32)
    query_ids = lax.dynamic_slice_in_dim(segment_ids, first_row, local_len, 1)
    cosine_table, sine_table = rope_tables(query_pos, head_width)
    cosine_table = cosine_table[None, :, None, :]
    sine_table = sine_table[None, :, None, :]

    def mask_for(offset, count):
        key_pos = offset + jnp.arange(count, dtype=jnp.int32)
        key_ids = lax.dynamic_slice_in_dim(segment_ids, offset, count, 1)
        allowed = (key_pos[None, None, :] <= query_pos[None, :, None]) & (
            key_ids[:, None, :] == query_ids[:, :, None]
        )
        return allowed[:, None, None]

    attn_full = (
        lax.all_gather(w_query, ("dp", "seq"), axis=0, tiled=True),
        lax.all_gather(w_key, ("dp", "seq"), axis=0, tiled=True),
        lax.all_gather(w_value, ("dp", "seq"), axis=0, tiled=True),
        lax.all_gather(w_out, ("dp", "seq"), axis=0, tiled=True),
        lax.all_gather(attn_gain, ("dp", "seq"), axis=0, tiled=True),
    )
    query_all, key_all, value_all, out_all, attn_gain_all = attn_full
    stream = tokens.astype(jnp.float32)
    scale_one = rms_scale(stream)
    normed_one = (stream * scale_one * attn_gain_all.astype(jnp.float32)).astype(jnp.bfloat16)
    query_pre = jnp.einsum(
        "sct,te->sce", normed_one, query_all, preferred_element_type=jnp.float32
    ).reshape(seq_count, local_len, query_heads, head_width)
    key_pre = jnp.einsum(
        "sct,te->sce", normed_one, key_all, preferred_element_type=jnp.float32
    ).reshape(seq_count, local_len, key_heads, head_width)
    value_pre = jnp.einsum("sct,te->sce", normed_one, value_all, preferred_element_type=jnp.float32)
    query_scale = rms_scale(query_pre)
    key_scale = rms_scale(key_pre)
    query_rot = (
        rotate(query_pre * query_scale * query_gain.astype(jnp.float32), cosine_table, sine_table)
        .astype(jnp.bfloat16)
        .reshape(seq_count, local_len, key_heads, group_size, head_width)
    )
    key_rot = (
        rotate(key_pre * key_scale * key_gain.astype(jnp.float32), cosine_table, sine_table)
        .astype(jnp.bfloat16)
        .reshape(seq_count, local_len, key_heads * head_width)
    )
    value_send = value_pre.astype(jnp.bfloat16)
    start_state = (
        jnp.zeros((seq_count, key_heads, group_size, local_len), jnp.float32),
        jnp.zeros((seq_count, local_len, key_heads, group_size, head_width), jnp.float32),
    )
    offset = jnp.int32(0)
    key_piece = lax.all_gather(key_rot, "seq", axis=1, tiled=True)
    value_piece = lax.all_gather(value_send, "seq", axis=1, tiled=True)
    count = key_piece.shape[1]

    def attend(state):
        key_block = key_piece.reshape(seq_count, count, key_heads, head_width)
        value_block = value_piece.reshape(seq_count, count, key_heads, head_width)
        scores = (
            jnp.einsum(
                "sqgrd,skgd->sgrqk", query_rot, key_block, preferred_element_type=jnp.float32
            )
            * softmax_scale
        )
        weights = jnp.where(mask_for(offset, count), jnp.exp(scores), 0.0)
        denominator = jnp.sum(weights, axis=-1)
        summed = jnp.einsum(
            "sgrqk,skgd->sqgrd",
            weights.astype(jnp.bfloat16),
            value_block,
            preferred_element_type=jnp.float32,
        )
        return (denominator, summed)

    denominator, summed = lax.cond(offset <= last_row, attend, lambda state: state, start_state)
    attended = (summed / jnp.moveaxis(denominator, 3, 1)[..., None]).astype(jnp.bfloat16)
    log_total = jnp.log(denominator)
    attended_flat = attended.reshape(seq_count, local_len, query_heads * head_width)
    middle = stream + jnp.einsum(
        "sce,et->sct", attended_flat, out_all, preferred_element_type=jnp.float32
    )
    mlp_full = (
        lax.all_gather(w_gate, ("dp", "seq"), axis=0, tiled=True),
        lax.all_gather(w_up, ("dp", "seq"), axis=0, tiled=True),
        lax.all_gather(w_down, ("dp", "seq"), axis=0, tiled=True),
        lax.all_gather(ffn_gain, ("dp", "seq"), axis=0, tiled=True),
    )
    gate_all, up_all, down_all, ffn_gain_all = mlp_full
    scale_two = rms_scale(middle)
    normed_two = (middle * scale_two * ffn_gain_all.astype(jnp.float32)).astype(jnp.bfloat16)
    gate_pre = jnp.einsum("sct,tf->scf", normed_two, gate_all, preferred_element_type=jnp.float32)
    up_pre = jnp.einsum("sct,tf->scf", normed_two, up_all, preferred_element_type=jnp.float32)
    sigmoid_gate = jax.nn.sigmoid(gate_pre)
    silu_gate = gate_pre * sigmoid_gate
    hidden = (silu_gate * up_pre).astype(jnp.bfloat16)
    output = (
        middle + jnp.einsum("scf,fe->sce", hidden, down_all, preferred_element_type=jnp.float32)
    ).astype(jnp.bfloat16)
    gate_all, up_all, down_all, ffn_gain_all = (
        lax.all_gather(w_gate, ("dp", "seq"), axis=0, tiled=True),
        lax.all_gather(w_up, ("dp", "seq"), axis=0, tiled=True),
        lax.all_gather(w_down, ("dp", "seq"), axis=0, tiled=True),
        lax.all_gather(ffn_gain, ("dp", "seq"), axis=0, tiled=True),
    )
    grad_output = cotangent.astype(jnp.float32)
    grad_hidden = jnp.einsum("sce,fe->scf", cotangent, down_all, preferred_element_type=jnp.float32)
    grad_down_w = jnp.einsum("scf,sce->fe", hidden, cotangent, preferred_element_type=jnp.float32)
    grad_gate = (
        grad_hidden * up_pre * sigmoid_gate * (1.0 + gate_pre * (1.0 - sigmoid_gate))
    ).astype(jnp.bfloat16)
    grad_up = (grad_hidden * silu_gate).astype(jnp.bfloat16)
    grad_gate_w = jnp.einsum(
        "sct,scf->tf", normed_two, grad_gate, preferred_element_type=jnp.float32
    )
    grad_up_w = jnp.einsum("sct,scf->tf", normed_two, grad_up, preferred_element_type=jnp.float32)
    grad_normed_two = jnp.einsum(
        "scf,tf->sct", grad_gate, gate_all, preferred_element_type=jnp.float32
    ) + jnp.einsum("scf,tf->sct", grad_up, up_all, preferred_element_type=jnp.float32)
    grad_mid_norm, grad_ffn_gain = norm_back(
        grad_normed_two, middle, scale_two, ffn_gain_all.astype(jnp.float32), (0, 1)
    )
    grad_middle = grad_output + grad_mid_norm
    mlp_grads = (
        lax.psum_scatter(grad_gate_w, ("dp", "seq"), scatter_dimension=0, tiled=True),
        lax.psum_scatter(grad_up_w, ("dp", "seq"), scatter_dimension=0, tiled=True),
        lax.psum_scatter(grad_down_w, ("dp", "seq"), scatter_dimension=0, tiled=True),
        lax.psum_scatter(grad_ffn_gain, ("dp", "seq"), scatter_dimension=0, tiled=True),
    )
    query_all, key_all, value_all, out_all, attn_gain_all = (
        lax.all_gather(w_query, ("dp", "seq"), axis=0, tiled=True),
        lax.all_gather(w_key, ("dp", "seq"), axis=0, tiled=True),
        lax.all_gather(w_value, ("dp", "seq"), axis=0, tiled=True),
        lax.all_gather(w_out, ("dp", "seq"), axis=0, tiled=True),
        lax.all_gather(attn_gain, ("dp", "seq"), axis=0, tiled=True),
    )
    grad_middle_bf = grad_middle.astype(jnp.bfloat16)
    grad_out_w = jnp.einsum(
        "sce,sct->et", attended_flat, grad_middle_bf, preferred_element_type=jnp.float32
    )
    grad_attended = (
        jnp.einsum("sct,et->sce", grad_middle_bf, out_all, preferred_element_type=jnp.float32)
        .astype(jnp.bfloat16)
        .reshape(seq_count, local_len, key_heads, group_size, head_width)
    )
    delta_rows = jnp.moveaxis(
        jnp.sum(grad_attended.astype(jnp.float32) * attended.astype(jnp.float32), axis=-1), 1, 3
    )
    keys_all, values_all = (
        lax.all_gather(key_rot, "seq", axis=1, tiled=True),
        lax.all_gather(value_send, "seq", axis=1, tiled=True),
    )
    block_len = min(512, seq_len)
    needed = last_row // block_len + 1

    def key_block_step(block_num, running):
        grad_query, grad_keys, grad_values = running
        offset = block_num * block_len
        key_block = lax.dynamic_slice_in_dim(keys_all, offset, block_len, 1).reshape(
            seq_count, block_len, key_heads, head_width
        )
        value_block = lax.dynamic_slice_in_dim(values_all, offset, block_len, 1).reshape(
            seq_count, block_len, key_heads, head_width
        )
        scores = (
            jnp.einsum(
                "sqgrd,skgd->sgrqk", query_rot, key_block, preferred_element_type=jnp.float32
            )
            * softmax_scale
        )
        probabilities = jnp.where(
            mask_for(offset, block_len), jnp.exp(scores - log_total[..., None]), 0.0
        )
        grad_probs = jnp.einsum(
            "sqgrd,skgd->sgrqk", grad_attended, value_block, preferred_element_type=jnp.float32
        )
        grad_scores = (probabilities * (grad_probs - delta_rows[..., None])).astype(jnp.bfloat16)
        value_term = jnp.einsum(
            "sgrqk,sqgrd->skgd",
            probabilities.astype(jnp.bfloat16),
            grad_attended,
            preferred_element_type=jnp.float32,
        )
        key_term = (
            jnp.einsum(
                "sgrqk,sqgrd->skgd", grad_scores, query_rot, preferred_element_type=jnp.float32
            )
            * softmax_scale
        )
        grad_query = (
            grad_query
            + jnp.einsum(
                "sgrqk,skgd->sqgrd", grad_scores, key_block, preferred_element_type=jnp.float32
            )
            * softmax_scale
        )
        grad_keys = lax.dynamic_update_slice_in_dim(
            grad_keys, key_term.reshape(seq_count, block_len, key_heads * head_width), offset, 1
        )
        grad_values = lax.dynamic_update_slice_in_dim(
            grad_values, value_term.reshape(seq_count, block_len, key_heads * head_width), offset, 1
        )
        return (grad_query, grad_keys, grad_values)

    start_grads = (
        jnp.zeros((seq_count, local_len, key_heads, group_size, head_width), jnp.float32),
        jnp.zeros((seq_count, seq_len, key_heads * head_width), jnp.float32),
        jnp.zeros((seq_count, seq_len, key_heads * head_width), jnp.float32),
    )
    grad_query, grad_keys, grad_values = lax.fori_loop(0, needed, key_block_step, start_grads)
    key_sum, value_sum = (
        lax.psum_scatter(
            grad_keys.astype(jnp.bfloat16), "seq", scatter_dimension=1, tiled=True
        ).astype(jnp.float32),
        lax.psum_scatter(
            grad_values.astype(jnp.bfloat16), "seq", scatter_dimension=1, tiled=True
        ).astype(jnp.float32),
    )
    grad_qnorm = unrotate(
        grad_query.reshape(seq_count, local_len, query_heads, head_width), cosine_table, sine_table
    )
    grad_qpre, grad_qgain = norm_back(
        grad_qnorm, query_pre, query_scale, query_gain.astype(jnp.float32), (0, 1, 2)
    )
    grad_knorm = unrotate(
        key_sum.reshape(seq_count, local_len, key_heads, head_width), cosine_table, sine_table
    )
    grad_kpre, grad_kgain = norm_back(
        grad_knorm, key_pre, key_scale, key_gain.astype(jnp.float32), (0, 1, 2)
    )
    query_bf = grad_qpre.reshape(seq_count, local_len, query_heads * head_width).astype(
        jnp.bfloat16
    )
    key_bf = grad_kpre.reshape(seq_count, local_len, key_heads * head_width).astype(jnp.bfloat16)
    value_grad_bf = value_sum.astype(jnp.bfloat16)
    grad_query_w = jnp.einsum(
        "sct,sce->te", normed_one, query_bf, preferred_element_type=jnp.float32
    )
    grad_key_w = jnp.einsum("sct,sce->te", normed_one, key_bf, preferred_element_type=jnp.float32)
    grad_value_w = jnp.einsum(
        "sct,sce->te", normed_one, value_grad_bf, preferred_element_type=jnp.float32
    )
    grad_normed_one = (
        jnp.einsum("sce,te->sct", query_bf, query_all, preferred_element_type=jnp.float32)
        + jnp.einsum("sce,te->sct", key_bf, key_all, preferred_element_type=jnp.float32)
        + jnp.einsum("sce,te->sct", value_grad_bf, value_all, preferred_element_type=jnp.float32)
    )
    grad_stream, grad_attn_gain = norm_back(
        grad_normed_one, stream, scale_one, attn_gain_all.astype(jnp.float32), (0, 1)
    )
    grad_tokens = grad_middle + grad_stream
    attn_grads = (
        lax.psum_scatter(grad_query_w, ("dp", "seq"), scatter_dimension=0, tiled=True),
        lax.psum_scatter(grad_key_w, ("dp", "seq"), scatter_dimension=0, tiled=True),
        lax.psum_scatter(grad_value_w, ("dp", "seq"), scatter_dimension=0, tiled=True),
        lax.psum_scatter(grad_out_w, ("dp", "seq"), scatter_dimension=0, tiled=True),
        lax.psum_scatter(grad_attn_gain, ("dp", "seq"), scatter_dimension=0, tiled=True),
    )
    head_grads = lax.psum((grad_qgain, grad_kgain), ("dp", "seq"))
    return (
        output,
        grad_tokens,
        attn_grads[0],
        attn_grads[1],
        attn_grads[2],
        attn_grads[3],
        attn_grads[4],
        head_grads[0],
        head_grads[1],
        mlp_grads[0],
        mlp_grads[1],
        mlp_grads[2],
        mlp_grads[3],
    )


def solution(mesh):
    in_specs = (
        P("dp", "seq", None),
        P("dp", None),
        P(("dp", "seq"), None),
        P(("dp", "seq"), None),
        P(("dp", "seq"), None),
        P(("dp", "seq"), None),
        P(("dp", "seq")),
        P(),
        P(),
        P(("dp", "seq"), None),
        P(("dp", "seq"), None),
        P(("dp", "seq"), None),
        P(("dp", "seq")),
        P("dp", "seq", None),
    )
    out_specs = (
        P("dp", "seq", None),
        P("dp", "seq", None),
        P(("dp", "seq"), None),
        P(("dp", "seq"), None),
        P(("dp", "seq"), None),
        P(("dp", "seq"), None),
        P(("dp", "seq")),
        P(),
        P(),
        P(("dp", "seq"), None),
        P(("dp", "seq"), None),
        P(("dp", "seq"), None),
        P(("dp", "seq")),
    )
    return jax.shard_map(body, mesh=mesh, in_specs=in_specs, out_specs=out_specs, check_vma=False)
```

profile of v0, /device:TPU:0, one launch (start us, length us, event | category | flops | bytes accessed | tf_op | source)
XLA Modules:
  0.0 1955.6 jit_solution(18228670385323394021)
XLA Ops:
  11.2 42.0 %all-reduce.5 = (bf16[1024]{0:T(1024)(128)(2,1)S(1)}, bf16[1024]{0:T(1024)(128)(2,1)S(1)}) all-reduce(bf16[1024]{0:T(1024)(128)(2,1)S(1)} %dynamic-update-slice, bf16[1024]{0:T(1024)(128)(2,1)S(1)} %dynamic-update-slice.1), channel_id=1, replica_groups=mesh['dp'=4,'seq'=8] {'dp','seq'}, use_global_device_ids=true, to_apply=%add | all-reduce | flops 2048 | bytes 8192
  55.3 12.2 all-gather.11.cloned.1.call-done
  71.4 52.1 %all-gather.17.cloned.1.call-done = bf16[1024,512]{1,0:T(8,128)(2,1)} async-done(((bf16[32,512]{1,0:T(8,128)(2,1)}), bf16[1024,512]{1,0:T(8,128)(2,1)}) %all-gather.17.cloned.1.call-update) | async-done | bytes 1048592 | tf_op jit(solution)/shard_map/all_gather | solution.py:100
  123.4 2.4 convolution_convert_fusion.1
  128.8 53.0 %all-gather.15.cloned.1.call-done = bf16[1024,1024]{1,0:T(8,128)(2,1)} async-done(((bf16[32,1024]{1,0:T(8,128)(2,1)}), bf16[1024,1024]{1,0:T(8,128)(2,1)}) %all-gather.15.cloned.1.call-update) | async-done | bytes 2097168 | tf_op jit(solution)/shard_map/all_gather | solution.py:98
  181.8 2.3 fusion.84
  185.9 27.4 %all-gather.13.cloned.1.call-done = bf16[1,2048,512]{1,2,0:T(8,128)(2,1)} async-done(((bf16[1,256,512]{1,2,0:T(8,128)(2,1)}), bf16[1,2048,512]{1,2,0:T(8,128)(2,1)}) %all-gather.13.cloned.1.call-update) | async-done | bytes 2097168 | tf_op jit(solution)/shard_map/all_gather | solution.py:133
  213.3 30.2 %all-gather.27.cloned.1.call-done = bf16[2048,512]{1,0:T(8,128)(2,1)} async-done(((bf16[256,512]{1,0:T(8,128)(2,1)}), bf16[2048,512]{1,0:T(8,128)(2,1)}) %all-gather.27.cloned.1.call-update) | async-done | bytes 2097168 | tf_op jit(solution)/shard_map/all_gather | solution.py:134
  243.5 36.5 %conditional.1 = (f32[1,8,2,256]{3,2,1,0:T(2,128)}, f32[1,256,8,2,64]{1,4,3,2,0:T(8,128)S(1)}, f32[1,8,2,256]{3,2,1,0:T(2,128)S(1)}) conditional(s32[]{:T(128)} %convert_element_type.133, () %tuple.22, (s32[256]{0:T(256)S(1)}, s32[1,2048]{1,0:T(1,128)S(1)}, s32[1,256]{1,0:T(1,128)S(1)}, bf16[1,2048,512]{1,2,0:T(8,128)(2,1)}, ...), branch_computations={%region_3.0_spmd, %region_4.6_spmd} | conditional | flops 2199384064 | bytes 80799800 | solution.py:156
  244.3 17.1 fusion.3
  261.4 3.9 copy.94
  265.4 14.0 fusion.9
  280.9 21.2 %all-gather.19.cloned.1.call-done = bf16[1024,1024]{1,0:T(8,128)(2,1)} async-done(((bf16[32,1024]{1,0:T(8,128)(2,1)}), bf16[1024,1024]{1,0:T(8,128)(2,1)}) %all-gather.19.cloned.1.call-update) | async-done | bytes 2097168 | tf_op jit(solution)/shard_map/all_gather | solution.py:101
  302.2 2.4 multiply_reduce_fusion.3
  304.8 80.8 %all-gather.21.cloned.1.call-done = bf16[1024,4608]{1,0:T(8,128)(2,1)} async-done(((bf16[32,4608]{1,0:T(8,128)(2,1)}), bf16[1024,4608]{1,0:T(8,128)(2,1)}) %all-gather.21.cloned.1.call-update) | async-done | bytes 9437200 | tf_op jit(solution)/shard_map/all_gather | solution.py:164
  385.6 7.9 fusion.88
  393.6 75.2 %all-gather.23.cloned.1.call-done = bf16[1024,4608]{1,0:T(8,128)(2,1)} async-done(((bf16[32,4608]{1,0:T(8,128)(2,1)}), bf16[1024,4608]{1,0:T(8,128)(2,1)}) %all-gather.23.cloned.1.call-update) | async-done | bytes 9437200 | tf_op jit(solution)/shard_map/all_gather | solution.py:165
  468.8 8.0 fusion.89
  476.7 75.2 %all-gather.25.cloned.1.call-done = bf16[4608,1024]{1,0:T(8,128)(2,1)} async-done(((bf16[144,1024]{1,0:T(8,128)(2,1)}), bf16[4608,1024]{1,0:T(8,128)(2,1)}) %all-gather.25.cloned.1.call-update) | async-done | bytes 9437200 | tf_op jit(solution)/shard_map/all_gather | solution.py:166
  551.9 13.6 multiply_convert_fusion
  565.5 6.9 fusion.90
  573.6 3.4 fusion.55
  584.3 23.2 %while.15 = (s32[]{:T(128)}, f32[1,256,8,2,64]{1,4,3,2,0:T(8,128)S(1)}, bf16[1,2048,512]{1,2,0:T(8,128)(2,1)}, bf16[1,2048,512]{1,2,0:T(8,128)(2,1)}, s32[]{:T(1...) while((s32[]{:T(128)}, ...), condition=%wide.region_10.11_spmd.clone, body=%wide.region_9.10_spmd.clone.sunk | while | flops 1364591360 | bytes 52360452 | solution.py:290
  585.7 4.6 fusion.156
  592.3 6.4 fusion.157
  600.1 5.1 fusion.159
  609.5 101.2 %reduce-scatter.10.cloned.1.call-done = bf16[1,256,512]{1,2,0:T(8,128)(2,1)} async-done(((bf16[1,2048,512]{1,2,0:T(8,128)(2,1)}), bf16[1,256,512]{1,2,0:T(8,128)(2,1)}) %reduce-scatter.10.cloned.1.call-update) | async-done | bytes 262160 | tf_op jit(solution)/shard_map/reduce_scatter | solution.py:292
  714.7 1.9 fusion.79
  717.8 2.5 copy.101
  724.6 2.1 multiply_reduce_fusion
  726.7 2.8 fusion.81
  729.6 18.1 reduce-scatter.12.cloned.1.call-done
  747.7 2.8 fusion.72
  750.6 2.7 fusion.65
  753.4 9.6 fusion.92
  763.1 9.6 fusion.93
  773.8 9.5 fusion.68
  783.4 3.4 fusion.91
  786.8 7.9 fusion.38
  794.8 2.0 convolution_add_fusion.1
  798.8 38.2 %all-reduce.4 = (f32[1024]{0:T(1024)S(1)}, f32[64]{0:T(128)}, f32[64]{0:T(128)}, f32[1024]{0:T(1024)S(1)}) all-reduce(f32[1024]{0:T(1024)S(1)} %get-tuple-element.230, f32[64]{0:T(128)S(1)} %reduce_sum.157, f32[64]{0:T(128)S(1)} %reduce_sum.160, f32[1024]{0:T(1024)S(1)} %copy-done.41), channel_id=9, replica_groups=mesh['dp'=4,'seq'=8] {'dp','seq'}, use_global_device_ids=true, to_apply=%region_21.22.clone | all-reduce | flops 2176 | bytes 17408
  839.5 48.1 %reduce-scatter.16.cloned.1.call-done = f32[32,512]{1,0:T(8,128)} async-done(((f32[1024,512]{1,0:T(8,128)}), f32[32,512]{1,0:T(8,128)}) %reduce-scatter.16.cloned.1.call-update) | async-done | bytes 65552 | tf_op jit(solution)/shard_map/reduce_scatter | solution.py:334
  887.6 143.7 %reduce-scatter.14.cloned.1.call-done = f32[32,1024]{1,0:T(8,128)} async-done(((f32[1024,1024]{1,0:T(8,128)}), f32[32,1024]{1,0:T(8,128)}) %reduce-scatter.14.cloned.1.call-update) | async-done | bytes 131088 | tf_op jit(solution)/shard_map/reduce_scatter | solution.py:333
  1031.2 137.6 %reduce-scatter.18.cloned.1.call-done = f32[32,512]{1,0:T(8,128)} async-done(((f32[1024,512]{1,0:T(8,128)}), f32[32,512]{1,0:T(8,128)}) %reduce-scatter.18.cloned.1.call-update) | async-done | bytes 65552 | tf_op jit(solution)/shard_map/reduce_scatter | solution.py:335
  1168.8 143.6 %reduce-scatter.20.cloned.1.call-done = f32[32,1024]{1,0:T(8,128)} async-done(((f32[1024,1024]{1,0:T(8,128)}), f32[32,1024]{1,0:T(8,128)}) %reduce-scatter.20.cloned.1.call-update) | async-done | bytes 131088 | tf_op jit(solution)/shard_map/reduce_scatter | solution.py:336
  1312.4 210.1 %reduce-scatter.22.cloned.1.call-done = f32[32,4608]{1,0:T(8,128)} async-done(((f32[1024,4608]{1,0:T(8,128)}), f32[32,4608]{1,0:T(8,128)}) %reduce-scatter.22.cloned.1.call-update) | async-done | bytes 589840 | tf_op jit(solution)/shard_map/reduce_scatter | solution.py:205
  1522.6 213.0 %reduce-scatter.24.cloned.1.call-done = f32[32,4608]{1,0:T(8,128)} async-done(((f32[1024,4608]{1,0:T(8,128)}), f32[32,4608]{1,0:T(8,128)}) %reduce-scatter.24.cloned.1.call-update) | async-done | bytes 589840 | tf_op jit(solution)/shard_map/reduce_scatter | solution.py:206
  1735.6 213.0 %reduce-scatter.26.cloned.1.call-done = f32[144,1024]{1,0:T(8,128)} async-done(((f32[4608,1024]{1,0:T(8,128)}), f32[144,1024]{1,0:T(8,128)}) %reduce-scatter.26.cloned.1.call-update) | async-done | bytes 589840 | tf_op jit(solution)/shard_map/reduce_scatter | solution.py:207
  (215 shorter events, 48.7 us)
Async XLA Ops:
  7.2 116.2 %copy-start = (bf16[1,256,1024]{2,1,0:T(8,128)(2,1)S(1)}, bf16[1,256,1024]{2,1,0:T(8,128)(2,1)}, u32[]{:S(2)}) copy-start(bf16[1,256,1024]{2,1,0:T(8,128)(2,1)} %param.18) | copy-start | bytes 1572868
  7.2 60.4 %all-gather.11.cloned.1.call-start = ((), (), s32[]{:S(2)}) async-start(), calls=%async_computation.9 | async-start | bytes 1081344 | tf_op jit(solution)/shard_map/all_gather | solution.py:99
  7.9 115.5 %all-gather.17.cloned.1.call-start = ((), (), s32[]{:S(2)}) async-start(), calls=%async_computation.12 | async-start | bytes 1081344 | tf_op jit(solution)/shard_map/all_gather | solution.py:100
  8.7 173.1 %all-gather.15.cloned.1.call-start = ((), (), s32[]{:S(2)}) async-start(), calls=%async_computation.11 | async-start | bytes 2162688 | tf_op jit(solution)/shard_map/all_gather | solution.py:98
  9.4 203.9 %all-gather.13.cloned.1.call-start = ((), (), s32[]{:S(2)}) async-start(), calls=%async_computation.10 | async-start | bytes 2359296 | tf_op jit(solution)/shard_map/all_gather | solution.py:133
  53.2 128.6 %copy-start.32 = (f32[1024]{0:T(1024)}, f32[1024]{0:T(1024)S(1)}, u32[]{:S(2)}) copy-start(f32[1024]{0:T(1024)S(1)} %convert_element_type.134) | copy-start | bytes 12292
  53.8 72.0 %copy-start.42 = (f32[64]{0:T(128)}, f32[64]{0:T(128)S(1)}, u32[]{:S(2)}) copy-start(f32[64]{0:T(128)S(1)} %convert_element_type.136) | copy-start | bytes 772
  55.1 126.7 %copy-start.36 = (f32[256]{0:T(256)}, f32[256]{0:T(256)S(1)}, u32[]{:S(2)}) copy-start(f32[256]{0:T(256)S(1)} %add_rsqrt_fusion.3) | copy-start | bytes 3076
  55.3 130.3 %copy-start.27 = (f32[256,32]{0,1:T(8,128)}, f32[256,32]{0,1:T(8,128)S(1)}, u32[]{:S(2)}) copy-start(f32[256,32]{0,1:T(8,128)S(1)} %get-tuple-element.289) | copy-start | bytes 98308
  55.3 130.3 %copy-start.29 = (f32[256,32]{0,1:T(8,128)}, f32[256,32]{0,1:T(8,128)S(1)}, u32[]{:S(2)}) copy-start(f32[256,32]{0,1:T(8,128)S(1)} %get-tuple-element.290) | copy-start | bytes 98308
  55.3 73.4 %copy-start.47 = (bf16[64]{0:T(256)(128)(2,1)S(1)}, bf16[64]{0:T(256)(128)(2,1)}, u32[]{:S(2)}) copy-start(bf16[64]{0:T(256)(128)(2,1)} %param.25) | copy-start | bytes 388
  55.3 73.4 %copy-start.40 = (s32[1,2048]{1,0:T(1,128)S(1)}, s32[1,2048]{1,0:T(1,128)}, u32[]{:S(2)}) copy-start(s32[1,2048]{1,0:T(1,128)} %param.19) | copy-start | bytes 24580
  69.5 112.3 %copy-start.24 = (f32[256,512]{1,0:T(8,128)}, f32[256,512]{1,0:T(8,128)S(1)}, u32[]{:S(2)}) copy-start(f32[256,512]{1,0:T(8,128)S(1)} %fusion.86) | copy-start | bytes 1572868
  69.7 114.5 %copy-start.14 = (f32[256,512]{0,1:T(8,128)}, f32[256,512]{0,1:T(8,128)S(1)}, u32[]{:S(2)}) copy-start(f32[256,512]{0,1:T(8,128)S(1)} %copy.92) | copy-start | bytes 1572868
  71.3 172.2 %all-gather.27.cloned.1.call-start = ((), (), s32[]{:S(2)}) async-start(), calls=%async_computation.26 | async-start | bytes 2359296 | tf_op jit(solution)/shard_map/all_gather | solution.py:134
  125.9 176.3 %all-gather.19.cloned.1.call-start = ((), (), s32[]{:S(2)}) async-start(), calls=%async_computation.13 | async-start | bytes 2162688 | tf_op jit(solution)/shard_map/all_gather | solution.py:101
  126.4 259.2 %all-gather.21.cloned.1.call-start = ((), (), s32[]{:S(2)}) async-start(), calls=%async_computation.14 | async-start | bytes 9732096 | tf_op jit(solution)/shard_map/all_gather | solution.py:164
  127.2 341.6 %all-gather.23.cloned.1.call-start = ((), (), s32[]{:S(2)}) async-start(), calls=%async_computation.15 | async-start | bytes 9732096 | tf_op jit(solution)/shard_map/all_gather | solution.py:165
  127.9 424.0 %all-gather.25.cloned.1.call-start = ((), (), s32[]{:S(2)}) async-start(), calls=%async_computation.16 | async-start | bytes 9732096 | tf_op jit(solution)/shard_map/all_gather | solution.py:166
  128.7 582.0 %reduce-scatter.10.cloned.1.call-start = ((), (), s32[]{:S(2)}) async-start(), calls=%async_computation.17 | async-start | bytes 2359296 | tf_op jit(solution)/shard_map/reduce_scatter | solution.py:292
  128.7 57.1 %copy-start.44 = (f32[64]{0:T(128)}, f32[64]{0:T(128)S(1)}, u32[]{:S(2)}) copy-start(f32[64]{0:T(128)S(1)} %convert_element_type.139) | copy-start | bytes 772
  184.2 59.4 %copy-start.11 = (f32[256,1024]{1,0:T(8,128)}, f32[256,1024]{1,0:T(8,128)S(1)}, u32[]{:S(2)}) copy-start(f32[256,1024]{1,0:T(8,128)S(1)} %fusion.84) | copy-start | bytes 3145732
  184.5 59.0 %copy-start.1 = (f32[256,1024]{0,1:T(8,128)}, f32[256,1024]{0,1:T(8,128)S(1)}, u32[]{:S(2)}) copy-start(f32[256,1024]{0,1:T(8,128)S(1)} %copy.93) | copy-start | bytes 3145732
  244.3 17.1 copy-start.31
  280.1 22.1 %copy-start.10 = (f32[1,256,8,2,64]{1,4,3,2,0:T(8,128)}, f32[1,256,8,2,64]{1,4,3,2,0:T(8,128)S(1)}, u32[]{:S(2)}) copy-start(f32[1,256,8,2,64]{1,4,3,2,0:T(8,128)S(1)} %get-tuple-element.110) | copy-start | bytes 3145732
  280.9 23.7 %copy-start.16 = (bf16[1,256,8,2,64]{1,4,3,2,0:T(8,128)(2,1)}, bf16[1,256,8,2,64]{1,4,3,2,0:T(8,128)(2,1)S(1)}, u32[]{:S(2)}) copy-start(bf16[1,256,8,2,64]{1,4,3,2,0:T(8,128)(2,1)S(1)} %divide_convert_fusion) | copy-start | bytes 1572868
  304.6 272.5 %copy-start.8 = (f32[1,256,1024]{2,1,0:T(8,128)}, f32[1,256,1024]{2,1,0:T(8,128)S(1)}, u32[]{:S(2)}) copy-start(f32[1,256,1024]{2,1,0:T(8,128)S(1)} %get-tuple-element.292) | copy-start | bytes 3145732
  304.8 164.0 %copy-start.5 = (bf16[256,1024]{1,0:T(8,128)(2,1)}, bf16[256,1024]{1,0:T(8,128)(2,1)S(1)}, u32[]{:S(2)}) copy-start(bf16[256,1024]{1,0:T(8,128)(2,1)S(1)} %fusion.63) | copy-start | bytes 1572868
  393.6 158.3 %copy-start.22 = (bf16[1,256,1024]{2,1,0:T(8,128)(2,1)S(1)}, bf16[1,256,1024]{2,1,0:T(8,128)(2,1)}, u32[]{:S(2)}) copy-start(bf16[1,256,1024]{2,1,0:T(8,128)(2,1)} %param.31) | copy-start | bytes 1572868
  584.3 24.1 %copy-start.46 = (bf16[64]{0:T(256)(128)(2,1)S(1)}, bf16[64]{0:T(256)(128)(2,1)}, u32[]{:S(2)}) copy-start(bf16[64]{0:T(256)(128)(2,1)} %param.26) | copy-start | bytes 388
  584.3 24.2 %copy-start.39 = (f32[256,8]{0,1:T(8,128)S(1)}, f32[256,8]{0,1:T(8,128)}, u32[]{:S(2)}) copy-start(f32[256,8]{0,1:T(8,128)} %copy-done.38) | copy-start | bytes 24580
  607.5 104.2 %copy-start.28 = (f32[256,32]{0,1:T(8,128)S(1)}, f32[256,32]{0,1:T(8,128)}, u32[]{:S(2)}) copy-start(f32[256,32]{0,1:T(8,128)} %copy-done.27) | copy-start | bytes 98308
  607.5 104.2 %copy-start.30 = (f32[256,32]{0,1:T(8,128)S(1)}, f32[256,32]{0,1:T(8,128)}, u32[]{:S(2)}) copy-start(f32[256,32]{0,1:T(8,128)} %copy-done.29) | copy-start | bytes 98308
  607.5 104.3 %copy-start.15 = (f32[256,512]{0,1:T(8,128)S(1)}, f32[256,512]{0,1:T(8,128)}, u32[]{:S(2)}) copy-start(f32[256,512]{0,1:T(8,128)} %copy-done.14) | copy-start | bytes 1572868
  607.5 104.3 %copy-start.43 = (f32[64]{0:T(128)S(1)}, f32[64]{0:T(128)}, u32[]{:S(2)}) copy-start(f32[64]{0:T(128)} %copy-done.42) | copy-start | bytes 772
  607.6 140.1 %reduce-scatter.12.cloned.1.call-start = ((), (), s32[]{:S(2)}) async-start(), calls=%async_computation.18 | async-start | bytes 2359296 | tf_op jit(solution)/shard_map/reduce_scatter | solution.py:295
  607.6 105.6 %copy-start.25 = (f32[256,512]{1,0:T(8,128)S(1)}, f32[256,512]{1,0:T(8,128)}, u32[]{:S(2)}) copy-start(f32[256,512]{1,0:T(8,128)} %copy-done.24) | copy-start | bytes 1572868
  608.3 279.3 %reduce-scatter.16.cloned.1.call-start = ((), (), s32[]{:S(2)}) async-start(), calls=%async_computation.20 | async-start | bytes 2162688 | tf_op jit(solution)/shard_map/reduce_scatter | solution.py:334
  608.5 106.1 %copy-start.33 = (f32[1024]{0:T(1024)S(1)}, f32[1024]{0:T(1024)}, u32[]{:S(2)}) copy-start(f32[1024]{0:T(1024)} %copy-done.32) | copy-start | bytes 12292
  608.5 106.1 %copy-start.37 = (f32[256]{0:T(256)S(1)}, f32[256]{0:T(256)}, u32[]{:S(2)}) copy-start(f32[256]{0:T(256)} %copy-done.36) | copy-start | bytes 3076
  716.6 314.6 %reduce-scatter.14.cloned.1.call-start = ((), (), s32[]{:S(2)}) async-start(), calls=%async_computation.19 | async-start | bytes 4325376 | tf_op jit(solution)/shard_map/reduce_scatter | solution.py:333
  729.5 21.1 %copy-start.4 = (f32[1,256,1024]{2,1,0:T(8,128)S(1)}, f32[1,256,1024]{2,1,0:T(8,128)}, u32[]{:S(2)}) copy-start(f32[1,256,1024]{2,1,0:T(8,128)} %copy-done.3) | copy-start | bytes 3145732
  729.5 21.1 %copy-start.17 = (bf16[1,256,8,2,64]{1,4,3,2,0:T(8,128)(2,1)S(1)}, bf16[1,256,8,2,64]{1,4,3,2,0:T(8,128)(2,1)}, u32[]{:S(2)}) copy-start(bf16[1,256,8,2,64]{1,4,3,2,0:T(8,128)(2,1)} %copy-done.16) | copy-start | bytes 1572868
  729.5 439.2 %reduce-scatter.18.cloned.1.call-start = ((), (), s32[]{:S(2)}) async-start(), calls=%async_computation.21 | async-start | bytes 2162688 | tf_op jit(solution)/shard_map/reduce_scatter | solution.py:335
  750.6 561.9 %reduce-scatter.20.cloned.1.call-start = ((), (), s32[]{:S(2)}) async-start(), calls=%async_computation.22 | async-start | bytes 4325376 | tf_op jit(solution)/shard_map/reduce_scatter | solution.py:336
  753.3 769.2 %reduce-scatter.22.cloned.1.call-start = ((), (), s32[]{:S(2)}) async-start(), calls=%async_computation.23 | async-start | bytes 19464192 | tf_op jit(solution)/shard_map/reduce_scatter | solution.py:205
  763.0 972.6 %reduce-scatter.24.cloned.1.call-start = ((), (), s32[]{:S(2)}) async-start(), calls=%async_computation.24 | async-start | bytes 19464192 | tf_op jit(solution)/shard_map/reduce_scatter | solution.py:206
  772.7 1175.8 %reduce-scatter.26.cloned.1.call-start = ((), (), s32[]{:S(2)}) async-start(), calls=%async_computation.25 | async-start | bytes 19464192 | tf_op jit(solution)/shard_map/reduce_scatter | solution.py:207
  (19 other events, 80.7 us)
Sparse Core Ops, SparseCore 0:
  11.0 56.5 all-gather.10
  70.6 52.7 all-gather.16
  126.4 55.3 all-gather.14
  183.8 29.4 all-gather.12
  215.3 28.1 all-gather.26
  246.4 55.7 all-gather.18
  305.2 80.3 all-gather.20
  388.6 80.0 all-gather.22
  471.8 80.0 all-gather.24
  607.7 102.9 reduce-scatter.9
  713.0 34.6 reduce-scatter.11
  750.4 137.1 reduce-scatter.15
  890.4 140.7 reduce-scatter.13
  1033.9 134.8 reduce-scatter.17
  1171.5 140.9 reduce-scatter.19
  1319.3 203.2 reduce-scatter.21
  1529.4 206.1 reduce-scatter.23
  1742.4 206.0 reduce-scatter.25
where the time goes:
time: 1960 us
  waiting for transfers between devices  1660 us (85%)
  matrix products  153 us (8%)
  blocking collectives  80.2 us (4%)
  local copies, waits for them, and re-layouts  29.4 us (2%)
    reduce_scatter x1, waiting for transfers between devices, body(): lax.psum_scatter(grad_up_w, ('dp', 'seq'), scatter_dimension=0, tiled=True)  213 us
    reduce_scatter x1, waiting for transfers between devices, body(): lax.psum_scatter(grad_down_w, ('dp', 'seq'), scatter_dimension=0, tiled=T...  213 us
    reduce_scatter x1, waiting for transfers between devices, body(): lax.psum_scatter(grad_gate_w, ('dp', 'seq'), scatter_dimension=0, tiled=T...  210 us
    reduce_scatter x1, waiting for transfers between devices, body(): lax.psum_scatter(grad_query_w, ('dp', 'seq'), scatter_dimension=0, tiled=...  144 us
    reduce_scatter x1, waiting for transfers between devices, body(): lax.psum_scatter(grad_out_w, ('dp', 'seq'), scatter_dimension=0, tiled=True)  144 us
    reduce_scatter x1, waiting for transfers between devices, body(): lax.psum_scatter(grad_value_w, ('dp', 'seq'), scatter_dimension=0, tiled=...  138 us
    reduce_scatter x1, waiting for transfers between devices, body(): lax.psum_scatter(grad_keys.astype(jnp.bfloat16), 'seq', scatter_dimension...  101 us
    all_gather x1, waiting for transfers between devices, body(): lax.all_gather(w_gate, ('dp', 'seq'), axis=0, tiled=True)  80.8 us
  transfers between devices with their start and end apart: 18, of which 18 were waited for; matrix products, arithmetic and copies ran while one was open for 7% of the time, Pallas kernels for 0%

commit v1 on v0

v1 whole, which is shorter than its diff:
```python
import jax
import jax.numpy as jnp
from jax import lax
from jax.sharding import PartitionSpec as P

EPSILON = 1e-05
ROPE_BASE = 1000000.0
F32 = jnp.float32
BF16 = jnp.bfloat16
BOTH = ("dp", "seq")


def rms_scale(values):
    return lax.rsqrt(jnp.mean(values * values, axis=-1, keepdims=True) + EPSILON)


def rope_tables(positions, head_width):
    half_width = head_width // 2
    frequency = ROPE_BASE ** (-(jnp.arange(half_width, dtype=F32) * 2.0 / head_width))
    angles = positions.astype(F32)[:, None] * frequency[None, :]
    return (jnp.cos(angles), jnp.sin(angles))


def rotate(values, cosine_table, sine_table):
    half_width = values.shape[-1] // 2
    front_half = values[..., :half_width]
    back_half = values[..., half_width:]
    return jnp.concatenate(
        [
            front_half * cosine_table - back_half * sine_table,
            back_half * cosine_table + front_half * sine_table,
        ],
        axis=-1,
    )


def unrotate(incoming, cosine_table, sine_table):
    return rotate(incoming, cosine_table, -sine_table)


def norm_back(incoming, values, scale_vec, gain_vector, sum_axes):
    upstream = incoming * gain_vector
    grad_values = scale_vec * (
        upstream
        - values * scale_vec * scale_vec * jnp.mean(upstream * values, axis=-1, keepdims=True)
    )
    grad_gain = jnp.sum(incoming * values * scale_vec, axis=sum_axes)
    return (grad_values, grad_gain)


def dot(left, right):
    return jnp.dot(left, right, preferred_element_type=F32)


def dot_tn(left, right):
    return lax.dot_general(left, right, (((0,), (0,)), ((), ())), preferred_element_type=F32)


def dot_nt(left, right):
    return lax.dot_general(left, right, (((1,), (1,)), ((), ())), preferred_element_type=F32)


def swap_dp(value, bits, count):
    return lax.ppermute(value, "dp", [(i, i ^ bits) for i in range(count)])


def gather_dp(value, count):
    if count != 4:
        return lax.all_gather(value, "dp", axis=0, tiled=True)
    half = value.shape[0] // 2
    one = swap_dp(value, 1, count)
    two = swap_dp(value, 2, count)
    top = swap_dp(two[:half], 1, count)
    bottom = swap_dp(one[half:], 2, count)
    return jnp.concatenate([value, one, two, top, bottom], axis=0)


def scatter_sum_dp(parts, count):
    if count != 4:
        return lax.psum_scatter(parts, "dp", scatter_dimension=0, tiled=True).astype(F32)
    rows = parts.shape[0] // 4
    half = rows // 2
    own, one, two, far = (parts[i * rows : (i + 1) * rows] for i in range(4))
    top = swap_dp(far[:half], 1, count).astype(F32)
    bottom = swap_dp(far[half:], 2, count).astype(F32)
    two_sum = jnp.concatenate(
        [(two[:half].astype(F32) + top).astype(BF16), two[half:]], axis=0
    )
    one_sum = jnp.concatenate(
        [one[:half], (one[half:].astype(F32) + bottom).astype(BF16)], axis=0
    )
    from_one = swap_dp(one_sum, 1, count).astype(F32)
    from_two = swap_dp(two_sum, 2, count).astype(F32)
    return own.astype(F32) + from_one + from_two


def make_body(dp_count, seq_shards):
    def shift_seq(value, step):
        pairs = [(i, i + step) for i in range(seq_shards) if 0 <= i + step < seq_shards]
        return lax.ppermute(value, "seq", pairs)

    def swap_core(value):
        return lax.ppermute(value, "seq", [(i, i ^ 1) for i in range(seq_shards)])

    def body(
        tokens,
        segment_ids,
        w_query,
        w_key,
        w_value,
        w_out,
        attn_gain,
        query_gain,
        key_gain,
        w_gate,
        w_up,
        w_down,
        ffn_gain,
        cotangent,
    ):
        _, local_len, model_width = tokens.shape
        seq_len = segment_ids.shape[1]
        head_width = query_gain.shape[0]
        query_width = w_query.shape[1]
        key_width = w_key.shape[1]
        query_heads = query_width // head_width
        key_heads = key_width // head_width
        group_size = query_heads // key_heads
        softmax_scale = head_width ** (-0.5)
        rows = w_query.shape[0]
        ffn_width = w_gate.shape[1]
        ffn_part = ffn_width // dp_count
        seq_rank = lax.axis_index("seq")
        core = seq_rank % 2
        first_row = seq_rank * local_len
        tokens = tokens[0]
        cotangent = cotangent[0]
        ids = segment_ids[0]

        reach = -(-(seq_len // 2 - 1) // local_len)
        hops = -(-reach // 2)

        gains = jnp.stack([attn_gain, ffn_gain], axis=1)
        gains = jnp.pad(gains, ((0, 0), (0, 126)))
        pack = jnp.concatenate([w_query, w_key, w_value, gains], axis=1)
        pack = lax.all_gather(pack, BOTH, axis=0, tiled=True)
        qkv_all = pack[:, : query_width + 2 * key_width]
        gain_cols = pack[:, query_width + 2 * key_width :].astype(F32)
        attn_gain_all = gain_cols[:, 0]
        ffn_gain_all = gain_cols[:, 1]
        out_all = lax.all_gather(w_out, BOTH, axis=0, tiled=True)

        gate_up = jnp.concatenate(
            [
                w_gate.reshape(rows, dp_count, ffn_part),
                w_up.reshape(rows, dp_count, ffn_part),
            ],
            axis=2,
        )
        gate_up = lax.all_to_all(jnp.moveaxis(gate_up, 1, 0), "dp", 0, 0, tiled=True)
        down_all = lax.all_gather(w_down, "seq", axis=0, tiled=True)
        gate_up_all = lax.all_gather(gate_up, "seq", axis=1, tiled=True).reshape(
            model_width, 2 * ffn_part
        )
        cotangent_all = gather_dp(cotangent, dp_count)

        stream = tokens.astype(F32)
        scale_one = rms_scale(stream)
        normed_one = (stream * scale_one * attn_gain_all).astype(BF16)
        positions = first_row + jnp.arange(local_len, dtype=jnp.int32)
        cosine_table, sine_table = rope_tables(positions, head_width)
        cosine_table = cosine_table[:, None, :]
        sine_table = sine_table[:, None, :]
        qkv = dot(normed_one, qkv_all)
        query_pre = qkv[:, :query_width].reshape(local_len, query_heads, head_width)
        key_pre = qkv[:, query_width : query_width + key_width].reshape(
            local_len, key_heads, head_width
        )
        value_send = qkv[:, query_width + key_width :].astype(BF16)
        query_scale = rms_scale(query_pre)
        key_scale = rms_scale(key_pre)
        query_gain_f = query_gain.astype(F32)
        key_gain_f = key_gain.astype(F32)
        query_rot = rotate(
            query_pre * query_scale * query_gain_f, cosine_table, sine_table
        ).astype(BF16)
        key_rot = (
            rotate(key_pre * key_scale * key_gain_f, cosine_table, sine_table)
            .astype(BF16)
            .reshape(local_len, key_width)
        )

        both = [jnp.concatenate([key_rot, value_send], axis=1)]
        for _ in range(hops):
            both.append(shift_seq(both[-1], 2))
        for_even = jnp.concatenate(both[:-1], axis=0)
        for_odd = jnp.concatenate(both[1:], axis=0)
        across = swap_core(jnp.where(core == 0, for_even, for_odd))
        window = jnp.concatenate(both + [across], axis=0)
        block_steps = [-2 * i for i in range(hops + 1)] + [-1 - 2 * i for i in range(hops)]
        starts = [first_row + step * local_len for step in block_steps]
        key_pos = jnp.concatenate([start + jnp.arange(local_len, dtype=jnp.int32) for start in starts])
        key_ids = jnp.concatenate(
            [
                lax.dynamic_slice_in_dim(ids, jnp.maximum(start, 0), local_len, 0)
                for start in starts
            ]
        )
        query_ids = lax.dynamic_slice_in_dim(ids, first_row, local_len, 0)
        allowed = (
            (key_pos[None, :] <= positions[:, None])
            & (key_pos[None, :] >= 0)
            & (key_ids[None, :] == query_ids[:, None])
        )[None, None]
        window_len = window.shape[0]
        keys = window[:, :key_width].reshape(window_len, key_heads, head_width)
        values = window[:, key_width:].reshape(window_len, key_heads, head_width)
        queries = query_rot.reshape(local_len, key_heads, group_size, head_width)
        scores = (
            jnp.einsum("qgrd,kgd->grqk", queries, keys, preferred_element_type=F32)
            * softmax_scale
        )
        weights = jnp.where(allowed, jnp.exp(scores), 0.0)
        denominator = jnp.sum(weights, axis=-1)
        summed = jnp.einsum(
            "grqk,kgd->qgrd", weights.astype(BF16), values, preferred_element_type=F32
        )
        attended = (summed / jnp.moveaxis(denominator, 2, 0)[..., None]).astype(BF16)
        log_total = jnp.log(denominator)
        attended_flat = attended.reshape(local_len, query_width)
        middle = stream + dot(attended_flat, out_all)

        scale_two = rms_scale(middle)
        normed_two = (middle * scale_two * ffn_gain_all).astype(BF16)
        normed_all = gather_dp(normed_two, dp_count)
        both_pre = dot(normed_all, gate_up_all)
        gate_pre = both_pre[:, :ffn_part]
        up_pre = both_pre[:, ffn_part:]
        sigmoid_gate = jax.nn.sigmoid(gate_pre)
        silu_gate = gate_pre * sigmoid_gate
        hidden = (silu_gate * up_pre).astype(BF16)
        out_part = dot(hidden, down_all).astype(BF16)
        output = (middle + scatter_sum_dp(out_part, dp_count)).astype(BF16)
        grad_output = cotangent.astype(F32)
        grad_hidden = dot_nt(cotangent_all, down_all)
        grad_gate = (
            grad_hidden * up_pre * sigmoid_gate * (1.0 + gate_pre * (1.0 - sigmoid_gate))
        ).astype(BF16)
        grad_up = (grad_hidden * silu_gate).astype(BF16)
        grad_both = jnp.concatenate([grad_gate, grad_up], axis=1)
        grad_normed_two = scatter_sum_dp(dot_nt(grad_both, gate_up_all).astype(BF16), dp_count)
        grad_down_w = lax.psum_scatter(
            dot_tn(hidden, cotangent_all).astype(BF16), "seq", scatter_dimension=0, tiled=True
        )
        grad_gate_up = lax.psum_scatter(
            dot_tn(normed_all, grad_both)
            .astype(BF16)
            .reshape(dp_count, seq_shards * rows, 2 * ffn_part),
            "seq",
            scatter_dimension=1,
            tiled=True,
        )
        grad_gate_up = lax.all_to_all(grad_gate_up, "dp", 0, 0, tiled=True).astype(F32)
        grad_gate_up = jnp.moveaxis(grad_gate_up, 0, 1)
        grad_gate_w = grad_gate_up[..., :ffn_part].reshape(rows, ffn_width)
        grad_up_w = grad_gate_up[..., ffn_part:].reshape(rows, ffn_width)

        grad_mid_norm, grad_ffn_gain = norm_back(
            grad_normed_two, middle, scale_two, ffn_gain_all, (0,)
        )
        grad_middle = grad_output + grad_mid_norm

        grad_middle_bf = grad_middle.astype(BF16)
        grad_out_w = lax.psum_scatter(
            dot_tn(attended_flat, grad_middle_bf).astype(BF16),
            BOTH,
            scatter_dimension=0,
            tiled=True,
        )
        grad_attended = (
            dot_nt(grad_middle_bf, out_all)
            .astype(BF16)
            .reshape(local_len, key_heads, group_size, head_width)
        )
        delta_rows = jnp.moveaxis(
            jnp.sum(grad_attended.astype(F32) * attended.astype(F32), axis=-1), 0, 2
        )
        probabilities = jnp.where(allowed, jnp.exp(scores - log_total[..., None]), 0.0)
        grad_probs = jnp.einsum(
            "qgrd,kgd->grqk", grad_attended, values, preferred_element_type=F32
        )
        grad_scores = (probabilities * (grad_probs - delta_rows[..., None])).astype(BF16)
        value_term = jnp.einsum(
            "grqk,qgrd->kgd",
            probabilities.astype(BF16),
            grad_attended,
            preferred_element_type=F32,
        )
        key_term = (
            jnp.einsum("grqk,qgrd->kgd", grad_scores, queries, preferred_element_type=F32)
            * softmax_scale
        )
        grad_query = (
            jnp.einsum("grqk,kgd->qgrd", grad_scores, keys, preferred_element_type=F32)
            * softmax_scale
        )
        grad_window = jnp.concatenate(
            [
                key_term.reshape(window_len, key_width),
                value_term.reshape(window_len, key_width),
            ],
            axis=1,
        ).astype(BF16)
        split = (hops + 1) * local_len
        back = swap_core(grad_window[split:])
        zero = jnp.zeros((local_len, 2 * key_width), BF16)
        back = jnp.where(
            core == 0,
            jnp.concatenate([back, zero], axis=0),
            jnp.concatenate([zero, back], axis=0),
        )
        total = grad_window[:split].astype(F32) + back.astype(F32)
        running = total[hops * local_len :]
        for step in range(hops - 1, -1, -1):
            arrived = shift_seq(running.astype(BF16), -2)
            running = total[step * local_len : (step + 1) * local_len] + arrived.astype(F32)
        key_sum = running[:, :key_width]
        value_grad_bf = running[:, key_width:].astype(BF16)
        grad_qnorm = unrotate(
            grad_query.reshape(local_len, query_heads, head_width), cosine_table, sine_table
        )
        grad_qpre, grad_qgain = norm_back(
            grad_qnorm, query_pre, query_scale, query_gain_f, (0, 1)
        )
        grad_knorm = unrotate(
            key_sum.reshape(local_len, key_heads, head_width), cosine_table, sine_table
        )
        grad_kpre, grad_kgain = norm_back(grad_knorm, key_pre, key_scale, key_gain_f, (0, 1))
        grad_qkv = jnp.concatenate(
            [
                grad_qpre.reshape(local_len, query_width).astype(BF16),
                grad_kpre.reshape(local_len, key_width).astype(BF16),
                value_grad_bf,
            ],
            axis=1,
        )
        grad_qkv_w = lax.psum_scatter(
            dot_tn(normed_one, grad_qkv).astype(BF16), BOTH, scatter_dimension=0, tiled=True
        ).astype(F32)
        grad_normed_one = dot_nt(grad_qkv, qkv_all)
        grad_stream, grad_attn_gain = norm_back(
            grad_normed_one, stream, scale_one, attn_gain_all, (0,)
        )
        grad_tokens = grad_middle + grad_stream

        devices = dp_count * seq_shards
        head_gains = jnp.concatenate([grad_qgain, grad_kgain])
        small = jnp.concatenate(
            [
                grad_attn_gain.reshape(devices, rows),
                grad_ffn_gain.reshape(devices, rows),
                jnp.broadcast_to(head_gains, (devices, 2 * head_width)),
            ],
            axis=1,
        )
        small = jnp.sum(lax.all_to_all(small, BOTH, 0, 0, tiled=True), axis=0)
        return (
            output[None],
            grad_tokens[None],
            grad_qkv_w[:, :query_width],
            grad_qkv_w[:, query_width : query_width + key_width],
            grad_qkv_w[:, query_width + key_width :],
            grad_out_w.astype(F32),
            small[:rows],
            small[2 * rows : 2 * rows + head_width],
            small[2 * rows + head_width :],
            grad_gate_w,
            grad_up_w,
            grad_down_w.astype(F32),
            small[rows : 2 * rows],
        )

    return body


def solution(mesh):
    in_specs = (
        P("dp", "seq", None),
        P("dp", None),
        P(BOTH, None),
        P(BOTH, None),
        P(BOTH, None),
        P(BOTH, None),
        P(BOTH),
        P(),
        P(),
        P(BOTH, None),
        P(BOTH, None),
        P(BOTH, None),
        P(BOTH),
        P("dp", "seq", None),
    )
    out_specs = (
        P("dp", "seq", None),
        P("dp", "seq", None),
        P(BOTH, None),
        P(BOTH, None),
        P(BOTH, None),
        P(BOTH, None),
        P(BOTH),
        P(),
        P(),
        P(BOTH, None),
        P(BOTH, None),
        P(BOTH, None),
        P(BOTH),
    )
    body = make_body(mesh.shape["dp"], mesh.shape["seq"])
    return jax.shard_map(body, mesh=mesh, in_specs=in_specs, out_specs=out_specs, check_vma=False)
```

time: 1960 us -> 632 us (0.32)
  waiting for transfers between devices: 1660 us -> 340 us
  blocking collectives: 80.2 us -> 15.5 us
  starting transfers between devices: 0.89 us -> 35.6 us
  matrix products: 153 us -> 121 us
  other arithmetic: 14.8 us -> 42.4 us
  local copies, waits for them, and re-layouts: 29.4 us -> 55.8 us
    reduce_scatter x9 -> x4, waiting for transfers between devices: 1230 us -> 192 us  [the longest x1 139 us: body(): lax.psum_scatter(dot_tn(normed_one, grad_qkv).astype(BF16), BOTH, scatter...]
    all_gather x9 -> x4, waiting for transfers between devices: 427 us -> 60.8 us  [the longest x1 45.9 us: body(): pack = lax.all_gather(pack, BOTH, axis=0, tiled=True)]
    ppermute x0 -> x22, waiting for transfers between devices: none -> 80.9 us  [the longest x4 53.2 us: shift_seq(): return lax.ppermute(value, 'seq', pairs)]
    unnamed x2 -> x0, blocking collectives: 80.2 us -> none
    dot_general x28 -> x18, matrix products: 153 us -> 121 us  [the longest x4 23.6 us: dot_nt(): lax.dot_general(left, right, (((1,), (1,)), ((), ())), preferred_element_...]
    ppermute x0 -> x22, starting transfers between devices: none -> 28.5 us  [the longest x16 17.8 us: swap_dp(): return lax.ppermute(value, 'dp', [(i, i ^ bits) for i in range(count)])]
  transfers between devices with their start and end apart: 18 -> 32, of which waited for: 18 -> 16; matrix products, arithmetic and copies ran while one was open for 7% -> 31% of each run, Pallas kernels for 0% -> 0%
where the time goes in v1:
time: 632 us; the launch traced here: 626 us
  waiting for transfers between devices  340 us (54%)
  matrix products  121 us (19%)
  local copies, waits for them, and re-layouts  55.8 us (9%)
  other arithmetic  42.4 us (7%)
  starting transfers between devices  35.6 us (6%)
  between operations  15.6 us (2%)
  blocking collectives  15.5 us (2%)
    reduce_scatter x1, waiting for transfers between devices, body(): lax.psum_scatter(dot_tn(normed_one, grad_qkv).astype(BF16), BOTH, scatter...  139 us
    ppermute x4, waiting for transfers between devices, shift_seq(): return lax.ppermute(value, 'seq', pairs)  53.2 us
    reduce_scatter x1, waiting for transfers between devices, body(): lax.psum_scatter(dot_tn(attended_flat, grad_middle_bf).astype(BF16), BOTH...  52.5 us
    all_gather x1, waiting for transfers between devices, body(): pack = lax.all_gather(pack, BOTH, axis=0, tiled=True)  45.9 us
    ppermute x16, waiting for transfers between devices, swap_dp(): return lax.ppermute(value, 'dp', [(i, i ^ bits) for i in range(count)])  27.7 us
    dot_general x4, matrix products, dot_nt(): lax.dot_general(left, right, (((1,), (1,)), ((), ())), preferred_element_...  23.6 us
    dot_general x4, matrix products, dot(): return jnp.dot(left, right, preferred_element_type=F32)  19.2 us
    dot_general x4, matrix products, dot_tn(): lax.dot_general(left, right, (((0,), (0,)), ((), ())), preferred_element_...  18.9 us
  transfers between devices with their start and end apart: 32, of which 16 were waited for; matrix products, arithmetic and copies ran while one was open for 31% of the time, Pallas kernels for 0%

profile of v1, /device:TPU:0, one launch (start us, length us, event | category | flops | bytes accessed | tf_op | source)
XLA Modules:
  0.0 625.7 jit_solution(14495514735594717104)
XLA Ops:
  12.8 15.5 %all_to_all.19 = bf16[4,32,2304]{2,1,0:T(8,128)(2,1)S(1)} all-to-all(bf16[4,32,2304]{2,1,0:T(8,128)(2,1)S(1)} %copy.146), channel_id=1, replica_groups=mesh['dp'=4,'seq'=8] {'dp'}, dimensions={0} | all-to-all | bytes 1179648 | tf_op jit(solution)/shard_map/all_to_all | solution.py:160
  31.7 45.9 %all-gather.5.cloned.1.call-done = bf16[1024,2176]{1,0:T(8,128)(2,1)} async-done(((bf16[32,2176]{1,0:T(8,128)(2,1)}), bf16[1024,2176]{1,0:T(8,128)(2,1)}) %all-gather.5.cloned.1.call-update) | async-done | bytes 4456464 | tf_op jit(solution)/shard_map/all_gather | solution.py:146
  79.6 3.5 fusion.20
  84.0 3.3 collective-permute-start
  87.5 12.8 %collective-permute-done = bf16[256,1024]{1,0:T(8,128)(2,1)S(1)} collective-permute-done((bf16[256,1024]{1,0:T(8,128)(2,1)S(1)}, bf16[256,1024]{1,0:T(8,128)(2,1)S(1)}, u32[]{:S(2)}, u32[]{:S(2)}) %collective-permute-start) | collective-permute-done | bytes 524320 | tf_op jit(solution)/shard_map/ppermute | solution.py:100
  100.3 4.6 collective-permute-start.1
  104.9 13.0 %collective-permute-done.1 = bf16[256,1024]{1,0:T(8,128)(2,1)S(1)} collective-permute-done((bf16[256,1024]{1,0:T(8,128)(2,1)S(1)}, bf16[256,1024]{1,0:T(8,128)(2,1)S(1)}, u32[]{:S(2)}, u32[]{:S(2)}) %collective-permute-start.1) | collective-permute-done | bytes 524320 | tf_op jit(solution)/shard_map/ppermute | solution.py:100
  129.5 3.2 pad_maximum_fusion.3
  136.0 2.9 copy.142
  138.9 10.0 %fusion.5 = (f32[8,2,256]{2,1,0:T(2,128)S(1)}, f32[8,1280,256,2]{2,1,3,0:T(8,128)}) fusion(pred[256,1280]{0,1:T(8,128)(4,1)S(1)} %compare_and_fusion, bf16[1280,8,64,1]{0,2,3,1:T(8,128)(2,1)S(1)} %bitcast.153, bf16[256,8,2,32]{0,3,2,1:T(8,128)(2,1)S(1)} %bitcast.173, bf16[256,8,2,32]{0,3,2,1:T(8,128)(2,1)S(1)} %bitcast.171), kind=kOutput, calls=%fused_computation.9 | convolution fusion | flops 687861760 | bytes 23150592 | tf_op jit(solution)/shard_map/qgrd,kgd->grqk/dot_general | solution.py:220
  148.9 10.6 %divide_convert_fusion = bf16[256,8,2,64]{0,3,2,1:T(8,128)(2,1)S(1)} fusion(bf16[1280,8,64,1]{0,2,3,1:T(8,128)(2,1)S(1)} %bitcast.156, f32[8,1280,256,2]{2,1,3,0:T(8,128)} %get-tuple-element.74, pred[256,1280]{0,1:T(8,128)(4,1)S(1)} %compare_and_fusion, f32[256,8,2]{0,2,1:T(2,128)S(1)} %bitcast.178), kind=kOutput, calls=%fused_computation.91 | convolution fusion | flops 682098688 | bytes 23150592 | tf_op jit(solution)/shard_map/grqk,kgd->qgrd/dot_general | solution.py:225
  159.6 2.6 multiply_reduce_fusion.5
  174.2 4.6 collective-permute-done.4
  181.1 2.2 collective-permute-done.14
  184.1 3.8 all-gather.9.cloned.1.call-done
  187.9 3.1 copy.148
  193.6 5.9 collective-permute-done.6
  200.8 7.7 %fusion.82 = f32[1024,2304]{1,0:T(8,128)} fusion(bf16[1024,1024]{1,0:T(8,128)(2,1)S(1)} %constant_dynamic-update-slice_fusion.2, bf16[1024,2304]{1,0:T(8,128)(2,1)S(1)} %bitcast.159), kind=kOutput, calls=%fused_computation.195 | convolution fusion | flops 4831838208 | bytes 16252928 | tf_op jit(solution)/shard_map/dot_general | solution.py:52
  208.5 11.1 %all-gather.11.cloned.1.call-done = bf16[1152,1024]{1,0:T(8,128)(2,1)} async-done(((bf16[144,1024]{1,0:T(8,128)(2,1)}), bf16[1152,1024]{1,0:T(8,128)(2,1)}) %all-gather.11.cloned.1.call-update) | async-done | bytes 2359312 | tf_op jit(solution)/shard_map/all_gather | solution.py:161
  219.6 10.8 %multiply_convert_fusion.1 = (bf16[1024,1152]{1,0:T(8,128)(2,1)S(1)}, bf16[1024,1152]{1,0:T(8,128)(2,1)S(1)}, bf16[1024,1152]{1,0:T(8,128)(2,1)}) fusion(f32[1024,2304]{1,0:T(8,128)} %fusion.82, bf16[1024,1024]{1,0:T(8,128)(2,1)} %constant_dynamic-update-slice_fusion.7, bf16[1152,1024]{1,0:T(8,128)(2,1)} %all-gather.11.cloned.1.call-done), kind=kOutput, calls=%fused_computation.22 | convolution fusion | flops 2433613824 | bytes 20971520 | tf_op jit(solution)/shard_map/dot_general | solution.py:60
  230.5 6.8 %convolution_convert_fusion = bf16[1024,2304]{1,0:T(8,128)(2,1)} fusion(bf16[1024,1024]{1,0:T(8,128)(2,1)S(1)} %copy-done.35, bf16[1024,1152]{1,0:T(8,128)(2,1)S(1)} %get-tuple-element.22, bf16[1024,1152]{1,0:T(8,128)(2,1)S(1)} %get-tuple-element.21), kind=kOutput, calls=%fused_computation.19 | convolution fusion | flops 4843634688 | bytes 11534336 | tf_op jit(solution)/shard_map/dot_general | solution.py:56
  238.6 5.4 convolution_convert_fusion.3
  247.1 8.1 %fusion.31 = bf16[1024,1024]{1,0:T(8,128)(2,1)S(1)} fusion(bf16[1024,2304]{1,0:T(8,128)(2,1)} %bitcast.160, bf16[1024,1152]{1,0:T(8,128)(2,1)S(1)} %copy-done.60, bf16[1024,1152]{1,0:T(8,128)(2,1)S(1)} %copy-done.58), kind=kOutput, calls=%fused_computation.48 | convolution fusion | flops 4842323968 | bytes 11534336 | tf_op jit(solution)/shard_map/dot_general | solution.py:60
  261.4 3.2 collective-permute-done.15
  269.0 5.7 convolution_convert_fusion.1
  274.9 11.2 %collective-permute-done.16 = bf16[256,1024]{1,0:T(8,128)(2,1)S(1)} collective-permute-done((bf16[256,1024]{1,0:T(8,128)(2,1)}, bf16[256,1024]{1,0:T(8,128)(2,1)S(1)}, u32[]{:S(2)}, u32[]{:S(2)}) %collective-permute-start.16) | collective-permute-done | bytes 524320 | tf_op jit(solution)/shard_map/ppermute | solution.py:64
  286.1 2.5 multiply_reduce_fusion.1
  288.6 3.7 multiply_add_fusion
  293.3 10.4 %fusion.28 = bf16[8,64,1280]{2,1,0:T(8,128)(2,1)} fusion(bf16[256,8,2,64]{0,3,2,1:T(8,128)(2,1)S(1)} %bitcast.165, f32[8,1280,256,2]{2,1,3,0:T(8,128)} %get-tuple-element.74, f32[8,2,256]{2,1,0:T(2,128)} %log.7, pred[256,1280]{0,1:T(8,128)(4,1)S(1)} %compare_and_fusion), kind=kOutput, calls=%fused_computation.38 | convolution fusion | flops 687472640 | bytes 23150592 | tf_op jit(solution)/shard_map/grqk,qgrd->kgd/dot_general | solution.py:293
  306.7 13.4 %fusion.1 = bf16[8,2,256,1280]{2,3,1,0:T(8,128)(2,1)} fusion(f32[8,1280,256,2]{2,1,3,0:T(8,128)} %get-tuple-element.74, bf16[1280,8,64,1]{0,2,3,1:T(8,128)(2,1)} %bitcast.155, bf16[256,8,2,64]{0,3,2,1:T(8,128)(2,1)} %bitcast.166, f32[8,2,256]{2,1,0:T(2,128)S(1)} %bitcast.179, f32[8,2,256]{2,1,0:T(2,128)S(1)} %copy-done.45, pred[256,1280]{0,1:T(8,128)(4,1)} %copy-done.25), kind=kOutput, calls=%fused_computation.2 | convolution fusion | flops 697303040 | bytes 33652736 | tf_op jit(solution)/shard_map/qgrd,kgd->grqk/dot_general | solution.py:289
  320.1 8.4 %fusion.27 = bf16[8,64,1280]{2,1,0:T(8,128)(2,1)} fusion(bf16[8,2,256,1280]{2,3,1,0:T(8,128)(2,1)} %fusion.1, bf16[256,8,2,32]{0,3,2,1:T(8,128)(2,1)S(1)} %bitcast.174, bf16[256,8,2,32]{0,3,2,1:T(8,128)(2,1)S(1)} %bitcast.172), kind=kOutput, calls=%fused_computation.37 | convolution fusion | flops 673447936 | bytes 12320768 | tf_op jit(solution)/shard_map/grqk,qgrd->kgd/dot_general | solution.py:300
  328.5 2.5 copy.158
  330.9 2.2 pad_maximum_fusion.6
  333.2 2.1 convolution_convert_fusion.4
  336.5 2.5 copy.155
  339.9 2.0 copy.165
  341.9 6.3 %convolution_multiply_fusion.1 = f32[8,64,2,256]{3,1,2,0:T(8,128)S(1)} fusion(bf16[1280,8,64,1]{0,2,3,1:T(8,128)(2,1)} %bitcast.154, bf16[8,2,256,1280]{2,3,1,0:T(8,128)(2,1)} %fusion.1), kind=kOutput, calls=%fused_computation.53 | convolution fusion | flops 671350784 | bytes 12845056 | tf_op jit(solution)/shard_map/grqk,kgd->qgrd/dot_general | solution.py:304
  348.3 2.2 convert_add_fusion
  352.4 16.3 %collective-permute-done.20 = bf16[256,1024]{1,0:T(8,128)(2,1)S(1)} collective-permute-done((bf16[256,1024]{1,0:T(8,128)(2,1)S(1)}, bf16[256,1024]{1,0:T(8,128)(2,1)S(1)}, u32[]{:S(2)}, u32[]{:S(2)}) %collective-permute-start.20) | collective-permute-done | bytes 524320 | tf_op jit(solution)/shard_map/ppermute | solution.py:100
  373.9 3.2 multiply_reduce_fusion
  377.1 11.1 %collective-permute-done.21 = bf16[256,1024]{1,0:T(8,128)(2,1)} collective-permute-done((bf16[256,1024]{1,0:T(8,128)(2,1)}, bf16[256,1024]{1,0:T(8,128)(2,1)}, u32[]{:S(2)}, u32[]{:S(2)}) %collective-permute-start.21) | collective-permute-done | bytes 524320 | tf_op jit(solution)/shard_map/ppermute | solution.py:100
  393.7 4.3 convolution_convert_fusion.2
  398.9 3.8 fusion.51
  403.6 3.3 all-to-all-start.1
  408.2 5.9 all-to-all-done.1
  414.2 3.5 all-to-all-start.2
  420.7 52.5 %reduce-scatter.7.cloned.1.call-done = bf16[32,1024]{1,0:T(8,128)(2,1)} async-done(((bf16[1024,1024]{1,0:T(8,128)(2,1)}), bf16[32,1024]{1,0:T(8,128)(2,1)}) %reduce-scatter.7.cloned.1.call-update) | async-done | bytes 65552 | tf_op jit(solution)/shard_map/reduce_scatter | solution.py:274
  476.6 139.1 %reduce-scatter.5.cloned.1.call-done = bf16[32,2048]{1,0:T(8,128)(2,1)} async-done(((bf16[1024,2048]{1,0:T(8,128)(2,1)}), bf16[32,2048]{1,0:T(8,128)(2,1)}) %reduce-scatter.5.cloned.1.call-update) | async-done | bytes 131088 | tf_op jit(solution)/shard_map/reduce_scatter | solution.py:347
  (303 shorter events, 91.2 us)
Async XLA Ops:
  7.2 70.4 %all-gather.5.cloned.1.call-start = ((), (), s32[]{:S(2)}) async-start(), calls=%async_computation.7 | async-start | bytes 4595712 | tf_op jit(solution)/shard_map/all_gather | solution.py:146
  9.6 150.0 %all-gather.7.cloned.1.call-start = ((), (), s32[]{:S(2)}) async-start(), calls=%async_computation.8 | async-start | bytes 2162688 | tf_op jit(solution)/shard_map/all_gather | solution.py:151
  10.3 177.5 %all-gather.9.cloned.1.call-start = ((), (), s32[]{:S(2)}) async-start(), calls=%async_computation.9 | async-start | bytes 5308416 | tf_op jit(solution)/shard_map/all_gather | solution.py:162
  12.7 18.4 %copy-start.11 = (bf16[1,256,1024]{2,1,0:T(8,128)(2,1)S(1)}, bf16[1,256,1024]{2,1,0:T(8,128)(2,1)}, u32[]{:S(2)}) copy-start(bf16[1,256,1024]{2,1,0:T(8,128)(2,1)} %param.14) | copy-start | bytes 1572868
  12.8 18.6 %copy-start.55 = (bf16[64]{0:T(256)(128)(2,1)S(1)}, bf16[64]{0:T(256)(128)(2,1)}, u32[]{:S(2)}) copy-start(bf16[64]{0:T(256)(128)(2,1)} %param.22) | copy-start | bytes 388
  29.7 189.9 %all-gather.11.cloned.1.call-start = ((), (), s32[]{:S(2)}) async-start(), calls=%async_computation.10 | async-start | bytes 2654208 | tf_op jit(solution)/shard_map/all_gather | solution.py:161
  29.7 137.6 %collective-permute-start.11 = (bf16[256,1024]{1,0:T(8,128)(2,1)}, bf16[256,1024]{1,0:T(8,128)(2,1)}, u32[]{:S(2)}, u32[]{:S(2)}) collective-permute-start(bf16[256,1024]{1,0:T(8,128)(2,1)} %bitcast.28), channel_id=1, source_target_pairs={{0,8},{8,0},{16,24},{24,16},{1,9},{9,1},{17,25},{25,17},{2,10},{10... | collective-permute-start | bytes 1572872 | tf_op jit(solution)/shard_map/ppermute | solution.py:64
  30.5 91.1 %collective-permute-start.12 = (bf16[256,1024]{1,0:T(8,128)(2,1)}, bf16[256,1024]{1,0:T(8,128)(2,1)}, u32[]{:S(2)}, u32[]{:S(2)}) collective-permute-start(bf16[256,1024]{1,0:T(8,128)(2,1)} %bitcast.28), channel_id=1, source_target_pairs={{0,16},{8,24},{16,0},{24,8},{1,17},{9,25},{17,1},{25,9},{2,18},{10... | collective-permute-start | bytes 1572872 | tf_op jit(solution)/shard_map/ppermute | solution.py:64
  31.1 383.1 %reduce-scatter.9.cloned.1.call-start = ((), (), s32[]{:S(2)}) async-start(), calls=%async_computation.13 | async-start | bytes 5308416 | tf_op jit(solution)/shard_map/reduce_scatter | solution.py:255
  31.4 51.7 %copy-start.49 = (f32[256]{0:T(256)}, f32[256]{0:T(256)S(1)}, u32[]{:S(2)}) copy-start(f32[256]{0:T(256)S(1)} %add_rsqrt_fusion.3) | copy-start | bytes 3076
  31.4 52.1 %copy-start.51 = (f32[64]{0:T(128)}, f32[64]{0:T(128)S(1)}, u32[]{:S(2)}) copy-start(f32[64]{0:T(128)S(1)} %convert_element_type.187) | copy-start | bytes 772
  31.7 52.0 %copy-start.31 = (f32[256,32]{0,1:T(8,128)}, f32[256,32]{0,1:T(8,128)S(1)}, u32[]{:S(2)}) copy-start(f32[256,32]{0,1:T(8,128)S(1)} %get-tuple-element.67) | copy-start | bytes 98308
  83.1 41.8 %copy-start.8 = (f32[256,2048]{1,0:T(8,128)}, f32[256,2048]{1,0:T(8,128)S(1)}, u32[]{:S(2)}) copy-start(f32[256,2048]{1,0:T(8,128)S(1)} %fusion.20) | copy-start | bytes 6291460
  83.4 35.9 %copy-start.5 = (f32[256,512]{0,1:T(8,128)}, f32[256,512]{0,1:T(8,128)S(1)}, u32[]{:S(2)}) copy-start(f32[256,512]{0,1:T(8,128)S(1)} %copy.140) | copy-start | bytes 1572868
  83.5 35.8 %copy-start.36 = (f32[256,8]{0,1:T(8,128)}, f32[256,8]{0,1:T(8,128)S(1)}, u32[]{:S(2)}) copy-start(f32[256,8]{0,1:T(8,128)S(1)} %add_rsqrt_fusion.1) | copy-start | bytes 24580
  84.0 16.3 %collective-permute-start = (bf16[256,1024]{1,0:T(8,128)(2,1)S(1)}, bf16[256,1024]{1,0:T(8,128)(2,1)S(1)}, u32[]{:S(2)}, u32[]{:S(2)}) collective-permute-start(bf16[256,1024]{1,0:T(8,128)(2,1)S(1)} %pad_maximum_fusion.9), channel_id=1, source_target_pairs={{0,2},{1,3},{2,4},{3,5},{4,6},{5,7},{8,10},{9,11},{10,12},{11,13},... | collective-permute-start | bytes 1572872 | tf_op jit(solution)/shard_map/ppermute | solution.py:100
  100.3 24.6 %copy-start.17 = (bf16[256,1024]{1,0:T(8,128)(2,1)}, bf16[256,1024]{1,0:T(8,128)(2,1)S(1)}, u32[]{:S(2)}) copy-start(bf16[256,1024]{1,0:T(8,128)(2,1)S(1)} %collective-permute-done) | copy-start | bytes 1572868
  100.3 17.7 %collective-permute-start.1 = (bf16[256,1024]{1,0:T(8,128)(2,1)S(1)}, bf16[256,1024]{1,0:T(8,128)(2,1)S(1)}, u32[]{:S(2)}, u32[]{:S(2)}) collective-permute-start(bf16[256,1024]{1,0:T(8,128)(2,1)S(1)} %collective-permute-done), channel_id=1, source_target_pairs={{0,2},{1,3},{2,4},{3,5},{4,6},{5,7},{8,10},{9,11},{10,12},{11,13},... | collective-permute-start | bytes 1572872 | tf_op jit(solution)/shard_map/ppermute | solution.py:100
  119.3 10.1 %collective-permute-start.2 = (bf16[512,1024]{1,0:T(8,128)(2,1)}, bf16[512,1024]{1,0:T(8,128)(2,1)}, u32[]{:S(2)}, u32[]{:S(2)}) collective-permute-start(bf16[512,1024]{1,0:T(8,128)(2,1)} %maximum_select_fusion), channel_id=1, source_target_pairs={{0,1},{1,0},{2,3},{3,2},{4,5},{5,4},{6,7},{7,6},{8,9},{9,8},{10,11... | collective-permute-start | bytes 3145736 | tf_op jit(solution)/shard_map/ppermute | solution.py:103
  120.4 172.9 %copy-start.25 = (pred[256,1280]{0,1:T(8,128)(4,1)}, pred[256,1280]{0,1:T(8,128)(4,1)S(1)}, u32[]{:S(2)}) copy-start(pred[256,1280]{0,1:T(8,128)(4,1)S(1)} %compare_and_fusion) | copy-start | bytes 983044
  123.3 49.3 %collective-permute-start.13 = (bf16[128,1024]{1,0:T(8,128)(2,1)}, bf16[128,1024]{1,0:T(8,128)(2,1)}, u32[]{:S(2)}, u32[]{:S(2)}) collective-permute-start(bf16[128,1024]{1,0:T(8,128)(2,1)} %slice.257), channel_id=1, source_target_pairs={{0,8},{8,0},{16,24},{24,16},{1,9},{9,1},{17,25},{25,17},{2,10},{10... | collective-permute-start | bytes 786440 | tf_op jit(solution)/shard_map/ppermute | solution.py:64
  136.0 12.9 %copy-start.7 = (bf16[1280,512]{0,1:T(8,128)(2,1)}, bf16[1280,512]{0,1:T(8,128)(2,1)S(1)}, u32[]{:S(2)}) copy-start(bf16[1280,512]{0,1:T(8,128)(2,1)S(1)} %copy.143) | copy-start | bytes 3932164
  163.4 27.6 %collective-permute-start.3 = (bf16[256,1024]{1,0:T(8,128)(2,1)}, bf16[256,1024]{1,0:T(8,128)(2,1)S(1)}, u32[]{:S(2)}, u32[]{:S(2)}) collective-permute-start(bf16[256,1024]{1,0:T(8,128)(2,1)} %get-tuple-element.20), channel_id=1, source_target_pairs={{0,8},{8,0},{16,24},{24,16},{1,9},{9,1},{17,25},{25,17},{2,10},{10... | collective-permute-start | bytes 1572872 | tf_op jit(solution)/shard_map/ppermute | solution.py:64
  163.8 15.0 %collective-permute-start.4 = (bf16[256,1024]{1,0:T(8,128)(2,1)}, bf16[256,1024]{1,0:T(8,128)(2,1)S(1)}, u32[]{:S(2)}, u32[]{:S(2)}) collective-permute-start(bf16[256,1024]{1,0:T(8,128)(2,1)} %get-tuple-element.20), channel_id=1, source_target_pairs={{0,16},{8,24},{16,0},{24,8},{1,17},{9,25},{17,1},{25,9},{2,18},{10... | collective-permute-start | bytes 1572872 | tf_op jit(solution)/shard_map/ppermute | solution.py:64
  168.3 15.0 %collective-permute-start.14 = (bf16[128,1024]{1,0:T(8,128)(2,1)S(1)}, bf16[128,1024]{1,0:T(8,128)(2,1)S(1)}, u32[]{:S(2)}, u32[]{:S(2)}) collective-permute-start(bf16[128,1024]{1,0:T(8,128)(2,1)S(1)} %slice.258), channel_id=1, source_target_pairs={{0,16},{8,24},{16,0},{24,8},{1,17},{9,25},{17,1},{25,9},{2,18},{10... | collective-permute-start | bytes 786440 | tf_op jit(solution)/shard_map/ppermute | solution.py:64
  179.5 13.1 %collective-permute-start.5 = (bf16[128,1024]{1,0:T(8,128)(2,1)}, bf16[128,1024]{1,0:T(8,128)(2,1)}, u32[]{:S(2)}, u32[]{:S(2)}) collective-permute-start(bf16[128,1024]{1,0:T(8,128)(2,1)} %slice.246), channel_id=1, source_target_pairs={{0,8},{8,0},{16,24},{24,16},{1,9},{9,1},{17,25},{25,17},{2,10},{10... | collective-permute-start | bytes 786440 | tf_op jit(solution)/shard_map/ppermute | solution.py:64
  191.0 8.5 %collective-permute-start.6 = (bf16[128,1024]{1,0:T(8,128)(2,1)S(1)}, bf16[128,1024]{1,0:T(8,128)(2,1)S(1)}, u32[]{:S(2)}, u32[]{:S(2)}) collective-permute-start(bf16[128,1024]{1,0:T(8,128)(2,1)S(1)} %slice.247), channel_id=1, source_target_pairs={{0,16},{8,24},{16,0},{24,8},{1,17},{9,25},{17,1},{25,9},{2,18},{10... | collective-permute-start | bytes 786440 | tf_op jit(solution)/shard_map/ppermute | solution.py:64
  237.3 181.6 %reduce-scatter.11.cloned.1.call-start = ((), (), s32[]{:S(2)}) async-start(), calls=%async_computation.14 | async-start | bytes 2654208 | tf_op jit(solution)/shard_map/reduce_scatter | solution.py:252
  244.1 12.4 %collective-permute-start.7 = (bf16[128,1024]{1,0:T(8,128)(2,1)S(1)}, bf16[128,1024]{1,0:T(8,128)(2,1)S(1)}, u32[]{:S(2)}, u32[]{:S(2)}) collective-permute-start(bf16[128,1024]{1,0:T(8,128)(2,1)S(1)} %get-tuple-element.39), channel_id=1, source_target_pairs={{0,16},{8,24},{16,0},{24,8},{1,17},{9,25},{17,1},{25,9},{2,18},{10... | collective-permute-start | bytes 786440 | tf_op jit(solution)/shard_map/ppermute | solution.py:64
  245.7 10.8 %collective-permute-start.9 = (bf16[128,1024]{1,0:T(8,128)(2,1)S(1)}, bf16[128,1024]{1,0:T(8,128)(2,1)S(1)}, u32[]{:S(2)}, u32[]{:S(2)}) collective-permute-start(bf16[128,1024]{1,0:T(8,128)(2,1)S(1)} %get-tuple-element.38), channel_id=1, source_target_pairs={{0,8},{8,0},{16,24},{24,16},{1,9},{9,1},{17,25},{25,17},{2,10},{10... | collective-permute-start | bytes 786440 | tf_op jit(solution)/shard_map/ppermute | solution.py:64
  255.4 9.2 %collective-permute-start.15 = (bf16[128,1024]{1,0:T(8,128)(2,1)S(1)}, bf16[128,1024]{1,0:T(8,128)(2,1)S(1)}, u32[]{:S(2)}, u32[]{:S(2)}) collective-permute-start(bf16[128,1024]{1,0:T(8,128)(2,1)S(1)} %get-tuple-element.33), channel_id=1, source_target_pairs={{0,16},{8,24},{16,0},{24,8},{1,17},{9,25},{17,1},{25,9},{2,18},{10... | collective-permute-start | bytes 786440 | tf_op jit(solution)/shard_map/ppermute | solution.py:64
  256.0 9.2 %collective-permute-start.17 = (bf16[128,1024]{1,0:T(8,128)(2,1)S(1)}, bf16[128,1024]{1,0:T(8,128)(2,1)S(1)}, u32[]{:S(2)}, u32[]{:S(2)}) collective-permute-start(bf16[128,1024]{1,0:T(8,128)(2,1)S(1)} %get-tuple-element.32), channel_id=1, source_target_pairs={{0,8},{8,0},{16,24},{24,16},{1,9},{9,1},{17,25},{25,17},{2,10},{10... | collective-permute-start | bytes 786440 | tf_op jit(solution)/shard_map/ppermute | solution.py:64
  257.5 31.0 %collective-permute-start.8 = (bf16[256,1024]{1,0:T(8,128)(2,1)}, bf16[256,1024]{1,0:T(8,128)(2,1)}, u32[]{:S(2)}, u32[]{:S(2)}) collective-permute-start(bf16[256,1024]{1,0:T(8,128)(2,1)} %pad_maximum_fusion.11), channel_id=1, source_target_pairs={{0,8},{8,0},{16,24},{24,16},{1,9},{9,1},{17,25},{25,17},{2,10},{10... | collective-permute-start | bytes 1572872 | tf_op jit(solution)/shard_map/ppermute | solution.py:64
  259.9 28.7 %collective-permute-start.10 = (bf16[256,1024]{1,0:T(8,128)(2,1)}, bf16[256,1024]{1,0:T(8,128)(2,1)}, u32[]{:S(2)}, u32[]{:S(2)}) collective-permute-start(bf16[256,1024]{1,0:T(8,128)(2,1)} %pad_maximum_fusion.12), channel_id=1, source_target_pairs={{0,16},{8,24},{16,0},{24,8},{1,17},{9,25},{17,1},{25,9},{2,18},{10... | collective-permute-start | bytes 1572872 | tf_op jit(solution)/shard_map/ppermute | solution.py:64
  266.2 19.9 %collective-permute-start.16 = (bf16[256,1024]{1,0:T(8,128)(2,1)}, bf16[256,1024]{1,0:T(8,128)(2,1)S(1)}, u32[]{:S(2)}, u32[]{:S(2)}) collective-permute-start(bf16[256,1024]{1,0:T(8,128)(2,1)} %pad_maximum_fusion.13), channel_id=1, source_target_pairs={{0,8},{8,0},{16,24},{24,16},{1,9},{9,1},{17,25},{25,17},{2,10},{10... | collective-permute-start | bytes 1572872 | tf_op jit(solution)/shard_map/ppermute | solution.py:64
  267.5 18.5 %collective-permute-start.18 = (bf16[256,1024]{1,0:T(8,128)(2,1)}, bf16[256,1024]{1,0:T(8,128)(2,1)S(1)}, u32[]{:S(2)}, u32[]{:S(2)}) collective-permute-start(bf16[256,1024]{1,0:T(8,128)(2,1)} %pad_maximum_fusion.14), channel_id=1, source_target_pairs={{0,16},{8,24},{16,0},{24,8},{1,17},{9,25},{17,1},{25,9},{2,18},{10... | collective-permute-start | bytes 1572872 | tf_op jit(solution)/shard_map/ppermute | solution.py:64
  274.8 198.4 %reduce-scatter.7.cloned.1.call-start = ((), (), s32[]{:S(2)}) async-start(), calls=%async_computation.12 | async-start | bytes 2162688 | tf_op jit(solution)/shard_map/reduce_scatter | solution.py:274
  274.9 13.7 %copy-start.39 = (f32[1024]{0:T(1024)S(1)}, f32[1024]{0:T(1024)}, u32[]{:S(2)}) copy-start(f32[1024]{0:T(1024)} %get-tuple-element.17) | copy-start | bytes 12292
  274.9 13.7 %copy-start.43 = (f32[256]{0:T(256)S(1)}, f32[256]{0:T(256)}, u32[]{:S(2)}) copy-start(f32[256]{0:T(256)} %copy-done.42) | copy-start | bytes 3076
  306.7 13.4 %copy-start.27 = (bf16[256,16,32]{0,2,1:T(8,128)(2,1)S(1)}, bf16[256,16,32]{0,2,1:T(8,128)(2,1)}, u32[]{:S(2)}) copy-start(bf16[256,16,32]{0,2,1:T(8,128)(2,1)} %copy-done.26) | copy-start | bytes 786436
  306.7 13.4 %copy-start.29 = (bf16[256,16,32]{0,2,1:T(8,128)(2,1)S(1)}, bf16[256,16,32]{0,2,1:T(8,128)(2,1)}, u32[]{:S(2)}) copy-start(bf16[256,16,32]{0,2,1:T(8,128)(2,1)} %get-tuple-element.47) | copy-start | bytes 786436
  333.2 15.1 %collective-permute-start.19 = (bf16[512,1024]{1,0:T(8,128)(2,1)}, bf16[512,1024]{1,0:T(8,128)(2,1)}, u32[]{:S(2)}, u32[]{:S(2)}) collective-permute-start(bf16[512,1024]{1,0:T(8,128)(2,1)} %pad_maximum_fusion.6), channel_id=1, source_target_pairs={{0,1},{1,0},{2,3},{3,2},{4,5},{5,4},{6,7},{7,6},{8,9},{9,8},{10,11... | collective-permute-start | bytes 3145736 | tf_op jit(solution)/shard_map/ppermute | solution.py:103
  335.3 280.5 %reduce-scatter.5.cloned.1.call-start = ((), (), s32[]{:S(2)}) async-start(), calls=%async_computation.11 | async-start | bytes 4325376 | tf_op jit(solution)/shard_map/reduce_scatter | solution.py:347
  350.6 18.1 %copy-start.1 = (f32[768,1024]{1,0:T(8,128)}, f32[768,1024]{1,0:T(8,128)S(1)}, u32[]{:S(2)}) copy-start(f32[768,1024]{1,0:T(8,128)S(1)} %convert_add_fusion) | copy-start | bytes 9437188
  350.7 18.0 %collective-permute-start.20 = (bf16[256,1024]{1,0:T(8,128)(2,1)S(1)}, bf16[256,1024]{1,0:T(8,128)(2,1)S(1)}, u32[]{:S(2)}, u32[]{:S(2)}) collective-permute-start(bf16[256,1024]{1,0:T(8,128)(2,1)S(1)} %slice.346), channel_id=1, source_target_pairs={{2,0},{3,1},{4,2},{5,3},{6,4},{7,5},{10,8},{11,9},{12,10},{13,11},... | collective-permute-start | bytes 1572872 | tf_op jit(solution)/shard_map/ppermute | solution.py:100
  369.7 18.5 %collective-permute-start.21 = (bf16[256,1024]{1,0:T(8,128)(2,1)}, bf16[256,1024]{1,0:T(8,128)(2,1)}, u32[]{:S(2)}, u32[]{:S(2)}) collective-permute-start(bf16[256,1024]{1,0:T(8,128)(2,1)} %fusion.52), channel_id=1, source_target_pairs={{2,0},{3,1},{4,2},{5,3},{6,4},{7,5},{10,8},{11,9},{12,10},{13,11},... | collective-permute-start | bytes 1572872 | tf_op jit(solution)/shard_map/ppermute | solution.py:100
  403.6 10.6 %all-to-all-start.1 = ((f32[32,1,192]{2,1,0:T(1,128)}), f32[32,1,192]{2,1,0:T(1,128)S(1)}, u32[]{:S(2)}, u32[]{:S(2)}) async-start(f32[32,1,192]{2,1,0:T(1,128)} %all_to_all.13), calls=%async_computation.3 | async-start | bytes 65536 | tf_op jit(solution)/shard_map/all_to_all | solution.py:366
  414.2 60.5 %all-to-all-start.2 = ((bf16[4,32,2304]{2,1,0:T(8,128)(2,1)}), bf16[4,32,2304]{2,1,0:T(8,128)(2,1)S(1)}, u32[]{:S(2)}, u32[]{:S(2)}) async-start(bf16[4,32,2304]{2,1,0:T(8,128)(2,1)} %reduce-scatter.9.cloned.1.call-done), calls=%async_computation.5 | async-start | bytes 1179648 | tf_op jit(solution)/shard_map/all_to_all | solution.py:263
  (46 other events, 218.8 us)
Sparse Core Ops, SparseCore 0:
  11.4 66.1 all-gather.4
  80.6 54.9 all-gather.6
  137.8 50.0 all-gather.8
  189.4 30.1 all-gather.10
  237.4 54.1 reduce-scatter.8
  293.8 35.5 reduce-scatter.10
  335.4 137.7 reduce-scatter.6
  475.5 140.2 reduce-scatter.4

commit v2 on v1

--- a/solution.py
+++ b/solution.py
@@ -101,6 +101,45 @@
 
     def swap_core(value):
         return lax.ppermute(value, "seq", [(i, i ^ 1) for i in range(seq_shards)])
+
+    def turn_seq(value, step):
+        return lax.ppermute(
+            value, "seq", [(i, (i + step) % seq_shards) for i in range(seq_shards)]
+        )
+
+    pairs = seq_shards // 2
+    in_slots = dp_count == 4
+
+    def slot_matrix(width):
+        rows = width // (dp_count * seq_shards)
+        slot_row = jnp.arange(width, dtype=jnp.int32)
+        inner = slot_row % rows
+        slot = slot_row // rows
+        chip = (lax.axis_index("seq") // 2 + slot % pairs) % pairs
+        peer = lax.axis_index("dp") ^ (slot // pairs % dp_count)
+        core = (lax.axis_index("seq") % 2) ^ (slot // (pairs * dp_count))
+        source = ((peer * seq_shards) + chip * 2 + core) * rows + inner
+        return (slot_row[:, None] == source[None, :]).astype(BF16)
+
+    def gather_rows(value):
+        if not in_slots:
+            return lax.all_gather(value, BOTH, axis=0, tiled=True)
+        line = [value] + [turn_seq(value, -2 * k) for k in range(1, pairs)]
+        plane = gather_dp(jnp.concatenate(line, axis=0), dp_count)
+        return jnp.concatenate([plane, swap_core(plane)], axis=0)
+
+    def scatter_rows(parts):
+        if not in_slots:
+            return lax.psum_scatter(parts, BOTH, scatter_dimension=0, tiled=True).astype(F32)
+        half = parts.shape[0] // 2
+        chip = (parts[:half].astype(F32) + swap_core(parts[half:]).astype(F32)).astype(BF16)
+        line = scatter_sum_dp(chip, dp_count)
+        rows = line.shape[0] // pairs
+        total = line[:rows]
+        for k in range(1, pairs):
+            piece = line[k * rows : (k + 1) * rows].astype(BF16)
+            total = total + turn_seq(piece, 2 * k).astype(F32)
+        return total
 
     def body(
         tokens,
@@ -142,13 +181,29 @@
 
         gains = jnp.stack([attn_gain, ffn_gain], axis=1)
         gains = jnp.pad(gains, ((0, 0), (0, 126)))
-        pack = jnp.concatenate([w_query, w_key, w_value, gains], axis=1)
-        pack = lax.all_gather(pack, BOTH, axis=0, tiled=True)
-        qkv_all = pack[:, : query_width + 2 * key_width]
-        gain_cols = pack[:, query_width + 2 * key_width :].astype(F32)
+        pack = gather_rows(jnp.concatenate([w_key, w_value, gains], axis=1))
+        kv_all = pack[:, : 2 * key_width]
+        gain_cols = pack[:, 2 * key_width :].astype(F32)
+        query_all = gather_rows(w_query)
+        out_all = gather_rows(w_out)
+        if in_slots:
+            slots = slot_matrix(model_width)
+            out_slots = slots if query_width == model_width else slot_matrix(query_width)
+            to_slots = lambda value, matrix: dot(value, matrix).astype(BF16)
+            from_slots = lambda value, matrix: dot_nt(value, matrix).astype(BF16)
+            whole_from_slots = lambda value: lax.dot_general(
+                value,
+                slots.astype(F32),
+                (((1,), (1,)), ((), ())),
+                precision=lax.Precision.HIGHEST,
+                preferred_element_type=F32,
+            )
+        else:
+            slots = out_slots = None
+            to_slots = from_slots = lambda value, matrix: value
+            whole_from_slots = lambda value: value
         attn_gain_all = gain_cols[:, 0]
-        ffn_gain_all = gain_cols[:, 1]
-        out_all = lax.all_gather(w_out, BOTH, axis=0, tiled=True)
+        ffn_gain_all = whole_from_slots(gain_cols[:, 1][None])[0]
 
         gate_up = jnp.concatenate(
             [
@@ -166,17 +221,16 @@
 
         stream = tokens.astype(F32)
         scale_one = rms_scale(stream)
-        normed_one = (stream * scale_one * attn_gain_all).astype(BF16)
+        stream_slots = to_slots(tokens, slots).astype(F32)
+        normed_one = (stream_slots * scale_one * attn_gain_all).astype(BF16)
         positions = first_row + jnp.arange(local_len, dtype=jnp.int32)
         cosine_table, sine_table = rope_tables(positions, head_width)
         cosine_table = cosine_table[:, None, :]
         sine_table = sine_table[:, None, :]
-        qkv = dot(normed_one, qkv_all)
-        query_pre = qkv[:, :query_width].reshape(local_len, query_heads, head_width)
-        key_pre = qkv[:, query_width : query_width + key_width].reshape(
-            local_len, key_heads, head_width
-        )
-        value_send = qkv[:, query_width + key_width :].astype(BF16)
+        query_pre = dot(normed_one, query_all).reshape(local_len, query_heads, head_width)
+        key_value = dot(normed_one, kv_all)
+        key_pre = key_value[:, :key_width].reshape(local_len, key_heads, head_width)
+        value_send = key_value[:, key_width:].astype(BF16)
         query_scale = rms_scale(query_pre)
         key_scale = rms_scale(key_pre)
         query_gain_f = query_gain.astype(F32)
@@ -228,7 +282,8 @@
         attended = (summed / jnp.moveaxis(denominator, 2, 0)[..., None]).astype(BF16)
         log_total = jnp.log(denominator)
         attended_flat = attended.reshape(local_len, query_width)
-        middle = stream + dot(attended_flat, out_all)
+        attended_slots = to_slots(attended_flat, out_slots)
+        middle = stream + dot(attended_slots, out_all)
 
         scale_two = rms_scale(middle)
         normed_two = (middle * scale_two * ffn_gain_all).astype(BF16)
@@ -271,17 +326,10 @@
         grad_middle = grad_output + grad_mid_norm
 
         grad_middle_bf = grad_middle.astype(BF16)
-        grad_out_w = lax.psum_scatter(
-            dot_tn(attended_flat, grad_middle_bf).astype(BF16),
-            BOTH,
-            scatter_dimension=0,
-            tiled=True,
-        )
-        grad_attended = (
-            dot_nt(grad_middle_bf, out_all)
-            .astype(BF16)
-            .reshape(local_len, key_heads, group_size, head_width)
-        )
+        grad_out_w = scatter_rows(dot_tn(attended_slots, grad_middle_bf).astype(BF16))
+        grad_attended = from_slots(
+            dot_nt(grad_middle_bf, out_all).astype(BF16), out_slots
+        ).reshape(local_len, key_heads, group_size, head_width)
         delta_rows = jnp.moveaxis(
             jnp.sum(grad_attended.astype(F32) * attended.astype(F32), axis=-1), 0, 2
         )
@@ -336,21 +384,18 @@
             key_sum.reshape(local_len, key_heads, head_width), cosine_table, sine_table
         )
         grad_kpre, grad_kgain = norm_back(grad_knorm, key_pre, key_scale, key_gain_f, (0, 1))
-        grad_qkv = jnp.concatenate(
-            [
-                grad_qpre.reshape(local_len, query_width).astype(BF16),
-                grad_kpre.reshape(local_len, key_width).astype(BF16),
-                value_grad_bf,
-            ],
-            axis=1,
-        )
-        grad_qkv_w = lax.psum_scatter(
-            dot_tn(normed_one, grad_qkv).astype(BF16), BOTH, scatter_dimension=0, tiled=True
-        ).astype(F32)
-        grad_normed_one = dot_nt(grad_qkv, qkv_all)
+        query_bf = grad_qpre.reshape(local_len, query_width).astype(BF16)
+        grad_query_w = scatter_rows(dot_tn(normed_one, query_bf).astype(BF16))
+        kv_bf = jnp.concatenate(
+            [grad_kpre.reshape(local_len, key_width).astype(BF16), value_grad_bf], axis=1
+        )
+        grad_kv_w = scatter_rows(dot_tn(normed_one, kv_bf).astype(BF16))
+        grad_normed_one = dot_nt(query_bf, query_all) + dot_nt(kv_bf, kv_all)
         grad_stream, grad_attn_gain = norm_back(
-            grad_normed_one, stream, scale_one, attn_gain_all, (0,)
-        )
+            grad_normed_one, stream_slots, scale_one, attn_gain_all, (0,)
+        )
+        grad_stream = whole_from_slots(grad_stream)
+        grad_attn_gain = whole_from_slots(grad_attn_gain[None])[0]
         grad_tokens = grad_middle + grad_stream
 
         devices = dp_count * seq_shards
@@ -367,10 +412,10 @@
         return (
             output[None],
             grad_tokens[None],
-            grad_qkv_w[:, :query_width],
-            grad_qkv_w[:, query_width : query_width + key_width],
-            grad_qkv_w[:, query_width + key_width :],
-            grad_out_w.astype(F32),
+            grad_query_w,
+            grad_kv_w[:, :key_width],
+            grad_kv_w[:, key_width:],
+            grad_out_w,
             small[:rows],
             small[2 * rows : 2 * rows + head_width],
             small[2 * rows + head_width :],

time: 632 us -> 520 us (0.82)
  waiting for transfers between devices: 340 us -> 102 us
  starting transfers between devices: 35.6 us -> 101 us
  local copies, waits for them, and re-layouts: 55.8 us -> 94.7 us
  matrix products: 121 us -> 142 us
    reduce_scatter x2 -> x0, waiting for transfers between devices: 192 us -> none  [the longest x1 139 us: body(): lax.psum_scatter(dot_tn(normed_one, grad_qkv).astype(BF16), BOTH, scatter...]
    all_gather x2 -> x0, waiting for transfers between devices: 45.9 us -> none  [the longest x1 45.9 us: body(): pack = lax.all_gather(pack, BOTH, axis=0, tiled=True)]
    ppermute x4, waiting for transfers between devices: 53.2 us -> 9.58 us  [shift_seq(): return lax.ppermute(value, 'seq', pairs)]
    ppermute x0 -> x18, starting transfers between devices: none -> 34.8 us  [turn_seq(): lax.ppermute(value, 'seq', [(i, (i + step) % seq_shards) for i in range(s...]
    ppermute x0 -> x18, waiting for transfers between devices: none -> 31.3 us  [turn_seq(): lax.ppermute(value, 'seq', [(i, (i + step) % seq_shards) for i in range(s...]
    ppermute x16 -> x40, waiting for transfers between devices: 27.7 us -> 56.5 us  [swap_dp(): return lax.ppermute(value, 'dp', [(i, i ^ bits) for i in range(count)])]
    unnamed x137 -> x193, local copies, waits for them, and re-layouts: 11.4 us -> 37.9 us
    ppermute x16 -> x40, starting transfers between devices: 17.8 us -> 43.5 us  [swap_dp(): return lax.ppermute(value, 'dp', [(i, i ^ bits) for i in range(count)])]
  transfers between devices with their start and end apart: 32 -> 76, of which waited for: 16 -> 28; matrix products, arithmetic and copies ran while one was open for 31% -> 47% of each run, Pallas kernels for 0% -> 0%
where the time goes in v2:
time: 520 us; the launch traced here: 515 us
  matrix products  142 us (27%)
  waiting for transfers between devices  102 us (20%)
  starting transfers between devices  101 us (19%)
  local copies, waits for them, and re-layouts  94.7 us (18%)
  other arithmetic  44.6 us (9%)
  between operations  15.7 us (3%)
  blocking collectives  14.5 us (3%)
    ppermute x40, waiting for transfers between devices, swap_dp(): return lax.ppermute(value, 'dp', [(i, i ^ bits) for i in range(count)])  56.5 us
    ppermute x40, starting transfers between devices, swap_dp(): return lax.ppermute(value, 'dp', [(i, i ^ bits) for i in range(count)])  43.5 us
    unnamed x193, local copies, waits for them, and re-layouts  37.9 us
    ppermute x18, starting transfers between devices, turn_seq(): lax.ppermute(value, 'seq', [(i, (i + step) % seq_shards) for i in range(s...  34.8 us
    ppermute x18, waiting for transfers between devices, turn_seq(): lax.ppermute(value, 'seq', [(i, (i + step) % seq_shards) for i in range(s...  31.3 us
    dot_general x7, matrix products, dot(): return jnp.dot(left, right, preferred_element_type=F32)  30.9 us
    dot_general x5, matrix products, dot_nt(): lax.dot_general(left, right, (((1,), (1,)), ((), ())), preferred_element_...  25.5 us
    dot_general x5, matrix products, dot_tn(): lax.dot_general(left, right, (((0,), (0,)), ((), ())), preferred_element_...  16.6 us
  transfers between devices with their start and end apart: 76, of which 28 were waited for; matrix products, arithmetic and copies ran while one was open for 47% of the time, Pallas kernels for 0%

profile of v2, /device:TPU:0, one launch (start us, length us, event | category | flops | bytes accessed | tf_op | source)
XLA Modules:
  0.0 514.5 jit_solution(15968545750167435022)
XLA Ops:
  9.7 14.5 %all_to_all.19 = bf16[4,32,2304]{2,1,0:T(8,128)(2,1)S(1)} all-to-all(bf16[4,32,2304]{2,1,0:T(8,128)(2,1)S(1)} %copy.154), channel_id=1, replica_groups=mesh['dp'=4,'seq'=8] {'dp'}, dimensions={0} | all-to-all | bytes 1179648 | tf_op jit(solution)/shard_map/all_to_all | solution.py:215
  25.6 3.7 collective-permute-start.19
  30.3 2.8 collective-permute-start.11
  46.1 3.8 collective-permute-start
  55.6 10.2 %collective-permute-done.1 = bf16[32,1152]{1,0:T(8,128)(2,1)S(1)} collective-permute-done((bf16[32,1152]{1,0:T(8,128)(2,1)S(1)}, bf16[32,1152]{1,0:T(8,128)(2,1)S(1)}, u32[]{:S(2)}, u32[]{:S(2)}) %collective-permute-start.1) | collective-permute-done | bytes 73760 | tf_op jit(solution)/shard_map/ppermute | solution.py:106
  69.3 5.4 %collective-permute-done.4 = bf16[128,1152]{1,0:T(8,128)(2,1)S(1)} collective-permute-done((bf16[128,1152]{1,0:T(8,128)(2,1)S(1)}, bf16[128,1152]{1,0:T(8,128)(2,1)S(1)}, u32[]{:S(2)}, u32[]{:S(2)}) %collective-permute-start.4) | collective-permute-done | bytes 294944 | tf_op jit(solution)/shard_map/ppermute | solution.py:64
  82.6 3.0 collective-permute-done.6
  104.5 8.9 %collective-permute-done.25 = bf16[64,1024]{1,0:T(8,128)(2,1)S(1)} collective-permute-done((bf16[64,1024]{1,0:T(8,128)(2,1)S(1)}, bf16[64,1024]{1,0:T(8,128)(2,1)S(1)}, u32[]{:S(2)}, u32[]{:S(2)}) %collective-permute-start.25) | collective-permute-done | bytes 131104 | tf_op jit(solution)/shard_map/ppermute | solution.py:64
  126.0 5.7 %collective-permute-start.8 = (bf16[256,1024]{1,0:T(8,128)(2,1)S(1)}, bf16[256,1024]{1,0:T(8,128)(2,1)}, u32[]{:S(2)}, u32[]{:S(2)}) collective-permute-start(bf16[256,1024]{1,0:T(8,128)(2,1)S(1)} %pad_maximum_fusion.8), channel_id=1, source_target_pairs={{0,2},{1,3},{2,4},{3,5},{4,6},{5,7},{8,10},{9,11},{10,12},{11,13},... | collective-permute-start | bytes 1572872 | tf_op jit(solution)/shard_map/ppermute | solution.py:100
  139.3 3.5 collective-permute-done.8
  142.8 5.3 %collective-permute-start.9 = (bf16[256,1024]{1,0:T(8,128)(2,1)}, bf16[256,1024]{1,0:T(8,128)(2,1)}, u32[]{:S(2)}, u32[]{:S(2)}) collective-permute-start(bf16[256,1024]{1,0:T(8,128)(2,1)} %collective-permute-done.8), channel_id=1, source_target_pairs={{0,2},{1,3},{2,4},{3,5},{4,6},{5,7},{8,10},{9,11},{10,12},{11,13},... | collective-permute-start | bytes 1572872 | tf_op jit(solution)/shard_map/ppermute | solution.py:100
  153.2 5.4 %collective-permute-done.9 = bf16[256,1024]{1,0:T(8,128)(2,1)} collective-permute-done((bf16[256,1024]{1,0:T(8,128)(2,1)}, bf16[256,1024]{1,0:T(8,128)(2,1)}, u32[]{:S(2)}, u32[]{:S(2)}) %collective-permute-start.9) | collective-permute-done | bytes 524320 | tf_op jit(solution)/shard_map/ppermute | solution.py:100
  164.2 3.3 pad_maximum_fusion.3
  170.9 2.9 copy.150
  173.8 10.8 %fusion.5 = (f32[8,2,256]{2,1,0:T(2,128)S(1)}, f32[8,1280,256,2]{2,1,3,0:T(8,128)}) fusion(pred[256,1280]{0,1:T(8,128)(4,1)S(1)} %compare_and_fusion, bf16[1280,8,64,1]{0,2,3,1:T(8,128)(2,1)S(1)} %bitcast.165, bf16[256,8,2,32]{0,3,2,1:T(8,128)(2,1)} %bitcast.186, bf16[256,8,2,32]{0,3,2,1:T(8,128)(2,1)S(1)} %bitcast.184), kind=kOutput, calls=%fused_computation.9 | convolution fusion | flops 687861760 | bytes 23150592 | tf_op jit(solution)/shard_map/qgrd,kgd->grqk/dot_general | solution.py:274
  184.6 10.5 %divide_convert_fusion = bf16[256,8,2,64]{0,3,2,1:T(8,128)(2,1)S(1)} fusion(bf16[1280,8,64,1]{0,2,3,1:T(8,128)(2,1)S(1)} %bitcast.167, f32[8,1280,256,2]{2,1,3,0:T(8,128)} %get-tuple-element.164, pred[256,1280]{0,1:T(8,128)(4,1)} %copy-done.35, f32[256,8,2]{0,2,1:T(2,128)S(1)} %bitcast.191), kind=kOutput, calls=%fused_computation.110 | convolution fusion | flops 682098688 | bytes 23150592 | tf_op jit(solution)/shard_map/grqk,kgd->qgrd/dot_general | solution.py:279
  207.3 7.5 %collective-permute-done.28 = bf16[256,1024]{1,0:T(8,128)(2,1)S(1)} collective-permute-done((bf16[256,1024]{1,0:T(8,128)(2,1)S(1)}, bf16[256,1024]{1,0:T(8,128)(2,1)S(1)}, u32[]{:S(2)}, u32[]{:S(2)}) %collective-permute-start.28) | collective-permute-done | bytes 524320 | tf_op jit(solution)/shard_map/ppermute | solution.py:64
  215.5 4.2 collective-permute-done.38
  223.1 4.3 collective-permute-done.30
  228.1 2.9 copy.156
  233.1 19.2 %fusion.147 = f32[1024,2304]{1,0:T(8,128)} fusion(bf16[1024,1024]{1,0:T(8,128)(2,1)} %constant_dynamic-update-slice_fusion.61, bf16[1024,2304]{1,0:T(8,128)(2,1)S(1)} %bitcast.171), kind=kOutput, calls=%fused_computation.356 | convolution fusion | flops 4831838208 | bytes 16252928 | tf_op jit(solution)/shard_map/dot_general | solution.py:52
  252.3 10.8 %multiply_convert_fusion.1 = (bf16[1024,1152]{1,0:T(8,128)(2,1)S(1)}, bf16[1024,1152]{1,0:T(8,128)(2,1)S(1)}, bf16[1024,1152]{1,0:T(8,128)(2,1)}) fusion(f32[1024,2304]{1,0:T(8,128)} %fusion.147, bf16[1024,1024]{1,0:T(8,128)(2,1)} %copy-done.48, bf16[1152,1024]{1,0:T(8,128)(2,1)} %all-gather.5.cloned.1.call-done), kind=kOutput, calls=%fused_computation.22 | convolution fusion | flops 2433613824 | bytes 20971520 | tf_op jit(solution)/shard_map/dot_general | solution.py:60
  263.1 9.2 %convolution_convert_fusion = bf16[1024,2304]{1,0:T(8,128)(2,1)} fusion(bf16[1024,1024]{1,0:T(8,128)(2,1)} %constant_dynamic-update-slice_fusion.61, bf16[1024,1152]{1,0:T(8,128)(2,1)S(1)} %get-tuple-element.26, bf16[1024,1152]{1,0:T(8,128)(2,1)S(1)} %get-tuple-element.25), kind=kOutput, calls=%fused_computation.19 | convolution fusion | flops 4843634688 | bytes 11534336 | tf_op jit(solution)/shard_map/dot_general | solution.py:56
  272.4 6.3 %fusion.43 = bf16[1024,1024]{1,0:T(8,128)(2,1)} fusion(bf16[1024,2304]{1,0:T(8,128)(2,1)S(1)} %bitcast.172, bf16[1024,1152]{1,0:T(8,128)(2,1)S(1)} %get-tuple-element.26, bf16[1024,1152]{1,0:T(8,128)(2,1)S(1)} %get-tuple-element.25), kind=kOutput, calls=%fused_computation.57 | convolution fusion | flops 4842323968 | bytes 11534336 | tf_op jit(solution)/shard_map/dot_general | solution.py:60
  281.7 5.3 %convolution_convert_fusion.2 = bf16[1024,1024]{1,0:T(8,128)(2,1)S(1)} fusion(bf16[1024,1152]{1,0:T(8,128)(2,1)} %get-tuple-element.27, bf16[1152,1024]{1,0:T(8,128)(2,1)} %all-gather.5.cloned.1.call-done), kind=kOutput, calls=%fused_computation.56 | convolution fusion | flops 2416967680 | bytes 6815744 | tf_op jit(solution)/shard_map/dot_general | solution.py:52
  294.1 3.1 collective-permute-done.33
  304.5 2.7 copy.163
  312.5 4.6 collective-permute-done.32
  317.0 3.8 multiply_add_fusion
  320.9 4.2 fusion.58
  328.5 13.4 %fusion.1 = bf16[8,2,256,1280]{2,3,1,0:T(8,128)(2,1)} fusion(f32[8,1280,256,2]{2,1,3,0:T(8,128)} %get-tuple-element.164, bf16[1280,8,64,1]{0,2,3,1:T(8,128)(2,1)S(1)} %bitcast.168, bf16[256,8,2,64]{0,3,2,1:T(8,128)(2,1)} %bitcast.177, f32[8,2,256]{2,1,0:T(2,128)S(1)} %bitcast.195, f32[8,2,256]{2,1,0:T(2,128)S(1)} %log.7, pred[256,1280]{0,1:T(8,128)(4,1)} %copy-done.35), kind=kOutput, calls=%fused_computation.2 | convolution fusion | flops 697303040 | bytes 33652736 | tf_op jit(solution)/shard_map/qgrd,kgd->grqk/dot_general | solution.py:337
  342.0 5.9 %convolution_multiply_fusion.1 = f32[8,64,2,256]{3,1,2,0:T(8,128)S(1)} fusion(bf16[1280,8,64,1]{0,2,3,1:T(8,128)(2,1)S(1)} %bitcast.166, bf16[8,2,256,1280]{2,3,1,0:T(8,128)(2,1)} %fusion.1), kind=kOutput, calls=%fused_computation.70 | convolution fusion | flops 671350784 | bytes 12845056 | tf_op jit(solution)/shard_map/grqk,kgd->qgrd/dot_general | solution.py:352
  351.6 10.0 %fusion.31 = bf16[8,64,1280]{2,1,0:T(8,128)(2,1)} fusion(bf16[256,8,2,64]{0,3,2,1:T(8,128)(2,1)S(1)} %bitcast.178, f32[8,1280,256,2]{2,1,3,0:T(8,128)} %get-tuple-element.164, f32[8,2,256]{2,1,0:T(2,128)S(1)} %log.7, pred[256,1280]{0,1:T(8,128)(4,1)S(1)} %copy-done.36), kind=kOutput, calls=%fused_computation.41 | convolution fusion | flops 687472640 | bytes 23150592 | tf_op jit(solution)/shard_map/grqk,qgrd->kgd/dot_general | solution.py:341
  363.2 8.3 %fusion.30 = bf16[8,64,1280]{2,1,0:T(8,128)(2,1)} fusion(bf16[8,2,256,1280]{2,3,1,0:T(8,128)(2,1)} %fusion.1, bf16[256,8,2,32]{0,3,2,1:T(8,128)(2,1)S(1)} %bitcast.187, bf16[256,8,2,32]{0,3,2,1:T(8,128)(2,1)S(1)} %bitcast.185), kind=kOutput, calls=%fused_computation.40 | convolution fusion | flops 673447936 | bytes 12320768 | tf_op jit(solution)/shard_map/grqk,qgrd->kgd/dot_general | solution.py:348
  381.1 4.1 convolution_convert_fusion.1
  405.6 3.2 collective-permute-done.64
  408.9 3.1 collective-permute-start.67
  414.2 3.0 collective-permute-start.69
  419.5 4.1 collective-permute-start.51
  428.7 16.6 %collective-permute-done.51 = bf16[32,1024]{1,0:T(8,128)(2,1)S(1)} collective-permute-done((bf16[32,1024]{1,0:T(8,128)(2,1)S(1)}, bf16[32,1024]{1,0:T(8,128)(2,1)S(1)}, u32[]{:S(2)}, u32[]{:S(2)}) %collective-permute-start.51) | collective-permute-done | bytes 65568 | tf_op jit(solution)/shard_map/ppermute | solution.py:106
  445.3 3.5 collective-permute-done.52
  458.0 3.4 multiply_reduce_fusion.2
  461.5 4.2 fusion.23
  466.4 4.3 all-to-all-start.1
  475.9 2.6 collective-permute-done.55
  482.0 4.9 fusion.50
  495.4 3.5 all-to-all-start.2
  501.5 4.4 all-to-all-done.2
  (491 shorter events, 208.6 us)
Async XLA Ops:
  7.2 220.9 %all-gather.3.cloned.1.call-start = ((), (), s32[]{:S(2)}) async-start(), calls=%async_computation.5 | async-start | bytes 5308416 | tf_op jit(solution)/shard_map/all_gather | solution.py:217
  25.6 226.8 %all-gather.5.cloned.1.call-start = ((), (), s32[]{:S(2)}) async-start(), calls=%async_computation.6 | async-start | bytes 2654208 | tf_op jit(solution)/shard_map/all_gather | solution.py:216
  25.6 19.8 %collective-permute-start.19 = (bf16[32,1024]{1,0:T(8,128)(2,1)S(1)}, bf16[32,1024]{1,0:T(8,128)(2,1)S(1)}, u32[]{:S(2)}, u32[]{:S(2)}) collective-permute-start(bf16[32,1024]{1,0:T(8,128)(2,1)S(1)} %copy-done.54), channel_id=1, source_target_pairs={{0,6},{1,7},{2,0},{3,1},{4,2},{5,3},{6,4},{7,5},{8,14},{9,15},{10,... | collective-permute-start | bytes 196616 | tf_op jit(solution)/shard_map/ppermute | solution.py:106
  29.3 16.9 %collective-permute-start.20 = (bf16[32,1024]{1,0:T(8,128)(2,1)S(1)}, bf16[32,1024]{1,0:T(8,128)(2,1)S(1)}, u32[]{:S(2)}, u32[]{:S(2)}) collective-permute-start(bf16[32,1024]{1,0:T(8,128)(2,1)S(1)} %copy-done.54), channel_id=1, source_target_pairs={{0,4},{1,5},{2,6},{3,7},{4,0},{5,1},{6,2},{7,3},{8,12},{9,13},{10,... | collective-permute-start | bytes 196616 | tf_op jit(solution)/shard_map/ppermute | solution.py:106
  29.3 21.4 %collective-permute-start.21 = (bf16[32,1024]{1,0:T(8,128)(2,1)S(1)}, bf16[32,1024]{1,0:T(8,128)(2,1)S(1)}, u32[]{:S(2)}, u32[]{:S(2)}) collective-permute-start(bf16[32,1024]{1,0:T(8,128)(2,1)S(1)} %copy-done.54), channel_id=1, source_target_pairs={{0,2},{1,3},{2,4},{3,5},{4,6},{5,7},{6,0},{7,1},{8,10},{9,11},{10,... | collective-permute-start | bytes 196616 | tf_op jit(solution)/shard_map/ppermute | solution.py:106
  30.3 21.1 %collective-permute-start.11 = (bf16[32,1024]{1,0:T(8,128)(2,1)}, bf16[32,1024]{1,0:T(8,128)(2,1)S(1)}, u32[]{:S(2)}, u32[]{:S(2)}) collective-permute-start(bf16[32,1024]{1,0:T(8,128)(2,1)} %param.16), channel_id=1, source_target_pairs={{0,6},{1,7},{2,0},{3,1},{4,2},{5,3},{6,4},{7,5},{8,14},{9,15},{10,... | collective-permute-start | bytes 196616 | tf_op jit(solution)/shard_map/ppermute | solution.py:106
  33.1 19.5 %collective-permute-start.12 = (bf16[32,1024]{1,0:T(8,128)(2,1)}, bf16[32,1024]{1,0:T(8,128)(2,1)S(1)}, u32[]{:S(2)}, u32[]{:S(2)}) collective-permute-start(bf16[32,1024]{1,0:T(8,128)(2,1)} %param.16), channel_id=1, source_target_pairs={{0,4},{1,5},{2,6},{3,7},{4,0},{5,1},{6,2},{7,3},{8,12},{9,13},{10,... | collective-permute-start | bytes 196616 | tf_op jit(solution)/shard_map/ppermute | solution.py:106
  34.2 461.2 %reduce-scatter.3.cloned.1.call-start = ((), (), s32[]{:S(2)}) async-start(), calls=%async_computation.7 | async-start | bytes 5308416 | tf_op jit(solution)/shard_map/reduce_scatter | solution.py:310
  45.4 40.8 %collective-permute-start.13 = (bf16[32,1024]{1,0:T(8,128)(2,1)}, bf16[32,1024]{1,0:T(8,128)(2,1)S(1)}, u32[]{:S(2)}, u32[]{:S(2)}) collective-permute-start(bf16[32,1024]{1,0:T(8,128)(2,1)} %param.16), channel_id=1, source_target_pairs={{0,2},{1,3},{2,4},{3,5},{4,6},{5,7},{6,0},{7,1},{8,10},{9,11},{10,... | collective-permute-start | bytes 196616 | tf_op jit(solution)/shard_map/ppermute | solution.py:106
  50.6 15.2 %collective-permute-start.1 = (bf16[32,1152]{1,0:T(8,128)(2,1)S(1)}, bf16[32,1152]{1,0:T(8,128)(2,1)S(1)}, u32[]{:S(2)}, u32[]{:S(2)}) collective-permute-start(bf16[32,1152]{1,0:T(8,128)(2,1)S(1)} %get-tuple-element.123), channel_id=1, source_target_pairs={{0,4},{1,5},{2,6},{3,7},{4,0},{5,1},{6,2},{7,3},{8,12},{9,13},{10,... | collective-permute-start | bytes 221192 | tf_op jit(solution)/shard_map/ppermute | solution.py:106
  51.3 14.5 %collective-permute-start.2 = (bf16[32,1152]{1,0:T(8,128)(2,1)S(1)}, bf16[32,1152]{1,0:T(8,128)(2,1)S(1)}, u32[]{:S(2)}, u32[]{:S(2)}) collective-permute-start(bf16[32,1152]{1,0:T(8,128)(2,1)S(1)} %get-tuple-element.123), channel_id=1, source_target_pairs={{0,2},{1,3},{2,4},{3,5},{4,6},{5,7},{6,0},{7,1},{8,10},{9,11},{10,... | collective-permute-start | bytes 221192 | tf_op jit(solution)/shard_map/ppermute | solution.py:106
  52.6 149.4 %collective-permute-start.35 = (bf16[256,1024]{1,0:T(8,128)(2,1)}, bf16[256,1024]{1,0:T(8,128)(2,1)}, u32[]{:S(2)}, u32[]{:S(2)}) collective-permute-start(bf16[256,1024]{1,0:T(8,128)(2,1)} %bitcast.29), channel_id=1, source_target_pairs={{0,8},{8,0},{16,24},{24,16},{1,9},{9,1},{17,25},{25,17},{2,10},{10... | collective-permute-start | bytes 1572872 | tf_op jit(solution)/shard_map/ppermute | solution.py:64
  54.6 36.2 %collective-permute-start.22 = (bf16[128,1024]{1,0:T(8,128)(2,1)}, bf16[128,1024]{1,0:T(8,128)(2,1)}, u32[]{:S(2)}, u32[]{:S(2)}) collective-permute-start(bf16[128,1024]{1,0:T(8,128)(2,1)} %get-tuple-element.126), channel_id=1, source_target_pairs={{0,8},{8,0},{16,24},{24,16},{1,9},{9,1},{17,25},{25,17},{2,10},{10... | collective-permute-start | bytes 786440 | tf_op jit(solution)/shard_map/ppermute | solution.py:64
  74.7 19.4 %collective-permute-start.23 = (bf16[128,1024]{1,0:T(8,128)(2,1)}, bf16[128,1024]{1,0:T(8,128)(2,1)}, u32[]{:S(2)}, u32[]{:S(2)}) collective-permute-start(bf16[128,1024]{1,0:T(8,128)(2,1)} %get-tuple-element.126), channel_id=1, source_target_pairs={{0,16},{8,24},{16,0},{24,8},{1,17},{9,25},{17,1},{25,9},{2,18},{10... | collective-permute-start | bytes 786440 | tf_op jit(solution)/shard_map/ppermute | solution.py:64
  86.3 32.9 %collective-permute-start.7 = (bf16[512,1152]{1,0:T(8,128)(2,1)}, bf16[512,1152]{1,0:T(8,128)(2,1)}, u32[]{:S(2)}, u32[]{:S(2)}) collective-permute-start(bf16[512,1152]{1,0:T(8,128)(2,1)} %get-tuple-element.101), channel_id=1, source_target_pairs={{0,1},{1,0},{2,3},{3,2},{4,5},{5,4},{6,7},{7,6},{8,9},{9,8},{10,11... | collective-permute-start | bytes 3538952 | tf_op jit(solution)/shard_map/ppermute | solution.py:103
  87.0 10.4 %collective-permute-start.14 = (bf16[128,1024]{1,0:T(8,128)(2,1)}, bf16[128,1024]{1,0:T(8,128)(2,1)S(1)}, u32[]{:S(2)}, u32[]{:S(2)}) collective-permute-start(bf16[128,1024]{1,0:T(8,128)(2,1)} %get-tuple-element.138), channel_id=1, source_target_pairs={{0,8},{8,0},{16,24},{24,16},{1,9},{9,1},{17,25},{25,17},{2,10},{10... | collective-permute-start | bytes 786440 | tf_op jit(solution)/shard_map/ppermute | solution.py:64
  94.1 39.7 %collective-permute-start.36 = (bf16[256,1024]{1,0:T(8,128)(2,1)}, bf16[256,1024]{1,0:T(8,128)(2,1)}, u32[]{:S(2)}, u32[]{:S(2)}) collective-permute-start(bf16[256,1024]{1,0:T(8,128)(2,1)} %bitcast.29), channel_id=1, source_target_pairs={{0,16},{8,24},{16,0},{24,8},{1,17},{9,25},{17,1},{25,9},{2,18},{10... | collective-permute-start | bytes 1572872 | tf_op jit(solution)/shard_map/ppermute | solution.py:64
  100.2 13.3 %collective-permute-start.25 = (bf16[64,1024]{1,0:T(8,128)(2,1)S(1)}, bf16[64,1024]{1,0:T(8,128)(2,1)S(1)}, u32[]{:S(2)}, u32[]{:S(2)}) collective-permute-start(bf16[64,1024]{1,0:T(8,128)(2,1)S(1)} %slice.456), channel_id=1, source_target_pairs={{0,16},{8,24},{16,0},{24,8},{1,17},{9,25},{17,1},{25,9},{2,18},{10... | collective-permute-start | bytes 393224 | tf_op jit(solution)/shard_map/ppermute | solution.py:64
  102.6 13.2 %collective-permute-start.16 = (bf16[64,1024]{1,0:T(8,128)(2,1)S(1)}, bf16[64,1024]{1,0:T(8,128)(2,1)S(1)}, u32[]{:S(2)}, u32[]{:S(2)}) collective-permute-start(bf16[64,1024]{1,0:T(8,128)(2,1)S(1)} %slice.451), channel_id=1, source_target_pairs={{0,8},{8,0},{16,24},{24,16},{1,9},{9,1},{17,25},{25,17},{2,10},{10... | collective-permute-start | bytes 393224 | tf_op jit(solution)/shard_map/ppermute | solution.py:64
  115.7 21.3 %collective-permute-start.26 = (bf16[512,1024]{1,0:T(8,128)(2,1)}, bf16[512,1024]{1,0:T(8,128)(2,1)}, u32[]{:S(2)}, u32[]{:S(2)}) collective-permute-start(bf16[512,1024]{1,0:T(8,128)(2,1)} %get-tuple-element.107), channel_id=1, source_target_pairs={{0,1},{1,0},{2,3},{3,2},{4,5},{5,4},{6,7},{7,6},{8,9},{9,8},{10,11... | collective-permute-start | bytes 3145736 | tf_op jit(solution)/shard_map/ppermute | solution.py:103
  119.2 28.9 %collective-permute-start.18 = (bf16[512,1024]{1,0:T(8,128)(2,1)}, bf16[512,1024]{1,0:T(8,128)(2,1)}, u32[]{:S(2)}, u32[]{:S(2)}) collective-permute-start(bf16[512,1024]{1,0:T(8,128)(2,1)} %get-tuple-element.111), channel_id=1, source_target_pairs={{0,1},{1,0},{2,3},{3,2},{4,5},{5,4},{6,7},{7,6},{8,9},{9,8},{10,11... | collective-permute-start | bytes 3145736 | tf_op jit(solution)/shard_map/ppermute | solution.py:103
  126.0 16.8 %collective-permute-start.8 = (bf16[256,1024]{1,0:T(8,128)(2,1)S(1)}, bf16[256,1024]{1,0:T(8,128)(2,1)}, u32[]{:S(2)}, u32[]{:S(2)}) collective-permute-start(bf16[256,1024]{1,0:T(8,128)(2,1)S(1)} %pad_maximum_fusion.8), channel_id=1, source_target_pairs={{0,2},{1,3},{2,4},{3,5},{4,6},{5,7},{8,10},{9,11},{10,12},{11,13},... | collective-permute-start | bytes 1572872 | tf_op jit(solution)/shard_map/ppermute | solution.py:100
  135.6 70.8 %collective-permute-start.37 = (bf16[128,1024]{1,0:T(8,128)(2,1)}, bf16[128,1024]{1,0:T(8,128)(2,1)}, u32[]{:S(2)}, u32[]{:S(2)}) collective-permute-start(bf16[128,1024]{1,0:T(8,128)(2,1)} %slice.469), channel_id=1, source_target_pairs={{0,8},{8,0},{16,24},{24,16},{1,9},{9,1},{17,25},{25,17},{2,10},{10... | collective-permute-start | bytes 786440 | tf_op jit(solution)/shard_map/ppermute | solution.py:64
  142.8 15.8 %collective-permute-start.9 = (bf16[256,1024]{1,0:T(8,128)(2,1)}, bf16[256,1024]{1,0:T(8,128)(2,1)}, u32[]{:S(2)}, u32[]{:S(2)}) collective-permute-start(bf16[256,1024]{1,0:T(8,128)(2,1)} %collective-permute-done.8), channel_id=1, source_target_pairs={{0,2},{1,3},{2,4},{3,5},{4,6},{5,7},{8,10},{9,11},{10,12},{11,13},... | collective-permute-start | bytes 1572872 | tf_op jit(solution)/shard_map/ppermute | solution.py:100
  198.6 21.1 %collective-permute-start.27 = (bf16[256,1024]{1,0:T(8,128)(2,1)S(1)}, bf16[256,1024]{1,0:T(8,128)(2,1)S(1)}, u32[]{:S(2)}, u32[]{:S(2)}) collective-permute-start(bf16[256,1024]{1,0:T(8,128)(2,1)S(1)} %get-tuple-element.24), channel_id=1, source_target_pairs={{0,8},{8,0},{16,24},{24,16},{1,9},{9,1},{17,25},{25,17},{2,10},{10... | collective-permute-start | bytes 1572872 | tf_op jit(solution)/shard_map/ppermute | solution.py:64
  200.0 14.8 %collective-permute-start.28 = (bf16[256,1024]{1,0:T(8,128)(2,1)S(1)}, bf16[256,1024]{1,0:T(8,128)(2,1)S(1)}, u32[]{:S(2)}, u32[]{:S(2)}) collective-permute-start(bf16[256,1024]{1,0:T(8,128)(2,1)S(1)} %get-tuple-element.24), channel_id=1, source_target_pairs={{0,16},{8,24},{16,0},{24,8},{1,17},{9,25},{17,1},{25,9},{2,18},{10... | collective-permute-start | bytes 1572872 | tf_op jit(solution)/shard_map/ppermute | solution.py:64
  203.0 16.7 %collective-permute-start.38 = (bf16[128,1024]{1,0:T(8,128)(2,1)S(1)}, bf16[128,1024]{1,0:T(8,128)(2,1)S(1)}, u32[]{:S(2)}, u32[]{:S(2)}) collective-permute-start(bf16[128,1024]{1,0:T(8,128)(2,1)S(1)} %slice.470), channel_id=1, source_target_pairs={{0,16},{8,24},{16,0},{24,8},{1,17},{9,25},{17,1},{25,9},{2,18},{10... | collective-permute-start | bytes 786440 | tf_op jit(solution)/shard_map/ppermute | solution.py:64
  278.7 221.0 %reduce-scatter.5.cloned.1.call-start = ((), (), s32[]{:S(2)}) async-start(), calls=%async_computation.8 | async-start | bytes 2654208 | tf_op jit(solution)/shard_map/reduce_scatter | solution.py:307
  291.6 18.4 %collective-permute-start.40 = (bf16[256,1024]{1,0:T(8,128)(2,1)}, bf16[256,1024]{1,0:T(8,128)(2,1)}, u32[]{:S(2)}, u32[]{:S(2)}) collective-permute-start(bf16[256,1024]{1,0:T(8,128)(2,1)} %pad_maximum_fusion.12), channel_id=1, source_target_pairs={{0,8},{8,0},{16,24},{24,16},{1,9},{9,1},{17,25},{25,17},{2,10},{10... | collective-permute-start | bytes 1572872 | tf_op jit(solution)/shard_map/ppermute | solution.py:64
  293.0 17.0 %collective-permute-start.42 = (bf16[256,1024]{1,0:T(8,128)(2,1)}, bf16[256,1024]{1,0:T(8,128)(2,1)}, u32[]{:S(2)}, u32[]{:S(2)}) collective-permute-start(bf16[256,1024]{1,0:T(8,128)(2,1)} %pad_maximum_fusion.13), channel_id=1, source_target_pairs={{0,16},{8,24},{16,0},{24,8},{1,17},{9,25},{17,1},{25,9},{2,18},{10... | collective-permute-start | bytes 1572872 | tf_op jit(solution)/shard_map/ppermute | solution.py:64
  298.2 18.9 %collective-permute-start.32 = (bf16[256,1024]{1,0:T(8,128)(2,1)}, bf16[256,1024]{1,0:T(8,128)(2,1)}, u32[]{:S(2)}, u32[]{:S(2)}) collective-permute-start(bf16[256,1024]{1,0:T(8,128)(2,1)} %pad_maximum_fusion.10), channel_id=1, source_target_pairs={{0,8},{8,0},{16,24},{24,16},{1,9},{9,1},{17,25},{25,17},{2,10},{10... | collective-permute-start | bytes 1572872 | tf_op jit(solution)/shard_map/ppermute | solution.py:64
  300.6 16.5 %collective-permute-start.34 = (bf16[256,1024]{1,0:T(8,128)(2,1)}, bf16[256,1024]{1,0:T(8,128)(2,1)}, u32[]{:S(2)}, u32[]{:S(2)}) collective-permute-start(bf16[256,1024]{1,0:T(8,128)(2,1)} %pad_maximum_fusion.11), channel_id=1, source_target_pairs={{0,16},{8,24},{16,0},{24,8},{1,17},{9,25},{17,1},{25,9},{2,18},{10... | collective-permute-start | bytes 1572872 | tf_op jit(solution)/shard_map/ppermute | solution.py:64
  374.3 12.1 %collective-permute-start.43 = (bf16[512,1024]{1,0:T(8,128)(2,1)}, bf16[512,1024]{1,0:T(8,128)(2,1)}, u32[]{:S(2)}, u32[]{:S(2)}) collective-permute-start(bf16[512,1024]{1,0:T(8,128)(2,1)} %pad_maximum_fusion.6), channel_id=1, source_target_pairs={{0,1},{1,0},{2,3},{3,2},{4,5},{5,4},{6,7},{7,6},{8,9},{9,8},{10,11... | collective-permute-start | bytes 3145736 | tf_op jit(solution)/shard_map/ppermute | solution.py:103
  376.8 13.6 %collective-permute-start.62 = (bf16[512,1024]{1,0:T(8,128)(2,1)}, bf16[512,1024]{1,0:T(8,128)(2,1)}, u32[]{:S(2)}, u32[]{:S(2)}) collective-permute-start(bf16[512,1024]{1,0:T(8,128)(2,1)} %slice.518), channel_id=1, source_target_pairs={{0,1},{1,0},{2,3},{3,2},{4,5},{5,4},{6,7},{7,6},{8,9},{9,8},{10,11... | collective-permute-start | bytes 3145736 | tf_op jit(solution)/shard_map/ppermute | solution.py:103
  380.6 13.4 %collective-permute-start.46 = (bf16[512,1024]{1,0:T(8,128)(2,1)}, bf16[512,1024]{1,0:T(8,128)(2,1)}, u32[]{:S(2)}, u32[]{:S(2)}) collective-permute-start(bf16[512,1024]{1,0:T(8,128)(2,1)} %slice.490), channel_id=1, source_target_pairs={{0,1},{1,0},{2,3},{3,2},{4,5},{5,4},{6,7},{7,6},{8,9},{9,8},{10,11... | collective-permute-start | bytes 3145736 | tf_op jit(solution)/shard_map/ppermute | solution.py:103
  388.9 29.1 %collective-permute-start.44 = (bf16[256,1024]{1,0:T(8,128)(2,1)S(1)}, bf16[256,1024]{1,0:T(8,128)(2,1)S(1)}, u32[]{:S(2)}, u32[]{:S(2)}) collective-permute-start(bf16[256,1024]{1,0:T(8,128)(2,1)S(1)} %slice.620), channel_id=1, source_target_pairs={{2,0},{3,1},{4,2},{5,3},{6,4},{7,5},{10,8},{11,9},{12,10},{13,11},... | collective-permute-start | bytes 1572872 | tf_op jit(solution)/shard_map/ppermute | solution.py:100
  403.2 11.0 %collective-permute-start.48 = (bf16[128,1024]{1,0:T(8,128)(2,1)S(1)}, bf16[128,1024]{1,0:T(8,128)(2,1)S(1)}, u32[]{:S(2)}, u32[]{:S(2)}) collective-permute-start(bf16[128,1024]{1,0:T(8,128)(2,1)S(1)} %pad_maximum_fusion.22), channel_id=1, source_target_pairs={{0,8},{8,0},{16,24},{24,16},{1,9},{9,1},{17,25},{25,17},{2,10},{10... | collective-permute-start | bytes 786440 | tf_op jit(solution)/shard_map/ppermute | solution.py:64
  404.5 12.7 %collective-permute-start.50 = (bf16[128,1024]{1,0:T(8,128)(2,1)S(1)}, bf16[128,1024]{1,0:T(8,128)(2,1)S(1)}, u32[]{:S(2)}, u32[]{:S(2)}) collective-permute-start(bf16[128,1024]{1,0:T(8,128)(2,1)S(1)} %pad_maximum_fusion.23), channel_id=1, source_target_pairs={{0,16},{8,24},{16,0},{24,8},{1,17},{9,25},{17,1},{25,9},{2,18},{10... | collective-permute-start | bytes 786440 | tf_op jit(solution)/shard_map/ppermute | solution.py:64
  408.9 14.7 %collective-permute-start.67 = (bf16[32,1024]{1,0:T(8,128)(2,1)S(1)}, bf16[32,1024]{1,0:T(8,128)(2,1)S(1)}, u32[]{:S(2)}, u32[]{:S(2)}) collective-permute-start(bf16[32,1024]{1,0:T(8,128)(2,1)S(1)} %get-tuple-element.84), channel_id=1, source_target_pairs={{0,2},{1,3},{2,4},{3,5},{4,6},{5,7},{6,0},{7,1},{8,10},{9,11},{10,... | collective-permute-start | bytes 196616 | tf_op jit(solution)/shard_map/ppermute | solution.py:106
  412.0 13.5 %collective-permute-start.68 = (bf16[32,1024]{1,0:T(8,128)(2,1)S(1)}, bf16[32,1024]{1,0:T(8,128)(2,1)S(1)}, u32[]{:S(2)}, u32[]{:S(2)}) collective-permute-start(bf16[32,1024]{1,0:T(8,128)(2,1)S(1)} %get-tuple-element.86), channel_id=1, source_target_pairs={{0,4},{1,5},{2,6},{3,7},{4,0},{5,1},{6,2},{7,3},{8,12},{9,13},{10,... | collective-permute-start | bytes 196616 | tf_op jit(solution)/shard_map/ppermute | solution.py:106
  414.2 13.8 %collective-permute-start.69 = (bf16[32,1024]{1,0:T(8,128)(2,1)S(1)}, bf16[32,1024]{1,0:T(8,128)(2,1)S(1)}, u32[]{:S(2)}, u32[]{:S(2)}) collective-permute-start(bf16[32,1024]{1,0:T(8,128)(2,1)S(1)} %get-tuple-element.85), channel_id=1, source_target_pairs={{0,6},{1,7},{2,0},{3,1},{4,2},{5,3},{6,4},{7,5},{8,14},{9,15},{10,... | collective-permute-start | bytes 196616 | tf_op jit(solution)/shard_map/ppermute | solution.py:106
  418.2 31.4 %collective-permute-start.45 = (bf16[256,1024]{1,0:T(8,128)(2,1)S(1)}, bf16[256,1024]{1,0:T(8,128)(2,1)S(1)}, u32[]{:S(2)}, u32[]{:S(2)}) collective-permute-start(bf16[256,1024]{1,0:T(8,128)(2,1)S(1)} %fusion.70), channel_id=1, source_target_pairs={{2,0},{3,1},{4,2},{5,3},{6,4},{7,5},{10,8},{11,9},{12,10},{13,11},... | collective-permute-start | bytes 1572872 | tf_op jit(solution)/shard_map/ppermute | solution.py:100
  419.5 25.8 %collective-permute-start.51 = (bf16[32,1024]{1,0:T(8,128)(2,1)S(1)}, bf16[32,1024]{1,0:T(8,128)(2,1)S(1)}, u32[]{:S(2)}, u32[]{:S(2)}) collective-permute-start(bf16[32,1024]{1,0:T(8,128)(2,1)S(1)} %get-tuple-element.90), channel_id=1, source_target_pairs={{0,2},{1,3},{2,4},{3,5},{4,6},{5,7},{6,0},{7,1},{8,10},{9,11},{10,... | collective-permute-start | bytes 196616 | tf_op jit(solution)/shard_map/ppermute | solution.py:106
  423.6 25.2 %collective-permute-start.52 = (bf16[32,1024]{1,0:T(8,128)(2,1)S(1)}, bf16[32,1024]{1,0:T(8,128)(2,1)S(1)}, u32[]{:S(2)}, u32[]{:S(2)}) collective-permute-start(bf16[32,1024]{1,0:T(8,128)(2,1)S(1)} %get-tuple-element.92), channel_id=1, source_target_pairs={{0,4},{1,5},{2,6},{3,7},{4,0},{5,1},{6,2},{7,3},{8,12},{9,13},{10,... | collective-permute-start | bytes 196616 | tf_op jit(solution)/shard_map/ppermute | solution.py:106
  425.5 23.3 %collective-permute-start.53 = (bf16[32,1024]{1,0:T(8,128)(2,1)S(1)}, bf16[32,1024]{1,0:T(8,128)(2,1)S(1)}, u32[]{:S(2)}, u32[]{:S(2)}) collective-permute-start(bf16[32,1024]{1,0:T(8,128)(2,1)S(1)} %get-tuple-element.91), channel_id=1, source_target_pairs={{0,6},{1,7},{2,0},{3,1},{4,2},{5,3},{6,4},{7,5},{8,14},{9,15},{10,... | collective-permute-start | bytes 196616 | tf_op jit(solution)/shard_map/ppermute | solution.py:106
  456.5 14.2 %collective-permute-start.54 = (bf16[512,1024]{1,0:T(8,128)(2,1)}, bf16[512,1024]{1,0:T(8,128)(2,1)}, u32[]{:S(2)}, u32[]{:S(2)}) collective-permute-start(bf16[512,1024]{1,0:T(8,128)(2,1)} %slice.503), channel_id=1, source_target_pairs={{0,1},{1,0},{2,3},{3,2},{4,5},{5,4},{6,7},{7,6},{8,9},{9,8},{10,11... | collective-permute-start | bytes 3145736 | tf_op jit(solution)/shard_map/ppermute | solution.py:103
  466.4 20.6 %all-to-all-start.1 = ((f32[32,1,192]{2,1,0:T(1,128)}), f32[32,1,192]{2,1,0:T(1,128)S(1)}, u32[]{:S(2)}, u32[]{:S(2)}) async-start(f32[32,1,192]{2,1,0:T(1,128)} %all_to_all.13), calls=%async_computation.1 | async-start | bytes 65536 | tf_op jit(solution)/shard_map/all_to_all | solution.py:411
  495.4 10.4 %all-to-all-start.2 = ((bf16[4,32,2304]{2,1,0:T(8,128)(2,1)}), bf16[4,32,2304]{2,1,0:T(8,128)(2,1)S(1)}, u32[]{:S(2)}, u32[]{:S(2)}) async-start(bf16[4,32,2304]{2,1,0:T(8,128)(2,1)} %reduce-scatter.3.cloned.1.call-done), calls=%async_computation.3 | async-start | bytes 1179648 | tf_op jit(solution)/shard_map/all_to_all | solution.py:318
  (108 other events, 861.0 us)
Sparse Core Ops, SparseCore 0:
  25.7 60.7 all-gather.2
  88.1 30.0 all-gather.4
  278.8 54.1 reduce-scatter.2
  385.3 53.1 reduce-scatter.4

commit v3 on v2

--- a/solution.py
+++ b/solution.py
@@ -64,23 +64,31 @@
     return lax.ppermute(value, "dp", [(i, i ^ bits) for i in range(count)])
 
 
-def gather_dp(value, count):
+def after(value, *others):
+    return lax.optimization_barrier((value, *others))[0]
+
+
+def gather_parts(value, count):
     if count != 4:
-        return lax.all_gather(value, "dp", axis=0, tiled=True)
+        return [lax.all_gather(value, "dp", axis=0, tiled=True)]
     half = value.shape[0] // 2
     one = swap_dp(value, 1, count)
     two = swap_dp(value, 2, count)
     top = swap_dp(two[:half], 1, count)
     bottom = swap_dp(one[half:], 2, count)
-    return jnp.concatenate([value, one, two, top, bottom], axis=0)
-
-
-def scatter_sum_dp(parts, count):
+    return [value, one, two, jnp.concatenate([top, bottom], axis=0)]
+
+
+def gather_dp(value, count):
+    return jnp.concatenate(gather_parts(value, count), axis=0)
+
+
+def scatter_parts(parts, count, fill=()):
     if count != 4:
-        return lax.psum_scatter(parts, "dp", scatter_dimension=0, tiled=True).astype(F32)
-    rows = parts.shape[0] // 4
-    half = rows // 2
-    own, one, two, far = (parts[i * rows : (i + 1) * rows] for i in range(4))
+        total = lax.psum_scatter(parts[0], "dp", scatter_dimension=0, tiled=True).astype(F32)
+        return (total, fill)
+    own, one, two, far = parts
+    half = own.shape[0] // 2
     top = swap_dp(far[:half], 1, count).astype(F32)
     bottom = swap_dp(far[half:], 2, count).astype(F32)
     two_sum = jnp.concatenate(
@@ -89,9 +97,34 @@
     one_sum = jnp.concatenate(
         [one[:half], (one[half:].astype(F32) + bottom).astype(BF16)], axis=0
     )
-    from_one = swap_dp(one_sum, 1, count).astype(F32)
-    from_two = swap_dp(two_sum, 2, count).astype(F32)
-    return own.astype(F32) + from_one + from_two
+    from_one = swap_dp(one_sum, 1, count)
+    from_two = swap_dp(two_sum, 2, count)
+    if fill:
+        from_one, from_two, *fill = lax.optimization_barrier((from_one, from_two, *fill))
+    return (own.astype(F32) + from_one.astype(F32) + from_two.astype(F32), tuple(fill))
+
+
+def scatter_sum_dp(value, count):
+    if count != 4:
+        return scatter_parts([value], count)[0]
+    rows = value.shape[0] // 4
+    return scatter_parts([value[i * rows : (i + 1) * rows] for i in range(4)], count)[0]
+
+
+def xor_order(value, rank):
+    split = value.reshape((2, 2) + value.shape[1:])
+    split = jnp.where(rank & 2, split[::-1], split)
+    split = jnp.where(rank & 1, split[:, ::-1], split)
+    return split.reshape(value.shape)
+
+
+def exchange_dp(value, count):
+    if count != 4:
+        return lax.all_to_all(value, "dp", 0, 0, tiled=True)
+    rank = lax.axis_index("dp")
+    value = xor_order(value, rank)
+    value = jnp.stack([value[0]] + [swap_dp(value[j], j, count) for j in range(1, 4)])
+    return xor_order(value, rank)
 
 
 def make_body(dp_count, seq_shards):
@@ -121,11 +154,16 @@
         source = ((peer * seq_shards) + chip * 2 + core) * rows + inner
         return (slot_row[:, None] == source[None, :]).astype(BF16)
 
-    def gather_rows(value):
+    def gather_line(value):
         if not in_slots:
-            return lax.all_gather(value, BOTH, axis=0, tiled=True)
+            return value
         line = [value] + [turn_seq(value, -2 * k) for k in range(1, pairs)]
-        plane = gather_dp(jnp.concatenate(line, axis=0), dp_count)
+        return jnp.concatenate(line, axis=0)
+
+    def gather_rest(line):
+        if not in_slots:
+            return lax.all_gather(line, BOTH, axis=0, tiled=True)
+        plane = gather_dp(line, dp_count)
         return jnp.concatenate([plane, swap_core(plane)], axis=0)
 
     def scatter_rows(parts):
@@ -181,11 +219,12 @@
 
         gains = jnp.stack([attn_gain, ffn_gain], axis=1)
         gains = jnp.pad(gains, ((0, 0), (0, 126)))
-        pack = gather_rows(jnp.concatenate([w_key, w_value, gains], axis=1))
+        pack_line = gather_line(jnp.concatenate([w_key, w_value, gains], axis=1))
+        query_line = gather_line(after(w_query, pack_line))
+        pack = gather_rest(pack_line)
         kv_all = pack[:, : 2 * key_width]
         gain_cols = pack[:, 2 * key_width :].astype(F32)
-        query_all = gather_rows(w_query)
-        out_all = gather_rows(w_out)
+        query_all = gather_rest(after(query_line, pack))
         if in_slots:
             slots = slot_matrix(model_width)
             out_slots = slots if query_width == model_width else slot_matrix(query_width)
@@ -212,12 +251,13 @@
             ],
             axis=2,
         )
-        gate_up = lax.all_to_all(jnp.moveaxis(gate_up, 1, 0), "dp", 0, 0, tiled=True)
-        down_all = lax.all_gather(w_down, "seq", axis=0, tiled=True)
+        gate_up = exchange_dp(jnp.moveaxis(gate_up, 1, 0), dp_count)
+        gate_up = after(gate_up, pack_line)
+        down_all = lax.all_gather(after(w_down, gate_up), "seq", axis=0, tiled=True)
         gate_up_all = lax.all_gather(gate_up, "seq", axis=1, tiled=True).reshape(
             model_width, 2 * ffn_part
         )
-        cotangent_all = gather_dp(cotangent, dp_count)
+        cotangent_parts = gather_parts(after(cotangent, query_all), dp_count)
 
         stream = tokens.astype(F32)
         scale_one = rms_scale(stream)
@@ -247,6 +287,7 @@
         both = [jnp.concatenate([key_rot, value_send], axis=1)]
         for _ in range(hops):
             both.append(shift_seq(both[-1], 2))
+        out_all = gather_rest(gather_line(after(w_out, both[-1])))
         for_even = jnp.concatenate(both[:-1], axis=0)
         for_odd = jnp.concatenate(both[1:], axis=0)
         across = swap_core(jnp.where(core == 0, for_even, for_odd))
@@ -287,36 +328,74 @@
 
         scale_two = rms_scale(middle)
         normed_two = (middle * scale_two * ffn_gain_all).astype(BF16)
-        normed_all = gather_dp(normed_two, dp_count)
-        both_pre = dot(normed_all, gate_up_all)
-        gate_pre = both_pre[:, :ffn_part]
-        up_pre = both_pre[:, ffn_part:]
-        sigmoid_gate = jax.nn.sigmoid(gate_pre)
-        silu_gate = gate_pre * sigmoid_gate
-        hidden = (silu_gate * up_pre).astype(BF16)
-        out_part = dot(hidden, down_all).astype(BF16)
-        output = (middle + scatter_sum_dp(out_part, dp_count)).astype(BF16)
+        normed_parts = gather_parts(normed_two, dp_count)
+
+        def chunked(parts):
+            if len(parts) == 1:
+                return list(parts)
+            own, one, two, far = parts
+            return [own, jnp.concatenate([one, two], axis=0), far]
+
+        def whole(chunks):
+            return chunks[0] if len(chunks) == 1 else jnp.concatenate(chunks, axis=0)
+
+        def parts_of(chunks):
+            if len(chunks) == 1:
+                return list(chunks)
+            own, middle_two, far = chunks
+            return [own, middle_two[:local_len], middle_two[local_len:], far]
+
+        normed_chunks = chunked(normed_parts)
+        cotangent_chunks = chunked(cotangent_parts)
+        saved = []
+        hidden_chunks = []
+        for chunk in normed_chunks:
+            both_pre = dot(chunk, gate_up_all)
+            gate_pre = both_pre[:, :ffn_part]
+            up_pre = both_pre[:, ffn_part:]
+            sigmoid_gate = jax.nn.sigmoid(gate_pre)
+            silu_gate = gate_pre * sigmoid_gate
+            hidden_chunks.append((silu_gate * up_pre).astype(BF16))
+            saved.append((gate_pre, up_pre, sigmoid_gate, silu_gate))
         grad_output = cotangent.astype(F32)
-        grad_hidden = dot_nt(cotangent_all, down_all)
-        grad_gate = (
-            grad_hidden * up_pre * sigmoid_gate * (1.0 + gate_pre * (1.0 - sigmoid_gate))
-        ).astype(BF16)
-        grad_up = (grad_hidden * silu_gate).astype(BF16)
-        grad_both = jnp.concatenate([grad_gate, grad_up], axis=1)
-        grad_normed_two = scatter_sum_dp(dot_nt(grad_both, gate_up_all).astype(BF16), dp_count)
-        grad_down_w = lax.psum_scatter(
-            dot_tn(hidden, cotangent_all).astype(BF16), "seq", scatter_dimension=0, tiled=True
+        grad_chunks = [None] * len(saved)
+        back_chunks = [None] * len(saved)
+        previous = None
+        for i in reversed(range(len(saved))):
+            gate_pre, up_pre, sigmoid_gate, silu_gate = saved[i]
+            incoming = cotangent_chunks[i]
+            if previous is not None:
+                incoming = after(incoming, previous)
+            grad_hidden = dot_nt(incoming, down_all)
+            grad_gate = (
+                grad_hidden * up_pre * sigmoid_gate * (1.0 + gate_pre * (1.0 - sigmoid_gate))
+            ).astype(BF16)
+            grad_up = (grad_hidden * silu_gate).astype(BF16)
+            grad_chunks[i] = jnp.concatenate([grad_gate, grad_up], axis=1)
+            back_chunks[i] = dot_nt(grad_chunks[i], gate_up_all).astype(BF16)
+            previous = back_chunks[i]
+        hidden = whole(hidden_chunks)
+        grad_both = whole(grad_chunks)
+        normed_all = whole(normed_chunks)
+        cotangent_all = whole(cotangent_chunks)
+        gate_up_part = dot_tn(normed_all, grad_both).astype(BF16)
+        down_part = dot_tn(hidden, cotangent_all).astype(BF16)
+        grad_normed_two, (gate_up_part, down_part) = scatter_parts(
+            parts_of(back_chunks), dp_count, (gate_up_part, down_part)
         )
         grad_gate_up = lax.psum_scatter(
-            dot_tn(normed_all, grad_both)
-            .astype(BF16)
-            .reshape(dp_count, seq_shards * rows, 2 * ffn_part),
+            gate_up_part.reshape(dp_count, seq_shards * rows, 2 * ffn_part),
             "seq",
             scatter_dimension=1,
             tiled=True,
         )
-        grad_gate_up = lax.all_to_all(grad_gate_up, "dp", 0, 0, tiled=True).astype(F32)
-        grad_gate_up = jnp.moveaxis(grad_gate_up, 0, 1)
+        grad_down_w = lax.psum_scatter(
+            after(down_part, gate_up_part), "seq", scatter_dimension=0, tiled=True
+        )
+        out_chunks = [dot(chunk, down_all).astype(BF16) for chunk in hidden_chunks]
+        output = (middle + scatter_parts(parts_of(out_chunks), dp_count)[0]).astype(BF16)
+        grad_gate_up = exchange_dp(grad_gate_up, dp_count)
+        grad_gate_up = jnp.moveaxis(grad_gate_up.astype(F32), 0, 1)
         grad_gate_w = grad_gate_up[..., :ffn_part].reshape(rows, ffn_width)
         grad_up_w = grad_gate_up[..., ffn_part:].reshape(rows, ffn_width)
 
@@ -359,6 +438,7 @@
             ],
             axis=1,
         ).astype(BF16)
+        grad_window, grad_out_w = lax.optimization_barrier((grad_window, grad_out_w))
         split = (hops + 1) * local_len
         back = swap_core(grad_window[split:])
         zero = jnp.zeros((local_len, 2 * key_width), BF16)

time: 520 us -> 558 us (1.073)
  waiting for transfers between devices: 102 us -> 144 us
  blocking collectives: 14.5 us -> 0 us
  local copies, waits for them, and re-layouts: 94.7 us -> 82.4 us
  starting transfers between devices: 101 us -> 110 us
  matrix products: 142 us -> 150 us
    ppermute x4, waiting for transfers between devices: 9.58 us -> 43.6 us  [shift_seq(): return lax.ppermute(value, 'seq', pairs)]
    dot_general x5, matrix products: 16.6 us -> 33.6 us  [dot_tn(): lax.dot_general(left, right, (((0,), (0,)), ((), ())), preferred_element_...]
    all_to_all x1 -> x0, blocking collectives: 14.5 us -> none  [body(): lax.all_to_all(jnp.moveaxis(gate_up, 1, 0), 'dp', 0, 0, tiled=True)]
    ppermute x40 -> x46, waiting for transfers between devices: 56.5 us -> 65 us  [swap_dp(): return lax.ppermute(value, 'dp', [(i, i ^ bits) for i in range(count)])]
    dot_general x7 -> x11, matrix products: 30.9 us -> 23.8 us  [dot(): return jnp.dot(left, right, preferred_element_type=F32)]
    ppermute x40 -> x46, starting transfers between devices: 43.5 us -> 50.6 us  [swap_dp(): return lax.ppermute(value, 'dp', [(i, i ^ bits) for i in range(count)])]
    unnamed x193 -> x205, local copies, waits for them, and re-layouts: 37.9 us -> 31.2 us
    ppermute x18, starting transfers between devices: 34.8 us -> 41.4 us  [turn_seq(): lax.ppermute(value, 'seq', [(i, (i + step) % seq_shards) for i in range(s...]
  transfers between devices with their start and end apart: 76 -> 81, of which waited for: 28 -> 38; matrix products, arithmetic and copies ran while one was open for 47% -> 44% of each run, Pallas kernels for 0% -> 0%
where the time goes in v3:
time: 558 us; the launch traced here: 550 us
  matrix products  150 us (27%)
  waiting for transfers between devices  144 us (26%)
  starting transfers between devices  110 us (20%)
  local copies, waits for them, and re-layouts  82.4 us (15%)
  other arithmetic  48 us (9%)
  between operations  15.9 us (3%)
    ppermute x46, waiting for transfers between devices, swap_dp(): return lax.ppermute(value, 'dp', [(i, i ^ bits) for i in range(count)])  65 us
    ppermute x46, starting transfers between devices, swap_dp(): return lax.ppermute(value, 'dp', [(i, i ^ bits) for i in range(count)])  50.6 us
    ppermute x4, waiting for transfers between devices, shift_seq(): return lax.ppermute(value, 'seq', pairs)  43.6 us
    ppermute x18, starting transfers between devices, turn_seq(): lax.ppermute(value, 'seq', [(i, (i + step) % seq_shards) for i in range(s...  41.4 us
    ppermute x18, waiting for transfers between devices, turn_seq(): lax.ppermute(value, 'seq', [(i, (i + step) % seq_shards) for i in range(s...  35.7 us
    dot_general x5, matrix products, dot_tn(): lax.dot_general(left, right, (((0,), (0,)), ((), ())), preferred_element_...  33.6 us
    unnamed x205, local copies, waits for them, and re-layouts  31.2 us
    dot_general x11, matrix products, dot(): return jnp.dot(left, right, preferred_element_type=F32)  23.8 us
  transfers between devices with their start and end apart: 81, of which 38 were waited for; matrix products, arithmetic and copies ran while one was open for 44% of the time, Pallas kernels for 0%

profile of v3, /device:TPU:0, one launch (start us, length us, event | category | flops | bytes accessed | tf_op | source)
XLA Modules:
  0.0 550.0 jit_solution(15863911696388105755)
XLA Ops:
  9.4 5.1 collective-permute-start
  21.9 3.6 collective-permute-done.29
  34.0 5.3 collective-permute-done.4
  51.9 2.8 collective-permute-done.13
  54.7 5.1 collective-permute-done.12
  68.7 7.2 %collective-permute-start.8 = (bf16[256,1024]{1,0:T(8,128)(2,1)S(1)}, bf16[256,1024]{1,0:T(8,128)(2,1)S(1)}, u32[]{:S(2)}, u32[]{:S(2)}) collective-permute-start(bf16[256,1024]{1,0:T(8,128)(2,1)S(1)} %pad_maximum_fusion.6), channel_id=1, source_target_pairs={{0,2},{1,3},{2,4},{3,5},{4,6},{5,7},{8,10},{9,11},{10,12},{11,13},... | collective-permute-start | bytes 1572872 | tf_op jit(solution)/shard_map/ppermute | solution.py:133
  79.3 11.2 %collective-permute-done.8 = bf16[256,1024]{1,0:T(8,128)(2,1)S(1)} collective-permute-done((bf16[256,1024]{1,0:T(8,128)(2,1)S(1)}, bf16[256,1024]{1,0:T(8,128)(2,1)S(1)}, u32[]{:S(2)}, u32[]{:S(2)}) %collective-permute-start.8) | collective-permute-done | bytes 524320 | tf_op jit(solution)/shard_map/ppermute | solution.py:133
  90.5 4.7 collective-permute-start.9
  103.7 12.1 %collective-permute-done.9 = bf16[256,1024]{1,0:T(8,128)(2,1)S(1)} collective-permute-done((bf16[256,1024]{1,0:T(8,128)(2,1)S(1)}, bf16[256,1024]{1,0:T(8,128)(2,1)S(1)}, u32[]{:S(2)}, u32[]{:S(2)}) %collective-permute-start.9) | collective-permute-done | bytes 524320 | tf_op jit(solution)/shard_map/ppermute | solution.py:133
  115.9 11.5 %collective-permute-start.19 = (bf16[32,1024]{1,0:T(8,128)(2,1)S(1)}, bf16[32,1024]{1,0:T(8,128)(2,1)S(1)}, u32[]{:S(2)}, u32[]{:S(2)}) collective-permute-start(bf16[32,1024]{1,0:T(8,128)(2,1)S(1)} %copy-done.63), channel_id=1, source_target_pairs={{0,6},{1,7},{2,0},{3,1},{4,2},{5,3},{6,4},{7,5},{8,14},{9,15},{10,... | collective-permute-start | bytes 196616 | tf_op jit(solution)/shard_map/ppermute | solution.py:139
  127.4 4.4 collective-permute-start.20
  142.7 3.8 collective-permute-done.23
  159.2 3.1 pad_maximum_fusion
  166.6 11.5 %fusion.5 = (f32[8,2,256]{2,1,0:T(2,128)S(1)}, f32[8,1280,256,2]{2,1,3,0:T(8,128)}) fusion(pred[256,1280]{0,1:T(8,128)(4,1)} %compare_and_fusion, bf16[1280,8,64,1]{0,2,3,1:T(8,128)(2,1)S(1)} %bitcast.201, bf16[256,8,2,32]{0,3,2,1:T(8,128)(2,1)} %bitcast.229, bf16[256,8,2,32]{0,3,2,1:T(8,128)(2,1)} %bitcast.227), kind=kOutput, calls=%fused_computation.9 | convolution fusion | flops 687861760 | bytes 23150592 | tf_op jit(solution)/shard_map/qgrd,kgd->grqk/dot_general | solution.py:315
  178.1 10.4 %divide_convert_fusion = bf16[256,8,2,64]{0,3,2,1:T(8,128)(2,1)S(1)} fusion(bf16[1280,8,64,1]{0,2,3,1:T(8,128)(2,1)S(1)} %bitcast.203, f32[8,1280,256,2]{2,1,3,0:T(8,128)} %get-tuple-element.198, pred[256,1280]{0,1:T(8,128)(4,1)S(1)} %copy-done.41, f32[256,8,2]{0,2,1:T(2,128)S(1)} %bitcast.241), kind=kOutput, calls=%fused_computation.152 | convolution fusion | flops 682098688 | bytes 23150592 | tf_op jit(solution)/shard_map/grqk,kgd->qgrd/dot_general | solution.py:320
  198.9 2.5 copy.129
  217.3 7.6 %collective-permute-done.30 = bf16[256,1024]{1,0:T(8,128)(2,1)S(1)} collective-permute-done((bf16[256,1024]{1,0:T(8,128)(2,1)}, bf16[256,1024]{1,0:T(8,128)(2,1)S(1)}, u32[]{:S(2)}, u32[]{:S(2)}) %collective-permute-start.30) | collective-permute-done | bytes 524320 | tf_op jit(solution)/shard_map/ppermute | solution.py:64
  232.8 5.4 fusion.118
  238.3 3.9 fusion.200
  242.1 3.8 multiply_convert_fusion.6
  250.3 4.2 fusion.101
  256.9 3.6 fusion.66
  266.6 23.9 %convolution_convert_fusion = bf16[1024,2304]{1,0:T(8,128)(2,1)} fusion(bf16[1024,1024]{1,0:T(8,128)(2,1)} %constant_dynamic-update-slice_fusion.51, bf16[256,1152]{1,0:T(8,128)(2,1)S(1)} %get-tuple-element.61, bf16[256,1152]{1,0:T(8,128)(2,1)S(1)} %get-tuple-element.60, bf16[512,1152]{1,0:T(8,128)(2,1)S(1)} %get-tuple-element.56, ...), kind=kOutput, calls=%fused_computation.19 | convolution fusion | flops 4862509056 | bytes 11534336 | tf_op jit(solution)/shard_map/dot_general | solution.py:56
  290.5 4.2 convolution_convert_fusion.1
  294.7 3.7 convolution_convert_fusion.5
  306.8 9.1 %collective-permute-done.43 = bf16[256,1024]{1,0:T(8,128)(2,1)S(1)} collective-permute-done((bf16[256,1024]{1,0:T(8,128)(2,1)S(1)}, bf16[256,1024]{1,0:T(8,128)(2,1)S(1)}, u32[]{:S(2)}, u32[]{:S(2)}) %collective-permute-start.43) | collective-permute-done | bytes 524320 | tf_op jit(solution)/shard_map/ppermute | solution.py:64
  318.7 6.0 %collective-permute-done.37 = bf16[256,1024]{1,0:T(8,128)(2,1)S(1)} collective-permute-done((bf16[256,1024]{1,0:T(8,128)(2,1)S(1)}, bf16[256,1024]{1,0:T(8,128)(2,1)S(1)}, u32[]{:S(2)}, u32[]{:S(2)}) %collective-permute-start.37) | collective-permute-done | bytes 524320 | tf_op jit(solution)/shard_map/ppermute | solution.py:64
  324.7 2.9 multiply_add_fusion
  327.6 4.3 fusion.80
  331.9 3.1 convolution_convert_fusion.4
  340.7 13.5 %fusion.1 = bf16[8,2,256,1280]{2,3,1,0:T(8,128)(2,1)} fusion(f32[8,1280,256,2]{2,1,3,0:T(8,128)} %get-tuple-element.198, bf16[1280,8,64,1]{0,2,3,1:T(8,128)(2,1)S(1)} %bitcast.204, bf16[256,8,2,64]{0,3,2,1:T(8,128)(2,1)} %bitcast.220, f32[8,2,256]{2,1,0:T(2,128)S(1)} %bitcast.242, f32[8,2,256]{2,1,0:T(2,128)S(1)} %log.7, pred[256,1280]{0,1:T(8,128)(4,1)} %compare_and_fusion), kind=kOutput, calls=%fused_computation.2 | convolution fusion | flops 697303040 | bytes 33652736 | tf_op jit(solution)/shard_map/qgrd,kgd->grqk/dot_general | solution.py:416
  354.2 5.9 %convolution_multiply_fusion.1 = f32[8,64,2,256]{3,1,2,0:T(8,128)S(1)} fusion(bf16[1280,8,64,1]{0,2,3,1:T(8,128)(2,1)S(1)} %bitcast.202, bf16[8,2,256,1280]{2,3,1,0:T(8,128)(2,1)} %fusion.1), kind=kOutput, calls=%fused_computation.86 | convolution fusion | flops 671350784 | bytes 12845056 | tf_op jit(solution)/shard_map/grqk,kgd->qgrd/dot_general | solution.py:431
  363.4 7.4 %fusion.39 = bf16[8,64,1280]{2,1,0:T(8,128)(2,1)S(1)} fusion(bf16[8,2,256,1280]{2,3,1,0:T(8,128)(2,1)} %fusion.1, bf16[256,8,2,32]{0,3,2,1:T(8,128)(2,1)S(1)} %bitcast.230, bf16[256,8,2,32]{0,3,2,1:T(8,128)(2,1)S(1)} %bitcast.228), kind=kOutput, calls=%fused_computation.44 | convolution fusion | flops 673447936 | bytes 12320768 | tf_op jit(solution)/shard_map/grqk,qgrd->kgd/dot_general | solution.py:427
  370.8 10.3 %fusion.40 = bf16[8,64,1280]{2,1,0:T(8,128)(2,1)} fusion(bf16[256,8,2,64]{0,3,2,1:T(8,128)(2,1)S(1)} %bitcast.221, f32[8,1280,256,2]{2,1,3,0:T(8,128)} %get-tuple-element.198, f32[8,2,256]{2,1,0:T(2,128)S(1)} %log.7, pred[256,1280]{0,1:T(8,128)(4,1)S(1)} %copy-done.42), kind=kOutput, calls=%fused_computation.45 | convolution fusion | flops 687472640 | bytes 23150592 | tf_op jit(solution)/shard_map/grqk,qgrd->kgd/dot_general | solution.py:420
  386.2 2.6 copy.133
  397.1 3.6 collective-permute-done.50
  406.4 3.2 collective-permute-done.53
  409.7 6.2 %collective-permute-done.52 = bf16[32,1024]{1,0:T(8,128)(2,1)S(1)} collective-permute-done((bf16[32,1024]{1,0:T(8,128)(2,1)S(1)}, bf16[32,1024]{1,0:T(8,128)(2,1)S(1)}, u32[]{:S(2)}, u32[]{:S(2)}) %collective-permute-start.52) | collective-permute-done | bytes 65568 | tf_op jit(solution)/shard_map/ppermute | solution.py:139
  420.3 4.0 collective-permute-done.58
  436.7 20.2 %collective-permute-done.55 = bf16[256,1024]{1,0:T(8,128)(2,1)} collective-permute-done((bf16[256,1024]{1,0:T(8,128)(2,1)}, bf16[256,1024]{1,0:T(8,128)(2,1)}, u32[]{:S(2)}, u32[]{:S(2)}) %collective-permute-start.55) | collective-permute-done | bytes 524320 | tf_op jit(solution)/shard_map/ppermute | solution.py:133
  460.9 4.1 collective-permute-start.64
  468.6 7.4 %collective-permute-done.64 = bf16[32,1024]{1,0:T(8,128)(2,1)S(1)} collective-permute-done((bf16[32,1024]{1,0:T(8,128)(2,1)}, bf16[32,1024]{1,0:T(8,128)(2,1)S(1)}, u32[]{:S(2)}, u32[]{:S(2)}) %collective-permute-start.64) | collective-permute-done | bytes 65568 | tf_op jit(solution)/shard_map/ppermute | solution.py:139
  476.0 6.3 %collective-permute-done.63 = bf16[32,1024]{1,0:T(8,128)(2,1)S(1)} collective-permute-done((bf16[32,1024]{1,0:T(8,128)(2,1)}, bf16[32,1024]{1,0:T(8,128)(2,1)S(1)}, u32[]{:S(2)}, u32[]{:S(2)}) %collective-permute-start.63) | collective-permute-done | bytes 65568 | tf_op jit(solution)/shard_map/ppermute | solution.py:139
  496.4 4.2 fusion.33
  501.4 2.8 all-to-all-start
  509.3 2.6 collective-permute-done.66
  515.4 4.9 fusion.70
  521.1 3.5 collective-permute-start.72
  (535 shorter events, 231.7 us)
Async XLA Ops:
  7.2 225.6 %all-gather.3.cloned.1.call-start = ((), (), s32[]{:S(2)}) async-start(), calls=%async_computation.3 | async-start | bytes 5308416 | tf_op jit(solution)/shard_map/all_gather | solution.py:257
  9.4 11.8 %collective-permute-start = (bf16[32,1152]{1,0:T(8,128)(2,1)S(1)}, bf16[32,1152]{1,0:T(8,128)(2,1)S(1)}, u32[]{:S(2)}, u32[]{:S(2)}) collective-permute-start(bf16[32,1152]{1,0:T(8,128)(2,1)S(1)} %get-tuple-element.169), channel_id=1, source_target_pairs={{0,6},{1,7},{2,0},{3,1},{4,2},{5,3},{6,4},{7,5},{8,14},{9,15},{10,... | collective-permute-start | bytes 221192 | tf_op jit(solution)/shard_map/ppermute | solution.py:139
  28.3 213.8 %all-gather.5.cloned.1.call-start = ((), (), s32[]{:S(2)}) async-start(), calls=%async_computation.4 | async-start | bytes 2654208 | tf_op jit(solution)/shard_map/all_gather | solution.py:256
  29.8 10.0 %collective-permute-start.3 = (bf16[128,1152]{1,0:T(8,128)(2,1)S(1)}, bf16[128,1152]{1,0:T(8,128)(2,1)S(1)}, u32[]{:S(2)}, u32[]{:S(2)}) collective-permute-start(bf16[128,1152]{1,0:T(8,128)(2,1)S(1)} %pad_maximum_fusion.18), channel_id=1, source_target_pairs={{0,8},{8,0},{16,24},{24,16},{1,9},{9,1},{17,25},{25,17},{2,10},{10... | collective-permute-start | bytes 884744 | tf_op jit(solution)/shard_map/ppermute | solution.py:64
  45.9 13.9 %collective-permute-start.7 = (bf16[512,1152]{1,0:T(8,128)(2,1)}, bf16[512,1152]{1,0:T(8,128)(2,1)}, u32[]{:S(2)}, u32[]{:S(2)}) collective-permute-start(bf16[512,1152]{1,0:T(8,128)(2,1)} %get-tuple-element.147), channel_id=1, source_target_pairs={{0,1},{1,0},{2,3},{3,2},{4,5},{5,4},{6,7},{7,6},{8,9},{9,8},{10,11... | collective-permute-start | bytes 3538952 | tf_op jit(solution)/shard_map/ppermute | solution.py:136
  46.4 8.2 %collective-permute-start.13 = (bf16[32,1024]{1,0:T(8,128)(2,1)S(1)}, bf16[32,1024]{1,0:T(8,128)(2,1)S(1)}, u32[]{:S(2)}, u32[]{:S(2)}) collective-permute-start(bf16[32,1024]{1,0:T(8,128)(2,1)S(1)} %copy-done.64), channel_id=1, source_target_pairs={{0,2},{1,3},{2,4},{3,5},{4,6},{5,7},{6,0},{7,1},{8,10},{9,11},{10,... | collective-permute-start | bytes 196616 | tf_op jit(solution)/shard_map/ppermute | solution.py:139
  49.0 10.8 %collective-permute-start.12 = (bf16[32,1024]{1,0:T(8,128)(2,1)S(1)}, bf16[32,1024]{1,0:T(8,128)(2,1)S(1)}, u32[]{:S(2)}, u32[]{:S(2)}) collective-permute-start(bf16[32,1024]{1,0:T(8,128)(2,1)S(1)} %copy-done.64), channel_id=1, source_target_pairs={{0,4},{1,5},{2,6},{3,7},{4,0},{5,1},{6,2},{7,3},{8,12},{9,13},{10,... | collective-permute-start | bytes 196616 | tf_op jit(solution)/shard_map/ppermute | solution.py:139
  50.4 9.3 %collective-permute-start.11 = (bf16[32,1024]{1,0:T(8,128)(2,1)S(1)}, bf16[32,1024]{1,0:T(8,128)(2,1)S(1)}, u32[]{:S(2)}, u32[]{:S(2)}) collective-permute-start(bf16[32,1024]{1,0:T(8,128)(2,1)S(1)} %copy-done.64), channel_id=1, source_target_pairs={{0,6},{1,7},{2,0},{3,1},{4,2},{5,3},{6,4},{7,5},{8,14},{9,15},{10,... | collective-permute-start | bytes 196616 | tf_op jit(solution)/shard_map/ppermute | solution.py:139
  65.3 32.4 %collective-permute-start.14 = (bf16[128,1024]{1,0:T(8,128)(2,1)S(1)}, bf16[128,1024]{1,0:T(8,128)(2,1)}, u32[]{:S(2)}, u32[]{:S(2)}) collective-permute-start(bf16[128,1024]{1,0:T(8,128)(2,1)S(1)} %pad_maximum_fusion.20), channel_id=1, source_target_pairs={{0,8},{8,0},{16,24},{24,16},{1,9},{9,1},{17,25},{25,17},{2,10},{10... | collective-permute-start | bytes 786440 | tf_op jit(solution)/shard_map/ppermute | solution.py:64
  66.8 28.5 %collective-permute-start.15 = (bf16[128,1024]{1,0:T(8,128)(2,1)S(1)}, bf16[128,1024]{1,0:T(8,128)(2,1)}, u32[]{:S(2)}, u32[]{:S(2)}) collective-permute-start(bf16[128,1024]{1,0:T(8,128)(2,1)S(1)} %pad_maximum_fusion.20), channel_id=1, source_target_pairs={{0,16},{8,24},{16,0},{24,8},{1,17},{9,25},{17,1},{25,9},{2,18},{10... | collective-permute-start | bytes 786440 | tf_op jit(solution)/shard_map/ppermute | solution.py:64
  68.7 21.8 %collective-permute-start.8 = (bf16[256,1024]{1,0:T(8,128)(2,1)S(1)}, bf16[256,1024]{1,0:T(8,128)(2,1)S(1)}, u32[]{:S(2)}, u32[]{:S(2)}) collective-permute-start(bf16[256,1024]{1,0:T(8,128)(2,1)S(1)} %pad_maximum_fusion.6), channel_id=1, source_target_pairs={{0,2},{1,3},{2,4},{3,5},{4,6},{5,7},{8,10},{9,11},{10,12},{11,13},... | collective-permute-start | bytes 1572872 | tf_op jit(solution)/shard_map/ppermute | solution.py:133
  78.0 448.2 %reduce-scatter.5.cloned.1.call-start = ((), (), s32[]{:S(2)}) async-start(), calls=%async_computation.6 | async-start | bytes 2654208 | tf_op jit(solution)/shard_map/reduce_scatter | solution.py:392
  90.5 25.4 %collective-permute-start.9 = (bf16[256,1024]{1,0:T(8,128)(2,1)S(1)}, bf16[256,1024]{1,0:T(8,128)(2,1)S(1)}, u32[]{:S(2)}, u32[]{:S(2)}) collective-permute-start(bf16[256,1024]{1,0:T(8,128)(2,1)S(1)} %collective-permute-done.8), channel_id=1, source_target_pairs={{0,2},{1,3},{2,4},{3,5},{4,6},{5,7},{8,10},{9,11},{10,12},{11,13},... | collective-permute-start | bytes 1572872 | tf_op jit(solution)/shard_map/ppermute | solution.py:133
  103.7 47.6 %collective-permute-start.18 = (bf16[512,1024]{1,0:T(8,128)(2,1)S(1)}, bf16[512,1024]{1,0:T(8,128)(2,1)S(1)}, u32[]{:S(2)}, u32[]{:S(2)}) collective-permute-start(bf16[512,1024]{1,0:T(8,128)(2,1)S(1)} %get-tuple-element.157), channel_id=1, source_target_pairs={{0,1},{1,0},{2,3},{3,2},{4,5},{5,4},{6,7},{7,6},{8,9},{9,8},{10,11... | collective-permute-start | bytes 3145736 | tf_op jit(solution)/shard_map/ppermute | solution.py:136
  115.9 18.7 %collective-permute-start.19 = (bf16[32,1024]{1,0:T(8,128)(2,1)S(1)}, bf16[32,1024]{1,0:T(8,128)(2,1)S(1)}, u32[]{:S(2)}, u32[]{:S(2)}) collective-permute-start(bf16[32,1024]{1,0:T(8,128)(2,1)S(1)} %copy-done.63), channel_id=1, source_target_pairs={{0,6},{1,7},{2,0},{3,1},{4,2},{5,3},{6,4},{7,5},{8,14},{9,15},{10,... | collective-permute-start | bytes 196616 | tf_op jit(solution)/shard_map/ppermute | solution.py:139
  138.7 9.1 %collective-permute-start.22 = (bf16[128,1024]{1,0:T(8,128)(2,1)S(1)}, bf16[128,1024]{1,0:T(8,128)(2,1)S(1)}, u32[]{:S(2)}, u32[]{:S(2)}) collective-permute-start(bf16[128,1024]{1,0:T(8,128)(2,1)S(1)} %get-tuple-element.172), channel_id=1, source_target_pairs={{0,8},{8,0},{16,24},{24,16},{1,9},{9,1},{17,25},{25,17},{2,10},{10... | collective-permute-start | bytes 786440 | tf_op jit(solution)/shard_map/ppermute | solution.py:64
  142.7 16.5 %collective-permute-start.10 = (bf16[512,1024]{1,0:T(8,128)(2,1)}, bf16[512,1024]{1,0:T(8,128)(2,1)}, u32[]{:S(2)}, u32[]{:S(2)}) collective-permute-start(bf16[512,1024]{1,0:T(8,128)(2,1)} %maximum_select_fusion), channel_id=1, source_target_pairs={{0,1},{1,0},{2,3},{3,2},{4,5},{5,4},{6,7},{7,6},{8,9},{9,8},{10,11... | collective-permute-start | bytes 3145736 | tf_op jit(solution)/shard_map/ppermute | solution.py:136
  147.1 8.8 %collective-permute-start.24 = (bf16[64,1024]{1,0:T(8,128)(2,1)}, bf16[64,1024]{1,0:T(8,128)(2,1)}, u32[]{:S(2)}, u32[]{:S(2)}) collective-permute-start(bf16[64,1024]{1,0:T(8,128)(2,1)} %slice.489), channel_id=1, source_target_pairs={{0,8},{8,0},{16,24},{24,16},{1,9},{9,1},{17,25},{25,17},{2,10},{10... | collective-permute-start | bytes 393224 | tf_op jit(solution)/shard_map/ppermute | solution.py:64
  148.4 9.1 %collective-permute-start.25 = (bf16[64,1024]{1,0:T(8,128)(2,1)}, bf16[64,1024]{1,0:T(8,128)(2,1)}, u32[]{:S(2)}, u32[]{:S(2)}) collective-permute-start(bf16[64,1024]{1,0:T(8,128)(2,1)} %slice.490), channel_id=1, source_target_pairs={{0,16},{8,24},{16,0},{24,8},{1,17},{9,25},{17,1},{25,9},{2,18},{10... | collective-permute-start | bytes 393224 | tf_op jit(solution)/shard_map/ppermute | solution.py:64
  152.1 49.3 %collective-permute-start.38 = (bf16[256,1024]{1,0:T(8,128)(2,1)}, bf16[256,1024]{1,0:T(8,128)(2,1)}, u32[]{:S(2)}, u32[]{:S(2)}) collective-permute-start(bf16[256,1024]{1,0:T(8,128)(2,1)} %bitcast.38), channel_id=1, source_target_pairs={{0,8},{8,0},{16,24},{24,16},{1,9},{9,1},{17,25},{25,17},{2,10},{10... | collective-permute-start | bytes 1572872 | tf_op jit(solution)/shard_map/ppermute | solution.py:64
  153.2 50.2 %collective-permute-start.39 = (bf16[256,1024]{1,0:T(8,128)(2,1)}, bf16[256,1024]{1,0:T(8,128)(2,1)}, u32[]{:S(2)}, u32[]{:S(2)}) collective-permute-start(bf16[256,1024]{1,0:T(8,128)(2,1)} %bitcast.38), channel_id=1, source_target_pairs={{0,16},{8,24},{16,0},{24,8},{1,17},{9,25},{17,1},{25,9},{2,18},{10... | collective-permute-start | bytes 1572872 | tf_op jit(solution)/shard_map/ppermute | solution.py:64
  159.1 30.3 %collective-permute-start.26 = (bf16[512,1024]{1,0:T(8,128)(2,1)}, bf16[512,1024]{1,0:T(8,128)(2,1)}, u32[]{:S(2)}, u32[]{:S(2)}) collective-permute-start(bf16[512,1024]{1,0:T(8,128)(2,1)} %get-tuple-element.153), channel_id=1, source_target_pairs={{0,1},{1,0},{2,3},{3,2},{4,5},{5,4},{6,7},{7,6},{8,9},{9,8},{10,11... | collective-permute-start | bytes 3145736 | tf_op jit(solution)/shard_map/ppermute | solution.py:136
  194.9 19.6 %collective-permute-start.31 = (bf16[256,1024]{1,0:T(8,128)(2,1)}, bf16[256,1024]{1,0:T(8,128)(2,1)}, u32[]{:S(2)}, u32[]{:S(2)}) collective-permute-start(bf16[256,1024]{1,0:T(8,128)(2,1)} %get-tuple-element.54), channel_id=1, source_target_pairs={{0,16},{8,24},{16,0},{24,8},{1,17},{9,25},{17,1},{25,9},{2,18},{10... | collective-permute-start | bytes 1572872 | tf_op jit(solution)/shard_map/ppermute | solution.py:64
  202.4 14.1 %collective-permute-start.41 = (bf16[128,1024]{1,0:T(8,128)(2,1)S(1)}, bf16[128,1024]{1,0:T(8,128)(2,1)S(1)}, u32[]{:S(2)}, u32[]{:S(2)}) collective-permute-start(bf16[128,1024]{1,0:T(8,128)(2,1)S(1)} %slice.511), channel_id=1, source_target_pairs={{0,16},{8,24},{16,0},{24,8},{1,17},{9,25},{17,1},{25,9},{2,18},{10... | collective-permute-start | bytes 786440 | tf_op jit(solution)/shard_map/ppermute | solution.py:64
  204.4 9.2 %collective-permute-start.40 = (bf16[128,1024]{1,0:T(8,128)(2,1)S(1)}, bf16[128,1024]{1,0:T(8,128)(2,1)S(1)}, u32[]{:S(2)}, u32[]{:S(2)}) collective-permute-start(bf16[128,1024]{1,0:T(8,128)(2,1)S(1)} %slice.510), channel_id=1, source_target_pairs={{0,8},{8,0},{16,24},{24,16},{1,9},{9,1},{17,25},{25,17},{2,10},{10... | collective-permute-start | bytes 786440 | tf_op jit(solution)/shard_map/ppermute | solution.py:64
  205.5 19.4 %collective-permute-start.30 = (bf16[256,1024]{1,0:T(8,128)(2,1)}, bf16[256,1024]{1,0:T(8,128)(2,1)S(1)}, u32[]{:S(2)}, u32[]{:S(2)}) collective-permute-start(bf16[256,1024]{1,0:T(8,128)(2,1)} %get-tuple-element.54), channel_id=1, source_target_pairs={{0,8},{8,0},{16,24},{24,16},{1,9},{9,1},{17,25},{25,17},{2,10},{10... | collective-permute-start | bytes 1572872 | tf_op jit(solution)/shard_map/ppermute | solution.py:64
  215.5 14.0 %collective-permute-start.32 = (bf16[128,1024]{1,0:T(8,128)(2,1)S(1)}, bf16[128,1024]{1,0:T(8,128)(2,1)S(1)}, u32[]{:S(2)}, u32[]{:S(2)}) collective-permute-start(bf16[128,1024]{1,0:T(8,128)(2,1)S(1)} %slice.502), channel_id=1, source_target_pairs={{0,8},{8,0},{16,24},{24,16},{1,9},{9,1},{17,25},{25,17},{2,10},{10... | collective-permute-start | bytes 786440 | tf_op jit(solution)/shard_map/ppermute | solution.py:64
  248.2 51.5 %collective-permute-start.44 = (bf16[128,1024]{1,0:T(8,128)(2,1)}, bf16[128,1024]{1,0:T(8,128)(2,1)}, u32[]{:S(2)}, u32[]{:S(2)}) collective-permute-start(bf16[128,1024]{1,0:T(8,128)(2,1)} %get-tuple-element.120), channel_id=1, source_target_pairs={{0,8},{8,0},{16,24},{24,16},{1,9},{9,1},{17,25},{25,17},{2,10},{10... | collective-permute-start | bytes 786440 | tf_op jit(solution)/shard_map/ppermute | solution.py:64
  249.3 50.5 %collective-permute-start.42 = (bf16[128,1024]{1,0:T(8,128)(2,1)}, bf16[128,1024]{1,0:T(8,128)(2,1)}, u32[]{:S(2)}, u32[]{:S(2)}) collective-permute-start(bf16[128,1024]{1,0:T(8,128)(2,1)} %get-tuple-element.121), channel_id=1, source_target_pairs={{0,16},{8,24},{16,0},{24,8},{1,17},{9,25},{17,1},{25,9},{2,18},{10... | collective-permute-start | bytes 786440 | tf_op jit(solution)/shard_map/ppermute | solution.py:64
  262.2 41.1 %collective-permute-start.34 = (bf16[128,1024]{1,0:T(8,128)(2,1)}, bf16[128,1024]{1,0:T(8,128)(2,1)S(1)}, u32[]{:S(2)}, u32[]{:S(2)}) collective-permute-start(bf16[128,1024]{1,0:T(8,128)(2,1)} %get-tuple-element.122), channel_id=1, source_target_pairs={{0,16},{8,24},{16,0},{24,8},{1,17},{9,25},{17,1},{25,9},{2,18},{10... | collective-permute-start | bytes 786440 | tf_op jit(solution)/shard_map/ppermute | solution.py:64
  263.2 40.1 %collective-permute-start.36 = (bf16[128,1024]{1,0:T(8,128)(2,1)}, bf16[128,1024]{1,0:T(8,128)(2,1)}, u32[]{:S(2)}, u32[]{:S(2)}) collective-permute-start(bf16[128,1024]{1,0:T(8,128)(2,1)} %get-tuple-element.123), channel_id=1, source_target_pairs={{0,8},{8,0},{16,24},{24,16},{1,9},{9,1},{17,25},{25,17},{2,10},{10... | collective-permute-start | bytes 786440 | tf_op jit(solution)/shard_map/ppermute | solution.py:64
  301.0 14.9 %collective-permute-start.43 = (bf16[256,1024]{1,0:T(8,128)(2,1)S(1)}, bf16[256,1024]{1,0:T(8,128)(2,1)S(1)}, u32[]{:S(2)}, u32[]{:S(2)}) collective-permute-start(bf16[256,1024]{1,0:T(8,128)(2,1)S(1)} %pad_maximum_fusion.10), channel_id=1, source_target_pairs={{0,8},{8,0},{16,24},{24,16},{1,9},{9,1},{17,25},{25,17},{2,10},{10... | collective-permute-start | bytes 1572872 | tf_op jit(solution)/shard_map/ppermute | solution.py:64
  302.1 14.9 %collective-permute-start.45 = (bf16[256,1024]{1,0:T(8,128)(2,1)S(1)}, bf16[256,1024]{1,0:T(8,128)(2,1)S(1)}, u32[]{:S(2)}, u32[]{:S(2)}) collective-permute-start(bf16[256,1024]{1,0:T(8,128)(2,1)S(1)} %pad_maximum_fusion.11), channel_id=1, source_target_pairs={{0,16},{8,24},{16,0},{24,8},{1,17},{9,25},{17,1},{25,9},{2,18},{10... | collective-permute-start | bytes 1572872 | tf_op jit(solution)/shard_map/ppermute | solution.py:64
  304.6 20.2 %collective-permute-start.37 = (bf16[256,1024]{1,0:T(8,128)(2,1)S(1)}, bf16[256,1024]{1,0:T(8,128)(2,1)S(1)}, u32[]{:S(2)}, u32[]{:S(2)}) collective-permute-start(bf16[256,1024]{1,0:T(8,128)(2,1)S(1)} %pad_maximum_fusion.9), channel_id=1, source_target_pairs={{0,16},{8,24},{16,0},{24,8},{1,17},{9,25},{17,1},{25,9},{2,18},{10... | collective-permute-start | bytes 1572872 | tf_op jit(solution)/shard_map/ppermute | solution.py:64
  305.7 19.1 %collective-permute-start.35 = (bf16[256,1024]{1,0:T(8,128)(2,1)S(1)}, bf16[256,1024]{1,0:T(8,128)(2,1)S(1)}, u32[]{:S(2)}, u32[]{:S(2)}) collective-permute-start(bf16[256,1024]{1,0:T(8,128)(2,1)S(1)} %pad_maximum_fusion.8), channel_id=1, source_target_pairs={{0,8},{8,0},{16,24},{24,16},{1,9},{9,1},{17,25},{25,17},{2,10},{10... | collective-permute-start | bytes 1572872 | tf_op jit(solution)/shard_map/ppermute | solution.py:64
  340.7 40.4 %collective-permute-start.46 = (bf16[512,1024]{1,0:T(8,128)(2,1)}, bf16[512,1024]{1,0:T(8,128)(2,1)}, u32[]{:S(2)}, u32[]{:S(2)}) collective-permute-start(bf16[512,1024]{1,0:T(8,128)(2,1)} %slice.521), channel_id=1, source_target_pairs={{0,1},{1,0},{2,3},{3,2},{4,5},{5,4},{6,7},{7,6},{8,9},{9,8},{10,11... | collective-permute-start | bytes 3145736 | tf_op jit(solution)/shard_map/ppermute | solution.py:136
  340.7 190.0 %reduce-scatter.3.cloned.1.call-start = ((), (), s32[]{:S(2)}) async-start(), calls=%async_computation.5 | async-start | bytes 5308416 | tf_op jit(solution)/shard_map/reduce_scatter | solution.py:386
  397.1 19.6 %collective-permute-start.57 = (bf16[512,1024]{1,0:T(8,128)(2,1)}, bf16[512,1024]{1,0:T(8,128)(2,1)}, u32[]{:S(2)}, u32[]{:S(2)}) collective-permute-start(bf16[512,1024]{1,0:T(8,128)(2,1)} %slice.541), channel_id=1, source_target_pairs={{0,1},{1,0},{2,3},{3,2},{4,5},{5,4},{6,7},{7,6},{8,9},{9,8},{10,11... | collective-permute-start | bytes 3145736 | tf_op jit(solution)/shard_map/ppermute | solution.py:136
  404.7 11.1 %collective-permute-start.52 = (bf16[32,1024]{1,0:T(8,128)(2,1)S(1)}, bf16[32,1024]{1,0:T(8,128)(2,1)S(1)}, u32[]{:S(2)}, u32[]{:S(2)}) collective-permute-start(bf16[32,1024]{1,0:T(8,128)(2,1)S(1)} %get-tuple-element.136), channel_id=1, source_target_pairs={{0,4},{1,5},{2,6},{3,7},{4,0},{5,1},{6,2},{7,3},{8,12},{9,13},{10,... | collective-permute-start | bytes 196616 | tf_op jit(solution)/shard_map/ppermute | solution.py:139
  405.3 10.5 %collective-permute-start.51 = (bf16[32,1024]{1,0:T(8,128)(2,1)S(1)}, bf16[32,1024]{1,0:T(8,128)(2,1)S(1)}, u32[]{:S(2)}, u32[]{:S(2)}) collective-permute-start(bf16[32,1024]{1,0:T(8,128)(2,1)S(1)} %get-tuple-element.134), channel_id=1, source_target_pairs={{0,2},{1,3},{2,4},{3,5},{4,6},{5,7},{6,0},{7,1},{8,10},{9,11},{10,... | collective-permute-start | bytes 196616 | tf_op jit(solution)/shard_map/ppermute | solution.py:139
  416.6 11.3 %collective-permute-start.54 = (bf16[512,1024]{1,0:T(8,128)(2,1)S(1)}, bf16[512,1024]{1,0:T(8,128)(2,1)S(1)}, u32[]{:S(2)}, u32[]{:S(2)}) collective-permute-start(bf16[512,1024]{1,0:T(8,128)(2,1)S(1)} %slice.429), channel_id=1, source_target_pairs={{0,1},{1,0},{2,3},{3,2},{4,5},{5,4},{6,7},{7,6},{8,9},{9,8},{10,11... | collective-permute-start | bytes 3145736 | tf_op jit(solution)/shard_map/ppermute | solution.py:136
  429.3 27.7 %collective-permute-start.55 = (bf16[256,1024]{1,0:T(8,128)(2,1)}, bf16[256,1024]{1,0:T(8,128)(2,1)}, u32[]{:S(2)}, u32[]{:S(2)}) collective-permute-start(bf16[256,1024]{1,0:T(8,128)(2,1)} %slice.667), channel_id=1, source_target_pairs={{2,0},{3,1},{4,2},{5,3},{6,4},{7,5},{10,8},{11,9},{12,10},{13,11},... | collective-permute-start | bytes 1572872 | tf_op jit(solution)/shard_map/ppermute | solution.py:133
  459.0 24.9 %collective-permute-start.56 = (bf16[256,1024]{1,0:T(8,128)(2,1)}, bf16[256,1024]{1,0:T(8,128)(2,1)}, u32[]{:S(2)}, u32[]{:S(2)}) collective-permute-start(bf16[256,1024]{1,0:T(8,128)(2,1)} %fusion.100), channel_id=1, source_target_pairs={{2,0},{3,1},{4,2},{5,3},{6,4},{7,5},{10,8},{11,9},{12,10},{13,11},... | collective-permute-start | bytes 1572872 | tf_op jit(solution)/shard_map/ppermute | solution.py:133
  460.9 15.1 %collective-permute-start.64 = (bf16[32,1024]{1,0:T(8,128)(2,1)}, bf16[32,1024]{1,0:T(8,128)(2,1)S(1)}, u32[]{:S(2)}, u32[]{:S(2)}) collective-permute-start(bf16[32,1024]{1,0:T(8,128)(2,1)} %get-tuple-element.132), channel_id=1, source_target_pairs={{0,6},{1,7},{2,0},{3,1},{4,2},{5,3},{6,4},{7,5},{8,14},{9,15},{10,... | collective-permute-start | bytes 196616 | tf_op jit(solution)/shard_map/ppermute | solution.py:139
  465.0 17.2 %collective-permute-start.63 = (bf16[32,1024]{1,0:T(8,128)(2,1)}, bf16[32,1024]{1,0:T(8,128)(2,1)S(1)}, u32[]{:S(2)}, u32[]{:S(2)}) collective-permute-start(bf16[32,1024]{1,0:T(8,128)(2,1)} %get-tuple-element.133), channel_id=1, source_target_pairs={{0,4},{1,5},{2,6},{3,7},{4,0},{5,1},{6,2},{7,3},{8,12},{9,13},{10,... | collective-permute-start | bytes 196616 | tf_op jit(solution)/shard_map/ppermute | solution.py:139
  465.0 17.2 %collective-permute-start.62 = (bf16[32,1024]{1,0:T(8,128)(2,1)}, bf16[32,1024]{1,0:T(8,128)(2,1)S(1)}, u32[]{:S(2)}, u32[]{:S(2)}) collective-permute-start(bf16[32,1024]{1,0:T(8,128)(2,1)} %get-tuple-element.131), channel_id=1, source_target_pairs={{0,2},{1,3},{2,4},{3,5},{4,6},{5,7},{6,0},{7,1},{8,10},{9,11},{10,... | collective-permute-start | bytes 196616 | tf_op jit(solution)/shard_map/ppermute | solution.py:139
  491.8 12.3 %collective-permute-start.65 = (bf16[512,1024]{1,0:T(8,128)(2,1)}, bf16[512,1024]{1,0:T(8,128)(2,1)}, u32[]{:S(2)}, u32[]{:S(2)}) collective-permute-start(bf16[512,1024]{1,0:T(8,128)(2,1)} %slice.554), channel_id=1, source_target_pairs={{0,1},{1,0},{2,3},{3,2},{4,5},{5,4},{6,7},{7,6},{8,9},{9,8},{10,11... | collective-permute-start | bytes 3145736 | tf_op jit(solution)/shard_map/ppermute | solution.py:136
  501.4 18.9 %all-to-all-start = ((f32[32,1,192]{2,1,0:T(1,128)}), f32[32,1,192]{2,1,0:T(1,128)S(1)}, u32[]{:S(2)}, u32[]{:S(2)}) async-start(f32[32,1,192]{2,1,0:T(1,128)} %all_to_all.6), calls=%async_computation | async-start | bytes 65536 | tf_op jit(solution)/shard_map/all_to_all | solution.py:491
  (120 other events, 1000.1 us)
Sparse Core Ops, SparseCore 0:
  28.4 56.8 all-gather.2
  86.9 39.0 all-gather.4
  340.8 35.1 reduce-scatter.4
  397.2 68.6 reduce-scatter.2
